TPU v7x, 32 devices: a whole 2x2x4 slice. The times are simulated.
32 devices in a mesh: seq: 8 (over z, x), rep: 4 (over y, core).
Axes of the slice: x: 2, y: 2, z: 4, core: 2. Of those that a mesh axis runs over, the one named last changes fastest.
Arguments:
- tokens: bfloat16 [4, 1024, 960], P('rep', 'seq'), may hold values from -6 to 6
- depths: int32 [4, 1024], P('rep', 'seq'), may hold values from 1 to 3
- seq_spans: int32 [4, 3], P('rep'), may hold values from 1 to 4, 8 in all within a row
- cotangent: bfloat16 [4, 1024, 960], P('rep', 'seq'), may hold values from -6 to 6
- w_query: float32 [921600], P(('seq', 'rep')), may hold values from -0.1875 to 0.1875
- key_weight: float32 [307200], P(('seq', 'rep')), may hold values from -0.1875 to 0.1875
- value_weight: float32 [307200], P(('seq', 'rep')), may hold values from -0.1875 to 0.1875
- w_out: float32 [921600], P(('seq', 'rep')), may hold values from -0.75 to 0.75
- w_gate: float32 [2457600], P(('seq', 'rep')), may hold values from -0.1875 to 0.1875
- w_up: float32 [2457600], P(('seq', 'rep')), may hold values from -0.1875 to 0.1875
- w_down: float32 [2457600], P(('seq', 'rep')), may hold values from -0.125 to 0.125
- attn_gain: float32 [960], replicated, may hold values from 0.1 to 1.9
- ffn_gain: float32 [960], replicated, may hold values from 0.1 to 1.9
- router: float32 [3, 960], replicated, may hold values from -0.1875 to 0.1875
Outputs:
- output: bfloat16 [4, 1024, 960], P('rep', 'seq')
- input_grad: float32 [4, 1024, 960], P('rep', 'seq')
- grad_query: float32 [921600], P(('seq', 'rep'))
- grad_key: float32 [307200], P(('seq', 'rep'))
- grad_value: float32 [307200], P(('seq', 'rep'))
- grad_out: float32 [921600], P(('seq', 'rep'))
- grad_gate: float32 [2457600], P(('seq', 'rep'))
- grad_up: float32 [2457600], P(('seq', 'rep'))
- grad_down: float32 [2457600], P(('seq', 'rep'))
- grad_attn_gain: float32 [960], replicated
- grad_ffn_gain: float32 [960], replicated
- grad_router: float32 [3, 960], replicated
Inputs may be any that keep to these rules, and one draw needn't show every extreme that they name: `seq_spans`: each row gives the span counts of the 3 sequences of a group; they add up to 8, and some sequence has exactly 4 spans.
All inputs are finite; a program needn't handle non-finite values.
Results may differ from a plain program's by a relative error of at most 0.025.
Values may be sent and summed in bfloat16 or wider, within the bound.
A program may use at most 448 MiB of HBM per device.

v0:
```python
import jax
import jax.numpy as jnp
from jax import lax
from jax.sharding import PartitionSpec as P

MODEL_WIDTH = 960
QUERY_HEADS = 15
KEY_VALUE_HEADS = 5
HEAD_SIZE = 64
FEEDFORWARD_UNITS = 2560
LOGC = 5
RECUR = 3


highest = lax.Precision.HIGHEST
epsilon = 1e-06
masked_score = -1e30


def passed_along(value, axis, steps):
    count = lax.axis_size(axis)
    initial, last = (max(0, -steps), min(count, count - steps))
    return lax.ppermute(value, axis, [(source, source + steps) for source in range(initial, last)])


def for_sending(x):

    def short(part):
        return part.astype(jnp.bfloat16) if part.dtype == jnp.float32 else part

    return jax.tree.map(short, x)


def unscaled_product(left, right):
    return jnp.dot(left, right, preferred_element_type=jnp.float32)


def left_product(left, right):
    return lax.dot_general(
        left, right, (((0,), (0,)), ((), ())), preferred_element_type=jnp.float32
    )


def right_product(left, right):
    return lax.dot_general(
        left, right, (((1,), (1,)), ((), ())), preferred_element_type=jnp.float32
    )


def rms_parts(vectors, gain):
    inv_rms = lax.rsqrt(jnp.mean(vectors * vectors, axis=-1, keepdims=True) + epsilon)
    normal_part = vectors * inv_rms
    return (normal_part * gain, normal_part, inv_rms)


def rms_backward(upstream, normal_part, inv_rms, gain):
    gain_grad = jnp.sum(upstream * normal_part, axis=0)
    scaled = upstream * gain
    inner = jnp.mean(scaled * normal_part, axis=-1, keepdims=True)
    return (inv_rms * (scaled - normal_part * inner), gain_grad)


def angle_tables(positions, width):
    half_width = width // 2
    frequency = 10000.0 ** (-jnp.arange(half_width, dtype=jnp.float32) / half_width)
    angle_grid = positions[:, None] * frequency[None, :]
    return (jnp.cos(angle_grid)[:, None, :], jnp.sin(angle_grid)[:, None, :])


def apply_rotation(vectors, cosine_table, sine_table):
    half_width = vectors.shape[-1] // 2
    front_half = vectors[..., :half_width]
    back_half = vectors[..., half_width:]
    return jnp.concatenate(
        [
            front_half * cosine_table - back_half * sine_table,
            back_half * cosine_table + front_half * sine_table,
        ],
        axis=-1,
    )


def masked_scores(query_b, keys_win, allowed):
    scores = (
        jnp.einsum("qgjd,kgd->gjqk", query_b, keys_win, preferred_element_type=jnp.float32) * 0.125
    )
    return jnp.where(allowed[None, None], scores, masked_score)


def per_device(
    tokens,
    depths,
    seq_spans,
    cotangent,
    w_query,
    key_weight,
    value_weight,
    w_out,
    w_gate,
    w_up,
    w_down,
    attn_gain,
    ffn_gain,
    router,
):
    narrow_float_type = jnp.bfloat16
    wide_float_type = jnp.float32
    count_of_rows = tokens.shape[1]
    query_groupings = QUERY_HEADS // KEY_VALUE_HEADS
    chain = lax.axis_size("seq")
    most_spans = min(2**LOGC, chain // 2)
    depth_levels = (most_spans - 1).bit_length()
    extra_rows = ((1 << depth_levels) - most_spans) * count_of_rows
    window = most_spans * count_of_rows
    target_tokens = (
        (MODEL_WIDTH, QUERY_HEADS * HEAD_SIZE),
        (MODEL_WIDTH, KEY_VALUE_HEADS * HEAD_SIZE),
        (MODEL_WIDTH, KEY_VALUE_HEADS * HEAD_SIZE),
        (QUERY_HEADS * HEAD_SIZE, MODEL_WIDTH),
        (MODEL_WIDTH, FEEDFORWARD_UNITS),
        (MODEL_WIDTH, FEEDFORWARD_UNITS),
        (FEEDFORWARD_UNITS, MODEL_WIDTH),
    )
    fetched = (
        lax.all_gather(w_query.astype(narrow_float_type), ("seq", "rep"), axis=0, tiled=True),
        lax.all_gather(key_weight.astype(narrow_float_type), ("seq", "rep"), axis=0, tiled=True),
        lax.all_gather(value_weight.astype(narrow_float_type), ("seq", "rep"), axis=0, tiled=True),
        lax.all_gather(w_out.astype(narrow_float_type), ("seq", "rep"), axis=0, tiled=True),
        lax.all_gather(w_gate.astype(narrow_float_type), ("seq", "rep"), axis=0, tiled=True),
        lax.all_gather(w_up.astype(narrow_float_type), ("seq", "rep"), axis=0, tiled=True),
        lax.all_gather(w_down.astype(narrow_float_type), ("seq", "rep"), axis=0, tiled=True),
    )
    attention_weights = tuple(
        (gathered.reshape(target) for gathered, target in zip(fetched, target_tokens))
    )
    place = lax.axis_index("seq")
    lengths = seq_spans[0]
    seq_ends = jnp.cumsum(lengths)
    span_ids = jnp.arange(chain, dtype=jnp.int32)
    owners = jnp.sum((seq_ends[None, :] <= span_ids[:, None]).astype(jnp.int32), axis=1)
    seq_starts = seq_ends - lengths
    numbers = jnp.arange(lengths.shape[0], dtype=jnp.int32)
    first_span = jnp.sum(
        jnp.where(numbers[None, :] == owners[:, None], seq_starts[None, :], 0), axis=1
    )
    index_of_span = jnp.sum(jnp.where(span_ids == place, span_ids - first_span, 0))
    positions = (index_of_span * count_of_rows + jnp.arange(count_of_rows, dtype=jnp.int32)).astype(
        wide_float_type
    )
    cosine_table, sine_table = angle_tables(positions, HEAD_SIZE)
    row_ids = jnp.arange(count_of_rows, dtype=jnp.int32)
    col_ids = jnp.arange(window, dtype=jnp.int32)
    offsets = most_spans - 1 - col_ids // count_of_rows
    local_col = col_ids - (most_spans - 1) * count_of_rows
    causal = jnp.where(offsets[None, :] == 0, local_col[None, :] <= row_ids[:, None], True)
    diagonal = (offsets[None, :] == 0) & (local_col[None, :] == row_ids[:, None])
    span_ok = (index_of_span >= offsets)[None, :]
    active_all = (depths[0][None, :] > jnp.arange(RECUR, dtype=jnp.int32)[:, None]).astype(
        wide_float_type
    )
    hidden_state = tokens[0].astype(wide_float_type)
    saved = []
    for recursion in range(RECUR):
        current_active = active_all[recursion]
        normalized_input, normal_a, inv_a = rms_parts(hidden_state, attn_gain)
        normalized_input_copy = normalized_input.astype(narrow_float_type)
        raw_query = unscaled_product(normalized_input_copy, attention_weights[0]).reshape(
            count_of_rows, QUERY_HEADS, HEAD_SIZE
        )
        query_b = (
            apply_rotation(raw_query, cosine_table, sine_table)
            .astype(narrow_float_type)
            .reshape(count_of_rows, KEY_VALUE_HEADS, query_groupings, HEAD_SIZE)
        )
        unrotated_key = unscaled_product(normalized_input_copy, attention_weights[1]).reshape(
            count_of_rows, KEY_VALUE_HEADS, HEAD_SIZE
        )
        key_b = apply_rotation(unrotated_key, cosine_table, sine_table).astype(narrow_float_type)
        value_copy = (
            unscaled_product(normalized_input_copy, attention_weights[2])
            .astype(narrow_float_type)
            .reshape(count_of_rows, KEY_VALUE_HEADS, HEAD_SIZE)
        )
        active_b = current_active.astype(narrow_float_type)
        keys_win = key_b
        values_win = value_copy
        active_win = active_b
        for level in range(depth_levels):
            far_key, far_value, far_active = passed_along(
                (keys_win, values_win, active_win), "seq", 1 << level
            )
            keys_win = jnp.concatenate([far_key, keys_win], axis=0)
            values_win = jnp.concatenate([far_value, values_win], axis=0)
            active_win = jnp.concatenate([far_active, active_win], axis=0)
        allowed = span_ok & causal & ((active_win > 0)[None, :] | diagonal)
        scores = masked_scores(query_b, keys_win, allowed)
        row_max = jnp.max(scores, axis=-1, keepdims=True)
        expon = jnp.exp(scores - row_max)
        row_total = jnp.sum(expon, axis=-1, keepdims=True)
        probs_b = (expon / row_total).astype(narrow_float_type)
        log_total = row_max + jnp.log(row_total)
        attended_b = (
            jnp.einsum(
                "gjqk,kgd->qgjd", probs_b, values_win, preferred_element_type=wide_float_type
            )
            .astype(narrow_float_type)
            .reshape(count_of_rows, QUERY_HEADS * HEAD_SIZE)
        )
        branch = unscaled_product(attended_b, attention_weights[3])
        middle = hidden_state + branch
        second, normal_z, inv_z = rms_parts(middle, ffn_gain)
        second_b = second.astype(narrow_float_type)
        gate_value = unscaled_product(second_b, attention_weights[4])
        up_value = unscaled_product(second_b, attention_weights[5])
        hidden_b = (jax.nn.silu(gate_value) * up_value).astype(narrow_float_type)
        ffn_out = unscaled_product(hidden_b, attention_weights[6])
        weight_gate = jax.nn.sigmoid(jnp.dot(hidden_state, router[recursion], precision=highest))
        saved.append(
            (
                hidden_state,
                normalized_input_copy,
                normal_a,
                inv_a,
                query_b,
                keys_win,
                values_win,
                allowed,
                log_total,
                attended_b,
                branch,
                normal_z,
                inv_z,
                second_b,
                gate_value,
                up_value,
                hidden_b,
                ffn_out,
                weight_gate,
                current_active,
            )
        )
        hidden_state = hidden_state + (current_active * weight_gate)[:, None] * (branch + ffn_out)
    output = hidden_state.astype(narrow_float_type)
    refetched = (
        lax.all_gather(w_query.astype(narrow_float_type), ("seq", "rep"), axis=0, tiled=True),
        lax.all_gather(key_weight.astype(narrow_float_type), ("seq", "rep"), axis=0, tiled=True),
        lax.all_gather(value_weight.astype(narrow_float_type), ("seq", "rep"), axis=0, tiled=True),
        lax.all_gather(w_out.astype(narrow_float_type), ("seq", "rep"), axis=0, tiled=True),
        lax.all_gather(w_gate.astype(narrow_float_type), ("seq", "rep"), axis=0, tiled=True),
        lax.all_gather(w_up.astype(narrow_float_type), ("seq", "rep"), axis=0, tiled=True),
        lax.all_gather(w_down.astype(narrow_float_type), ("seq", "rep"), axis=0, tiled=True),
    )
    back_weights = tuple(
        (gathered.reshape(target) for gathered, target in zip(refetched, target_tokens))
    )
    master_shapes = (w_query, key_weight, value_weight, w_out, w_gate, w_up, w_down)
    shares = tuple((jnp.zeros_like(master) for master in master_shapes))
    gain_a_total = jnp.zeros((MODEL_WIDTH,), wide_float_type)
    gain_f_total = jnp.zeros((MODEL_WIDTH,), wide_float_type)
    router_rows = [None] * RECUR
    grad_state = cotangent[0].astype(wide_float_type)
    for recursion in reversed(range(RECUR)):
        (
            state_in,
            normalized_input_copy,
            normal_a,
            inv_a,
            query_b,
            keys_win,
            values_win,
            allowed,
            log_total,
            attended_b,
            branch,
            normal_z,
            inv_z,
            second_b,
            gate_value,
            up_value,
            hidden_b,
            ffn_out,
            weight_gate,
            current_active,
        ) = saved[recursion]
        mixing = current_active * weight_gate
        grad_delta = mixing[:, None] * grad_state
        grad_mix = jnp.sum(grad_state * (branch + ffn_out), axis=-1)
        grad_logit = current_active * grad_mix * weight_gate * (1.0 - weight_gate)
        router_rows[recursion] = jnp.dot(grad_logit, state_in, precision=highest)
        grad_next = grad_state + grad_logit[:, None] * router[recursion][None, :]
        ffn_grad_b = grad_delta.astype(narrow_float_type)
        grad_hidden = right_product(ffn_grad_b, back_weights[6])
        d_down = left_product(hidden_b, ffn_grad_b)
        sigmoid_gate = jax.nn.sigmoid(gate_value)
        grad_gate_b = (
            grad_hidden * up_value * sigmoid_gate * (1.0 + gate_value * (1.0 - sigmoid_gate))
        ).astype(narrow_float_type)
        grad_up_b = (grad_hidden * gate_value * sigmoid_gate).astype(narrow_float_type)
        grad_second = right_product(grad_gate_b, back_weights[4]) + right_product(
            grad_up_b, back_weights[5]
        )
        d_gate = left_product(second_b, grad_gate_b)
        d_up = left_product(second_b, grad_up_b)
        grad_middle, gain_f_part = rms_backward(grad_second, normal_z, inv_z, ffn_gain)
        gain_f_total = gain_f_total + gain_f_part
        grad_branch_b = (grad_delta + grad_middle).astype(narrow_float_type)
        grad_attended_b = (
            right_product(grad_branch_b, back_weights[3])
            .astype(narrow_float_type)
            .reshape(count_of_rows, KEY_VALUE_HEADS, query_groupings, HEAD_SIZE)
        )
        d_out = left_product(attended_b, grad_branch_b)
        grad_next = grad_next + grad_middle
        scores = masked_scores(query_b, keys_win, allowed)
        probs = jnp.exp(scores - log_total)
        probs_b = probs.astype(narrow_float_type)
        grad_probs = jnp.einsum(
            "qgjd,kgd->gjqk", grad_attended_b, values_win, preferred_element_type=wide_float_type
        )
        row_dot = jnp.sum(probs * grad_probs, axis=-1, keepdims=True)
        grad_scores_b = (probs * (grad_probs - row_dot)).astype(narrow_float_type)
        grad_queries = (
            jnp.einsum(
                "gjqk,kgd->qgjd", grad_scores_b, keys_win, preferred_element_type=wide_float_type
            )
            * 0.125
        )
        grad_keys = (
            jnp.einsum(
                "gjqk,qgjd->kgd", grad_scores_b, query_b, preferred_element_type=wide_float_type
            )
            * 0.125
        )
        grad_values = jnp.einsum(
            "gjqk,qgjd->kgd", probs_b, grad_attended_b, preferred_element_type=wide_float_type
        )
        extra_zero_rows = jnp.zeros((extra_rows, KEY_VALUE_HEADS, HEAD_SIZE), wide_float_type)
        local_span_keys = jnp.concatenate([extra_zero_rows, grad_keys], axis=0)
        local_span_values = jnp.concatenate([extra_zero_rows, grad_values], axis=0)
        for level in reversed(range(depth_levels)):
            older_rows = (1 << level) * count_of_rows
            back_keys, back_values = passed_along(
                (
                    for_sending(local_span_keys[:older_rows]),
                    for_sending(local_span_values[:older_rows]),
                ),
                "seq",
                -(1 << level),
            )
            local_span_keys = local_span_keys[older_rows:] + back_keys
            local_span_values = local_span_values[older_rows:] + back_values
        grad_query_b = (
            apply_rotation(
                grad_queries.reshape(count_of_rows, QUERY_HEADS, HEAD_SIZE),
                cosine_table,
                -sine_table,
            )
            .astype(narrow_float_type)
            .reshape(count_of_rows, QUERY_HEADS * HEAD_SIZE)
        )
        grad_key_b = (
            apply_rotation(local_span_keys, cosine_table, -sine_table)
            .astype(narrow_float_type)
            .reshape(count_of_rows, KEY_VALUE_HEADS * HEAD_SIZE)
        )
        value_gradient_copy = local_span_values.astype(narrow_float_type).reshape(
            count_of_rows, KEY_VALUE_HEADS * HEAD_SIZE
        )
        grad_normed = (
            right_product(grad_query_b, back_weights[0])
            + right_product(grad_key_b, back_weights[1])
            + right_product(value_gradient_copy, back_weights[2])
        )
        d_query = left_product(normalized_input_copy, grad_query_b)
        d_key = left_product(normalized_input_copy, grad_key_b)
        d_value = left_product(normalized_input_copy, value_gradient_copy)
        grad_input, gain_a_part = rms_backward(grad_normed, normal_a, inv_a, attn_gain)
        gain_a_total = gain_a_total + gain_a_part
        grad_state = grad_next + grad_input
        local_grads = (
            d_query.reshape(-1),
            d_key.reshape(-1),
            d_value.reshape(-1),
            d_out.reshape(-1),
            d_gate.reshape(-1),
            d_up.reshape(-1),
            d_down.reshape(-1),
        )
        summed = (
            lax.psum_scatter(local_grads[0], ("seq", "rep"), scatter_dimension=0, tiled=True),
            lax.psum_scatter(local_grads[1], ("seq", "rep"), scatter_dimension=0, tiled=True),
            lax.psum_scatter(local_grads[2], ("seq", "rep"), scatter_dimension=0, tiled=True),
            lax.psum_scatter(local_grads[3], ("seq", "rep"), scatter_dimension=0, tiled=True),
            lax.psum_scatter(local_grads[4], ("seq", "rep"), scatter_dimension=0, tiled=True),
            lax.psum_scatter(local_grads[5], ("seq", "rep"), scatter_dimension=0, tiled=True),
            lax.psum_scatter(local_grads[6], ("seq", "rep"), scatter_dimension=0, tiled=True),
        )
        shares = tuple((old_share + new_share for old_share, new_share in zip(shares, summed)))
    router_grad = jnp.stack(router_rows, axis=0)
    gain_a_sum, gain_f_sum, router_sum = lax.psum(
        (gain_a_total, gain_f_total, router_grad), ("seq", "rep")
    )
    return (
        output[None],
        grad_state[None],
        shares[0],
        shares[1],
        shares[2],
        shares[3],
        shares[4],
        shares[5],
        shares[6],
        gain_a_sum,
        gain_f_sum,
        router_sum,
    )


def solution(mesh):
    placed = (
        P("rep", "seq", None),
        P("rep", "seq"),
        P("rep", None),
        P("rep", "seq", None),
        P(("seq", "rep")),
        P(("seq", "rep")),
        P(("seq", "rep")),
        P(("seq", "rep")),
        P(("seq", "rep")),
        P(("seq", "rep")),
        P(("seq", "rep")),
        P(),
        P(),
        P(),
    )
    return jax.shard_map(
        per_device,
        mesh=mesh,
        in_specs=placed,
        out_specs=(
            P("rep", "seq", None),
            P("rep", "seq", None),
            P(("seq", "rep")),
            P(("seq", "rep")),
            P(("seq", "rep")),
            P(("seq", "rep")),
            P(("seq", "rep")),
            P(("seq", "rep")),
            P(("seq", "rep")),
            P(),
            P(),
            P(),
        ),
        check_vma=False,
    )
```

profile of v0, /device:TPU:1, one launch (start us, length us, event | category | flops | bytes accessed | tf_op | source)
XLA Modules:
  0.0 1267.9 jit_solution(10185409907173691060)
XLA Ops:
  27.6 44.1 %all-gather = bf16[32,1,9600]{2,1,0:T(2,128)(2,1)S(1)} all-gather(bf16[1,1,9600]{2,1,0:T(2,128)(2,1)S(1)} %reshape.980), channel_id=1, replica_groups=mesh['seq'=8,'rep'=4] {'seq','rep'}, dimensions={0}, use_global_device_ids=true | all-gather | bytes 633600 | tf_op jit(solution)/shard_map/all_gather | solution.py:127
  78.5 44.4 %all-gather.1 = bf16[32,1,9600]{2,1,0:T(2,128)(2,1)S(1)} all-gather(bf16[1,1,9600]{2,1,0:T(2,128)(2,1)S(1)} %reshape.982), channel_id=1, replica_groups=mesh['seq'=8,'rep'=4] {'seq','rep'}, dimensions={0}, use_global_device_ids=true | all-gather | bytes 633600 | tf_op jit(solution)/shard_map/all_gather | solution.py:126
  140.6 4.6 collective-permute-start.1
  148.4 40.9 %reduce.3 = bf16[32,28800]{1,0:T(8,128)(2,1)} reduce(bf16[32,1,28800]{2,1,0:T(2,128)(2,1)} %all-gather.18.cloned.1.call-done, bf16[]{:T(256)} %constant.104), dimensions={1}, to_apply=%all-gather.3.reduce_sub_computation | reduce | bytes 3686402 | tf_op jit(solution)/shard_map/all_gather | solution.py:128
  192.3 40.8 %reduce.2 = bf16[32,28800]{1,0:T(8,128)(2,1)} reduce(bf16[32,1,28800]{2,1,0:T(2,128)(2,1)} %all-gather.16.cloned.1.call-done, bf16[]{:T(256)} %constant.104), dimensions={1}, to_apply=%all-gather.2.reduce_sub_computation | reduce | bytes 3686402 | tf_op jit(solution)/shard_map/all_gather | solution.py:125
  251.2 10.0 reshape.928
  261.2 13.8 %all-gather.12.cloned.1.call-done = bf16[2457600]{0:T(1024)(128)(2,1)} async-done(((bf16[76800]{0:T(1024)(128)(2,1)}), bf16[2457600]{0:T(1024)(128)(2,1)}) %all-gather.12.cloned.1.call-update) | async-done | bytes 4915216 | tf_op jit(solution)/shard_map/all_gather | solution.py:130
  275.0 10.0 reshape.929
  291.8 49.0 %all-gather.14.cloned.1.call-done = bf16[2457600]{0:T(1024)(128)(2,1)} async-done(((bf16[76800]{0:T(1024)(128)(2,1)}), bf16[2457600]{0:T(1024)(128)(2,1)}) %all-gather.14.cloned.1.call-update) | async-done | bytes 4915216 | tf_op jit(solution)/shard_map/all_gather | solution.py:131
  340.8 9.5 reshape.930
  350.3 5.4 multiply_reduce_fusion.15
  365.7 4.6 collective-permute-start.11
  389.0 5.3 collective-permute-start.12
  419.3 5.3 fusion.90
  424.6 5.2 fusion.183
  429.8 5.1 fusion.181
  444.9 4.2 collective-permute-done.18
  470.9 5.2 fusion.119
  476.1 5.1 fusion.184
  481.2 5.1 fusion.182
  536.6 5.6 reshape.973
  542.1 5.9 add_add_fusion.3
  548.1 5.6 reshape.976
  553.7 11.7 add_add_fusion
  565.4 11.2 copy.88
  576.6 13.2 %reshape.979 = f32[2457600]{0:T(1024)} reshape(f32[2560,960]{1,0:T(8,128)} %copy.88) | data formatting | bytes 19660800 | tf_op jit(solution)/shard_map/add | solution.py:398
  589.8 11.8 add_add_fusion.1
  601.6 11.0 reshape.978
  612.6 11.7 add_add_fusion.2
  624.3 11.1 reshape.977
  666.8 54.4 %all-reduce.7 = (f32[960]{0:T(1024)}, f32[960]{0:T(1024)}, f32[3,960]{1,0:T(4,128)}) all-reduce(f32[960]{0:T(1024)S(1)} %add_add_fusion.6, f32[960]{0:T(1024)} %add_add_fusion.5, f32[3,960]{1,0:T(4,128)S(1)} %pad_maximum_fusion.17), channel_id=1, replica_groups=mesh['seq'=8,'rep'=4] {'seq','rep'}, use_global_device_ids=true, to_apply=%region_52.53 | all-reduce | flops 4800 | bytes 38400 | tf_op jit(solution)/shard_map/psum | solution.py:400
  723.9 525.5 %all-reduce.11.cloned.1.call-done = (f32[921600]{0:T(1024)}, f32[307200]{0:T(1024)}, f32[307200]{0:T(1024)}, f32[921600]{0:T(1024)}, f32[2457600]{0:T(1024)}, /*index=5*/f32[2457600]{0:T(1024)}, f32[2457600]{0:T(1024)}) async-done(((f32[921600]{0:T(1024)}, f32[307200]{0:T(1024)}, f32[307200]{0:T(1024)}, f32[921600]{0:T(1024)}, f32[2457600]{0:T(1024)}, /*index=5*/f32[2457600]{0:T(1024)}, f32[2457600]{0:T(1024)}), ...) | async-done | bytes 39321616
  (619 shorter events, 253.7 us)
Async XLA Ops:
  7.2 141.1 %all-gather.18.cloned.1.call-start = ((), (), s32[]{:S(2)}) async-start(), calls=%async_computation.4 | async-start | bytes 3801600 | tf_op jit(solution)/shard_map/all_gather | solution.py:128
  9.0 183.3 %all-gather.16.cloned.1.call-start = ((), (), s32[]{:S(2)}) async-start(), calls=%async_computation.3 | async-start | bytes 3801600 | tf_op jit(solution)/shard_map/all_gather | solution.py:125
  10.7 240.5 %all-gather.10.cloned.1.call-start = ((), (), s32[]{:S(2)}) async-start(), calls=%async_computation | async-start | bytes 5068800 | tf_op jit(solution)/shard_map/all_gather | solution.py:129
  12.4 262.6 %all-gather.12.cloned.1.call-start = ((), (), s32[]{:S(2)}) async-start(), calls=%async_computation.1 | async-start | bytes 5068800 | tf_op jit(solution)/shard_map/all_gather | solution.py:130
  14.1 326.7 %all-gather.14.cloned.1.call-start = ((), (), s32[]{:S(2)}) async-start(), calls=%async_computation.2 | async-start | bytes 5068800 | tf_op jit(solution)/shard_map/all_gather | solution.py:131
  15.8 1233.6 %all-reduce.11.cloned.1.call-start = ((), (), s32[]{:S(2)}) async-start(), calls=%async_computation.5 | async-start | bytes 78643200
  16.5 116.9 %collective-permute-start.14 = (bf16[128]{0:T(256)(128)(2,1)S(1)}, bf16[128]{0:T(256)(128)(2,1)S(1)}, u32[]{:S(2)}, u32[]{:S(2)}) collective-permute-start(bf16[128]{0:T(256)(128)(2,1)S(1)} %get-tuple-element.86), channel_id=1, source_target_pairs={{0,4},{4,8},{8,12},{12,16},{16,20},{20,24},{24,28},{1,5},{5,9},{9,... | collective-permute-start | bytes 776 | tf_op jit(solution)/shard_map/ppermute | solution.py:23
  20.5 114.3 %collective-permute-start.2 = (bf16[128]{0:T(256)(128)(2,1)S(1)}, bf16[128]{0:T(256)(128)(2,1)S(1)}, u32[]{:S(2)}, u32[]{:S(2)}) collective-permute-start(bf16[128]{0:T(256)(128)(2,1)S(1)} %get-tuple-element.87), channel_id=1, source_target_pairs={{0,4},{4,8},{8,12},{12,16},{16,20},{20,24},{24,28},{1,5},{5,9},{9,... | collective-permute-start | bytes 776 | tf_op jit(solution)/shard_map/ppermute | solution.py:23
  23.7 112.4 %collective-permute-start.8 = (bf16[128]{0:T(256)(128)(2,1)S(1)}, bf16[128]{0:T(256)(128)(2,1)S(1)}, u32[]{:S(2)}, u32[]{:S(2)}) collective-permute-start(bf16[128]{0:T(256)(128)(2,1)S(1)} %get-tuple-element.89), channel_id=1, source_target_pairs={{0,4},{4,8},{8,12},{12,16},{16,20},{20,24},{24,28},{1,5},{5,9},{9,... | collective-permute-start | bytes 776 | tf_op jit(solution)/shard_map/ppermute | solution.py:23
  77.0 62.9 %collective-permute-start = (bf16[128,5,64]{0,2,1:T(8,128)(2,1)S(1)}, bf16[128,5,64]{0,2,1:T(8,128)(2,1)S(1)}, u32[]{:S(2)}, u32[]{:S(2)}) collective-permute-start(bf16[128,5,64]{0,2,1:T(8,128)(2,1)S(1)} %bitcast.539), channel_id=1, source_target_pairs={{0,4},{4,8},{8,12},{12,16},{16,20},{20,24},{24,28},{1,5},{5,9},{9,... | collective-permute-start | bytes 245768 | tf_op jit(solution)/shard_map/ppermute | solution.py:23
  130.0 15.2 %collective-permute-start.4 = (bf16[128,5,64]{0,2,1:T(8,128)(2,1)S(1)}, bf16[128,5,64]{0,2,1:T(8,128)(2,1)S(1)}, u32[]{:S(2)}, u32[]{:S(2)}) collective-permute-start(bf16[128,5,64]{0,2,1:T(8,128)(2,1)S(1)} %pad_maximum_fusion.13), channel_id=1, source_target_pairs={{0,4},{4,8},{8,12},{12,16},{16,20},{20,24},{24,28},{1,5},{5,9},{9,... | collective-permute-start | bytes 245768 | tf_op jit(solution)/shard_map/ppermute | solution.py:23
  140.6 105.4 %collective-permute-start.1 = (bf16[256,5,64]{0,2,1:T(8,128)(2,1)}, bf16[256,5,64]{0,2,1:T(8,128)(2,1)}, u32[]{:S(2)}, u32[]{:S(2)}) collective-permute-start(bf16[256,5,64]{0,2,1:T(8,128)(2,1)} %pad_maximum_fusion.4), channel_id=1, source_target_pairs={{0,8},{4,12},{8,16},{12,20},{16,24},{20,28},{1,9},{5,13},{9,17},{1... | collective-permute-start | bytes 491528 | tf_op jit(solution)/shard_map/ppermute | solution.py:23
  146.0 97.5 %collective-permute-start.5 = (bf16[256,5,64]{0,2,1:T(8,128)(2,1)}, bf16[256,5,64]{0,2,1:T(8,128)(2,1)}, u32[]{:S(2)}, u32[]{:S(2)}) collective-permute-start(bf16[256,5,64]{0,2,1:T(8,128)(2,1)} %maximum_maximum_fusion), channel_id=1, source_target_pairs={{0,8},{4,12},{8,16},{12,20},{16,24},{20,28},{1,9},{5,13},{9,17},{1... | collective-permute-start | bytes 491528 | tf_op jit(solution)/shard_map/ppermute | solution.py:23
  357.5 13.8 %collective-permute-start.6 = (bf16[128,5,64]{0,2,1:T(8,128)(2,1)S(1)}, bf16[128,5,64]{0,2,1:T(8,128)(2,1)S(1)}, u32[]{:S(2)}, u32[]{:S(2)}) collective-permute-start(bf16[128,5,64]{0,2,1:T(8,128)(2,1)S(1)} %bitcast.507), channel_id=1, source_target_pairs={{0,4},{4,8},{8,12},{12,16},{16,20},{20,24},{24,28},{1,5},{5,9},{9,... | collective-permute-start | bytes 245768 | tf_op jit(solution)/shard_map/ppermute | solution.py:23
  365.7 8.3 collective-permute-start.11
  371.3 5.1 collective-permute-start.7
  386.7 7.7 collective-permute-start.16
  389.0 8.5 collective-permute-start.12
  394.4 6.4 collective-permute-start.17
  397.5 6.1 collective-permute-start.13
  436.4 14.1 %collective-permute-start.20 = (bf16[256,5,64]{0,2,1:T(8,128)(2,1)}, bf16[256,5,64]{0,2,1:T(8,128)(2,1)}, u32[]{:S(2)}, u32[]{:S(2)}) collective-permute-start(bf16[256,5,64]{0,2,1:T(8,128)(2,1)} %slice.385), channel_id=1, source_target_pairs={{8,0},{12,4},{16,8},{20,12},{24,16},{28,20},{9,1},{13,5},{17,9},{2... | collective-permute-start | bytes 491528 | tf_op jit(solution)/shard_map/ppermute | solution.py:23
  441.3 7.8 collective-permute-start.18
  449.2 5.2 collective-permute-start.19
  451.5 5.8 collective-permute-start.21
  487.8 13.1 %collective-permute-start.24 = (bf16[256,5,64]{0,2,1:T(8,128)(2,1)}, bf16[256,5,64]{0,2,1:T(8,128)(2,1)}, u32[]{:S(2)}, u32[]{:S(2)}) collective-permute-start(bf16[256,5,64]{0,2,1:T(8,128)(2,1)} %slice.383), channel_id=1, source_target_pairs={{8,0},{12,4},{16,8},{20,12},{24,16},{28,20},{9,1},{13,5},{17,9},{2... | collective-permute-start | bytes 491528 | tf_op jit(solution)/shard_map/ppermute | solution.py:23
  498.2 7.5 collective-permute-start.22
  501.9 6.7 collective-permute-start.25
  505.7 6.1 collective-permute-start.23
  525.1 111.7 %collective-permute-start.28 = (bf16[256,5,64]{0,2,1:T(8,128)(2,1)}, bf16[256,5,64]{0,2,1:T(8,128)(2,1)}, u32[]{:S(2)}, u32[]{:S(2)}) collective-permute-start(bf16[256,5,64]{0,2,1:T(8,128)(2,1)} %slice.381), channel_id=1, source_target_pairs={{8,0},{12,4},{16,8},{20,12},{24,16},{28,20},{9,1},{13,5},{17,9},{2... | collective-permute-start | bytes 491528 | tf_op jit(solution)/shard_map/ppermute | solution.py:23
  531.9 107.6 %collective-permute-start.26 = (bf16[256,5,64]{0,2,1:T(8,128)(2,1)S(1)}, bf16[256,5,64]{0,2,1:T(8,128)(2,1)}, u32[]{:S(2)}, u32[]{:S(2)}) collective-permute-start(bf16[256,5,64]{0,2,1:T(8,128)(2,1)S(1)} %slice.382), channel_id=1, source_target_pairs={{8,0},{12,4},{16,8},{20,12},{24,16},{28,20},{9,1},{13,5},{17,9},{2... | collective-permute-start | bytes 491528 | tf_op jit(solution)/shard_map/ppermute | solution.py:23
  637.9 6.1 collective-permute-start.29
  641.1 8.1 collective-permute-start.27
  (169 other events, 2259.9 us)
Sparse Core Ops, SparseCore 0:
  11.5 63.7 all-gather.17
  78.7 63.7 all-gather.15
  145.9 62.5 all-gather.9
  211.8 63.1 all-gather.11
  277.7 63.1 all-gather.13
  657.4 591.9 all-reduce.10
where the time goes:
time: 1280 us; the launch traced here: 1270 us
  waiting for transfers between devices  606 us (47%)
  matrix products  178 us (14%)
  blocking collectives  143 us (11%)
  local copies, waits for them, and re-layouts  131 us (10%)
  other arithmetic  126 us (10%)
  starting transfers between devices  67.3 us (5%)
  between operations  17.8 us (1%)
    unnamed x7, waiting for transfers between devices  526 us
    dot_general x21, matrix products, left_product(): lax.dot_general(left, right, (((0,), (0,)), ((), ())), preferred_element_...  90.5 us
    ppermute x30, starting transfers between devices, passed_along(): lax.ppermute(value, axis, [(source, source + steps) for source in range(i...  67 us
    add x10, local copies, waits for them, and re-layouts, per_device(): old_share + new_share  64.8 us
    psum x1, blocking collectives, per_device(): lax.psum((gain_a_total, gain_f_total, router_grad), ('seq', 'rep'))  54.4 us
    all_gather x1, waiting for transfers between devices, per_device(): lax.all_gather(w_down.astype(narrow_float_type), ('seq', 'rep'), axis=0,...  49 us
    all_gather x1, blocking collectives, per_device(): lax.all_gather(key_weight.astype(narrow_float_type), ('seq', 'rep'), axis...  44.4 us
    all_gather x1, blocking collectives, per_device(): lax.all_gather(value_weight.astype(narrow_float_type), ('seq', 'rep'), ax...  44.1 us
  transfers between devices with their start and end apart: 36, of which 14 were waited for; matrix products, arithmetic and copies ran while one was open for 24% of the time, Pallas kernels for 0%

commit v1 on v0

--- a/solution.py
+++ b/solution.py
@@ -1,6 +1,8 @@
 import jax
 import jax.numpy as jnp
 from jax import lax
+from jax.experimental import pallas as pl
+from jax.experimental.pallas import tpu as pltpu
 from jax.sharding import PartitionSpec as P
 
 MODEL_WIDTH = 960
@@ -10,6 +12,9 @@
 FEEDFORWARD_UNITS = 2560
 LOGC = 5
 RECUR = 3
+OWN_ROWS = 30
+PADDED_ROWS = 32
+PADDED_WIDTH = 1024
 
 
 highest = lax.Precision.HIGHEST
@@ -416,7 +421,902 @@
     )
 
 
+MESH = pl.DeviceIdType.MESH
+N_Z = 4
+BLOCKS = ((32, 2688), (32, 2560), (32, 2560), (80, 1024))
+GATHER_ORDERS = ("uzw", "zuw", "uzw", "zuw")
+REDUCE_ORDERS = ("zuw", "uzw", "zuw", "uzw")
+
+
+def place():
+    seq = lax.axis_index("seq")
+    rep = lax.axis_index("rep")
+    z, x, y, core = seq // 2, seq % 2, rep // 2, rep % 2
+    return z, x + core * (y - x), y + core * (x - y), core
+
+
+def device_of(z, u, w, core):
+    x, y = u + core * (w - u), w + core * (u - w)
+    return (z * 2 + x, y * 2 + core)
+
+
+def block_of(z, u, w, core):
+    seq, rep = device_of(z, u, w, core)
+    return seq * 4 + rep
+
+
+def remote(src, dst, send_sem, recv_sem, device):
+    return pltpu.make_async_remote_copy(
+        src_ref=src,
+        dst_ref=dst,
+        send_sem=send_sem,
+        recv_sem=recv_sem,
+        device_id=device,
+        device_id_type=MESH,
+    )
+
+
+def gather_events():
+    events = [("own", group) for group in range(4)]
+    for step in range(6):
+        for group in range(4):
+            if GATHER_ORDERS[group] == "zuw":
+                if 1 <= step <= 3:
+                    events.append(("z", group, step, 0))
+                if 1 <= step <= 4:
+                    events.append(("u", group, step - 1))
+                    events.append(("w", group, step - 1, 0))
+                if 2 <= step <= 5:
+                    events.append(("w", group, step - 2, 1))
+            else:
+                if step == 1:
+                    events.append(("first", group))
+                if 1 <= step <= 3:
+                    events.append(("z", group, step, 0))
+                if 2 <= step <= 4:
+                    events.append(("z", group, step - 1, 1))
+                if 1 <= step <= 4:
+                    events.append(("w", group, step - 1, 0))
+                if 2 <= step <= 5:
+                    events.append(("w", group, step - 2, 1))
+    return events
+
+
+def gather_kernel(*refs):
+    own, full = refs[:4], refs[4:8]
+    recv_sem, z_sem, u_sem, w_sem, core_sem, local_sem = refs[8:]
+    z, u, w, core = place()
+    me = block_of(z, u, w, core)
+    above, below = device_of(z + 1, u, w, core), device_of(z - 1, u, w, core)
+    across_u, across_w = device_of(z, 1 - u, w, core), device_of(z, u, 1 - w, core)
+    sibling = device_of(z, w, u, 1 - core)
+
+    barrier = pltpu.get_barrier_semaphore()
+    for device in (across_u, across_w, sibling):
+        pl.semaphore_signal(barrier, inc=1, device_id=device, device_id_type=MESH)
+
+    @pl.when(z < N_Z - 1)
+    def _():
+        pl.semaphore_signal(barrier, inc=1, device_id=above, device_id_type=MESH)
+
+    @pl.when(z > 0)
+    def _():
+        pl.semaphore_signal(barrier, inc=1, device_id=below, device_id_type=MESH)
+
+    pl.semaphore_wait(barrier, 4 + (z + 1) // 2 - z // 3 * 2)
+
+    def rows(group, block):
+        count = BLOCKS[group][0]
+        return full[group].at[pl.ds(pl.multiple_of(block * count, 16), count)]
+
+    def copy(group, block, src, send_sem, device):
+        return remote(src, rows(group, block), send_sem, recv_sem.at[group, block], device)
+
+    def send(group, block, src, ways, slot=0):
+        if "z" in ways:
+
+            @pl.when(z < N_Z - 1)
+            def _():
+                copy(group, block, src, z_sem.at[group, 0, slot], above).start()
+
+            @pl.when(z > 0)
+            def _():
+                copy(group, block, src, z_sem.at[group, 1, slot], below).start()
+
+        if "+" in ways:
+
+            @pl.when(z < N_Z - 1)
+            def _():
+                copy(group, block, src, z_sem.at[group, 0, slot], above).start()
+
+        if "-" in ways:
+
+            @pl.when(z > 0)
+            def _():
+                copy(group, block, src, z_sem.at[group, 1, slot], below).start()
+
+        if "u" in ways:
+            copy(group, block, src, u_sem.at[group], across_u).start()
+        if "w" in ways:
+            copy(group, block, src, w_sem.at[group], across_w).start()
+        if "c" in ways:
+            copy(group, block, src, core_sem.at[group], sibling).start()
+
+    def passed_on(group, block, ways, slot=0):
+        copy(group, block, rows(group, block), core_sem.at[group], sibling).wait_recv()
+        send(group, block, rows(group, block), ways, slot)
+
+    def at_distance(step, action):
+        if step == 0:
+            action(z, "")
+            return
+
+        @pl.when(z - step >= 0)
+        def _():
+            action(z - step, "+")
+
+        @pl.when(z + step < N_Z)
+        def _():
+            action(z + step, "-")
+
+    def own_event(group):
+        send(group, me, own[group], "zuwc")
+        pltpu.make_async_copy(own[group], rows(group, me), local_sem.at[group]).start()
+
+    def first_event(group):
+        passed_on(group, block_of(z, 1 - u, w, core), "zwc", 1)
+
+    def z_event(group, step, other):
+        z_first = GATHER_ORDERS[group] == "zuw"
+        column = 1 - u if other else u
+        slot = step if z_first else 2 * step + other
+        at_distance(
+            step,
+            lambda far, way: passed_on(
+                group,
+                block_of(far, column, w, core),
+                way + ("uwc" if z_first else "wc"),
+                slot,
+            ),
+        )
+
+    def u_event(group, step):
+        at_distance(
+            step, lambda far, way: passed_on(group, block_of(far, 1 - u, w, core), "wc")
+        )
+
+    def w_event(group, step, other):
+        column = 1 - u if other else u
+        at_distance(
+            step, lambda far, way: passed_on(group, block_of(far, column, 1 - w, core), "c")
+        )
+
+    actions = {"own": own_event, "first": first_event, "z": z_event, "u": u_event, "w": w_event}
+    for event in gather_events():
+        actions[event[0]](*event[1:])
+
+    for group in range(4):
+        z_first = GATHER_ORDERS[group] == "zuw"
+        count = BLOCKS[group][0]
+        pltpu.make_async_copy(own[group], rows(group, me), local_sem.at[group]).wait()
+
+        @pl.loop(0, 16)
+        def _(i):
+            block = i * 2 + (1 - core)
+            copy(group, block, rows(group, block), core_sem.at[group], sibling).wait_recv()
+
+        for sem, sends in ((u_sem, 4 if z_first else 1), (w_sem, 8), (core_sem, 16)):
+            part = full[group].at[pl.ds(0, sends * count)]
+            remote(part, part, sem.at[group], recv_sem.at[group, 0], sibling).wait_send()
+        for step in range(N_Z):
+            for other in (0,) if z_first else (0, 1):
+                slot = step if z_first else 2 * step + other
+
+                @pl.when((z - step >= 0) & (z < N_Z - 1))
+                def _():
+                    copy(group, me, own[group], z_sem.at[group, 0, slot], above).wait_send()
+
+                @pl.when((z + step < N_Z) & (z > 0))
+                def _():
+                    copy(group, me, own[group], z_sem.at[group, 1, slot], below).wait_send()
+
+
+def gather_weights(packed):
+    sems = pltpu.SemaphoreType.DMA
+    return pl.pallas_call(
+        gather_kernel,
+        out_shape=[
+            jax.ShapeDtypeStruct((32 * rows, columns), jnp.bfloat16) for rows, columns in BLOCKS
+        ],
+        in_specs=[pl.BlockSpec(memory_space=pl.ANY)] * 4,
+        out_specs=[pl.BlockSpec(memory_space=pl.ANY)] * 4,
+        scratch_shapes=[
+            sems((4, 32)),
+            sems((4, 2, 8)),
+            sems((4,)),
+            sems((4,)),
+            sems((4,)),
+            sems((4,)),
+        ],
+        compiler_params=pltpu.CompilerParams(
+            collective_id=1, has_side_effects=True, vmem_limit_bytes=16 * 2**20
+        ),
+        name="gather_weights",
+    )(*packed)
+
+
+def reduce_events():
+    events = [("small", -1)]
+
+    def entry(group):
+        return [("core", group, plane) for plane in range(4)] + [
+            ("w", group, step) for step in (3, 2, 1, 0)
+        ]
+
+    def middle(group):
+        kind = "u" if REDUCE_ORDERS[group] == "zuw" else "z_early"
+        return [(kind, group, step) for step in (3, 2, 1, 0)]
+
+    def last(group):
+        if REDUCE_ORDERS[group] == "zuw":
+            return [("z_late", group, step) for step in (3, 2, 1, 0)]
+        return [("u_late", group)]
+
+    for stage in (
+        entry(0),
+        entry(1),
+        [("small", 0)],
+        middle(0),
+        entry(2),
+        [("small", 1)],
+        middle(1),
+        last(0),
+        [("small", 2)],
+        entry(3),
+        middle(2),
+        [("small", 3)],
+        last(1),
+        middle(3),
+        [("small", 4)],
+        last(2),
+        last(3),
+    ):
+        events += stage
+    return events
+
+
+def reduce_kernel(*refs):
+    partial, small_in, final, small_out = refs[:4], refs[4], refs[5:9], refs[9]
+    part, from_core, from_w, from_u, from_z = (refs[10 + 4 * i : 14 + 4 * i] for i in range(5))
+    small_held, small_got = refs[30:32]
+    (
+        local_sem,
+        core_send,
+        core_recv,
+        w_send,
+        w_recv,
+        u_send,
+        u_recv,
+        z_send,
+        z_recv,
+        small_send,
+        small_recv,
+    ) = refs[32:]
+    z, u, w, core = place()
+    me = block_of(z, u, w, core)
+    above, below = device_of(z + 1, u, w, core), device_of(z - 1, u, w, core)
+    across_u, across_w = device_of(z, 1 - u, w, core), device_of(z, u, 1 - w, core)
+    sibling = device_of(z, w, u, 1 - core)
+    near, far_z = z + 1 - 2 * (z % 2), (z + 2) % 4
+    partners = (
+        sibling,
+        across_u,
+        across_w,
+        device_of(near, u, w, core),
+        device_of(far_z, u, w, core),
+    )
+    middle_z = (z == 1) | (z == 2)
+
+    barrier = pltpu.get_barrier_semaphore()
+    for device in partners:
+        pl.semaphore_signal(barrier, inc=1, device_id=device, device_id_type=MESH)
+
+    @pl.when(middle_z)
+    def _():
+        pl.semaphore_signal(
+            barrier, inc=1, device_id=device_of(3 - z, u, w, core), device_id_type=MESH
+        )
+
+    def plane_rows(group, ref, plane):
+        count = 8 * BLOCKS[group][0]
+        return ref.at[pl.ds(plane * count, count)]
+
+    def load(group, plane):
+        return pltpu.make_async_copy(
+            plane_rows(group, partial[group], plane),
+            plane_rows(group, part[group], plane),
+            local_sem.at[group, plane],
+        )
+
+    for group in range(4):
+        for plane in range(4):
+            load(group, plane).start()
+
+    pl.semaphore_wait(barrier, 5 + (z + 1) // 2 - z // 3 * 2)
+
+    def rows(group, block):
+        count = BLOCKS[group][0]
+        return part[group].at[pl.ds(pl.multiple_of(block * count, 16), count)]
+
+    def slot_of(far, column, line):
+        return (far * 2 + column) * 2 + line
+
+    def small_copy(i):
+        return remote(
+            small_held.at[i], small_got.at[i], small_send.at[i], small_recv.at[i], partners[i]
+        )
+
+    def small_event(i):
+        if i < 0:
+            small_held[0] = small_in[...]
+            small_copy(0).start()
+            return
+        small_copy(i).wait_recv()
+        total = small_held[i] + small_got[i]
+        if i < 4:
+            small_held[i + 1] = total
+            small_copy(i + 1).start()
+        else:
+            small_out[...] = total
+
+    def core_event(group, plane):
+        load(group, plane).wait()
+        for column in (0, 1):
+            for line in (0, 1):
+                slot = slot_of(plane, column, line)
+                remote(
+                    rows(group, block_of(plane, column, line, 1 - core)),
+                    from_core[group].at[slot],
+                    core_send.at[group],
+                    core_recv.at[group, slot],
+                    sibling,
+                ).start()
+
+    def wait_core(group, slot):
+        held = from_core[group].at[slot]
+        remote(held, held, core_send.at[group], core_recv.at[group, slot], sibling).wait_recv()
+
+    def accumulate(group, block, terms):
+        count = BLOCKS[group][0]
+        first = pl.multiple_of(block * count, 16)
+
+        @pl.loop(0, count // 16)
+        def _(i):
+            at = pl.multiple_of(i * 16, 16)
+            total = part[group][pl.ds(first + at, 16), :].astype(jnp.float32)
+            for ref, slot in terms:
+                total = total + ref[slot, pl.ds(at, 16), :].astype(jnp.float32)
+            part[group][pl.ds(first + at, 16), :] = total.astype(jnp.bfloat16)
+
+    def at_distance(step, action):
+        if step == 0:
+            action(z, 0)
+            return
+
+        @pl.when(z + step < N_Z)
+        def _():
+            action(z + step, 1)
+
+        @pl.when(z - step >= 0)
+        def _():
+            action(z - step, -1)
+
+    def wait_w(group, slot):
+        held = from_w[group].at[slot]
+        remote(held, held, w_send.at[group], w_recv.at[group, slot], across_w).wait_recv()
+
+    def w_event(group, step):
+        def action(far, way, column):
+            block, slot = block_of(far, column, 1 - w, core), slot_of(far, column, 1 - w)
+            wait_core(group, slot)
+            accumulate(group, block, [(from_core[group], slot)])
+            remote(
+                rows(group, block),
+                from_w[group].at[far * 2 + column],
+                w_send.at[group],
+                w_recv.at[group, far * 2 + column],
+                across_w,
+            ).start()
+
+        for column in (1 - u, u):
+            at_distance(step, lambda far, way: action(far, way, column))
+
+    def gathered(group, far, column):
+        slot = slot_of(far, column, w)
+        wait_core(group, slot)
+        wait_w(group, far * 2 + column)
+        return [(from_core[group], slot), (from_w[group], far * 2 + column)]
+
+    def u_copy(group, src, slot):
+        return remote(
+            src, from_u[group].at[slot], u_send.at[group], u_recv.at[group, slot], across_u
+        )
+
+    def u_event(group, step):
+        def action(far, way):
+            block = block_of(far, 1 - u, w, core)
+            accumulate(group, block, gathered(group, far, 1 - u))
+            u_copy(group, rows(group, block), far).start()
+
+        at_distance(step, action)
+
+    def z_copy(group, block, way, slot):
+        return remote(
+            rows(group, block),
+            from_z[group].at[way, slot],
+            z_send.at[group, way, slot],
+            z_recv.at[group, way, slot],
+            below if way else above,
+        )
+
+    def z_take(group, block, way, slot):
+        z_copy(group, block, way, slot).wait_recv()
+        accumulate(group, block, [(from_z[group].at[way], slot)])
+
+    def z_step(group, step, column, z_slot, terms_of):
+        def action(far, way):
+            block, slot = block_of(far, column, w, core), z_slot(far)
+            accumulate(group, block, terms_of(far))
+            if way >= 0:
+
+                @pl.when(z > 0)
+                def _():
+                    z_take(group, block, 0, slot)
+
+            if way <= 0:
+
+                @pl.when(z < N_Z - 1)
+                def _():
+                    z_take(group, block, 1, slot)
+
+            if way:
+                z_copy(group, block, 0 if way > 0 else 1, slot).start()
+
+        at_distance(step, action)
+
+    def finish(group):
+        count = BLOCKS[group][0]
+        final[group][...] = part[group][
+            pl.ds(pl.multiple_of(me * count, 16), count), :
+        ].astype(jnp.float32)
+
+    def z_late_event(group, step):
+        def terms_of(far):
+            terms = gathered(group, far, u)
+            u_copy(group, from_u[group].at[far], far).wait_recv()
+            return terms + [(from_u[group], far)]
+
+        z_step(group, step, u, lambda far: far, terms_of)
+        if step == 0:
+            finish(group)
+
+    def z_early_event(group, step):
+        for column in (1 - u, u):
+            z_step(
+                group,
+                step,
+                column,
+                lambda far: far * 2 + column,
+                lambda far: gathered(group, far, column),
+            )
+            if step == 0 and column is not u:
+                u_copy(group, rows(group, block_of(z, 1 - u, w, core)), 0).start()
+
+    def u_late_event(group):
+        u_copy(group, from_u[group].at[0], 0).wait_recv()
+        accumulate(group, me, [(from_u[group], 0)])
+        finish(group)
+
+    actions = {
+        "small": small_event,
+        "core": core_event,
+        "w": w_event,
+        "u": u_event,
+        "z_early": z_early_event,
+        "z_late": z_late_event,
+        "u_late": u_late_event,
+    }
+    for event in reduce_events():
+        actions[event[0]](*event[1:])
+
+    for group in range(4):
+        z_first = REDUCE_ORDERS[group] == "zuw"
+        count = BLOCKS[group][0]
+        for sem, sends in ((core_send, 16), (w_send, 8), (u_send, 4 if z_first else 1)):
+            rows_sent = part[group].at[pl.ds(0, sends * count)]
+            remote(
+                rows_sent, rows_sent, sem.at[group], core_recv.at[group, 0], sibling
+            ).wait_send()
+        for far in range(N_Z):
+            for column in (0,) if z_first else (0, 1):
+                slot = far if z_first else far * 2 + column
+
+                @pl.when(z < far)
+                def _():
+                    z_copy(group, me, 0, slot).wait_send()
+
+                @pl.when(z > far)
+                def _():
+                    z_copy(group, me, 1, slot).wait_send()
+
+    for i in range(5):
+        small_copy(i).wait_send()
+
+
+def reduce_gradients(partials, small):
+    narrow, sems = jnp.bfloat16, pltpu.SemaphoreType.DMA
+    z_first = [order == "zuw" for order in REDUCE_ORDERS]
+    scratch = [pltpu.VMEM((32 * rows, columns), narrow) for rows, columns in BLOCKS]
+    scratch += [pltpu.VMEM((16, rows, columns), narrow) for rows, columns in BLOCKS]
+    scratch += [pltpu.VMEM((8, rows, columns), narrow) for rows, columns in BLOCKS]
+    scratch += [
+        pltpu.VMEM((4 if first else 1, rows, columns), narrow)
+        for (rows, columns), first in zip(BLOCKS, z_first)
+    ]
+    scratch += [
+        pltpu.VMEM((2, 4 if first else 8, rows, columns), narrow)
+        for (rows, columns), first in zip(BLOCKS, z_first)
+    ]
+    scratch += [pltpu.VMEM((5, 8, 1024), jnp.float32)] * 2
+    scratch += [
+        sems((4, 4)),
+        sems((4,)),
+        sems((4, 16)),
+        sems((4,)),
+        sems((4, 8)),
+        sems((4,)),
+        sems((4, 4)),
+        sems((4, 2, 8)),
+        sems((4, 2, 8)),
+        sems((5,)),
+        sems((5,)),
+    ]
+    return pl.pallas_call(
+        reduce_kernel,
+        out_shape=[jax.ShapeDtypeStruct(shape, jnp.float32) for shape in BLOCKS]
+        + [jax.ShapeDtypeStruct((8, 1024), jnp.float32)],
+        in_specs=[pl.BlockSpec(memory_space=pl.ANY)] * 4
+        + [pl.BlockSpec(memory_space=pltpu.VMEM)],
+        out_specs=[pl.BlockSpec(memory_space=pltpu.VMEM)] * 5,
+        scratch_shapes=scratch,
+        compiler_params=pltpu.CompilerParams(
+            collective_id=2, has_side_effects=True, vmem_limit_bytes=58 * 2**20
+        ),
+        name="reduce_gradients",
+    )(*partials, small)
+
+
+def per_device_fast(
+    tokens,
+    depths,
+    seq_spans,
+    cotangent,
+    w_query,
+    key_weight,
+    value_weight,
+    w_out,
+    w_gate,
+    w_up,
+    w_down,
+    attn_gain,
+    ffn_gain,
+    router,
+):
+    narrow, wide = jnp.bfloat16, jnp.float32
+    count_of_rows = tokens.shape[1]
+    query_groupings = QUERY_HEADS // KEY_VALUE_HEADS
+    chain = lax.axis_size("seq")
+    most_spans = min(2**LOGC, chain // 2)
+    depth_levels = (most_spans - 1).bit_length()
+    extra_rows = ((1 << depth_levels) - most_spans) * count_of_rows
+    window = most_spans * count_of_rows
+    natural = jnp.arange(MODEL_WIDTH, dtype=jnp.int32)
+    padded_at = (natural // OWN_ROWS) * PADDED_ROWS + natural % OWN_ROWS
+    spread = (padded_at[:, None] == jnp.arange(PADDED_WIDTH, dtype=jnp.int32)[None, :]).astype(narrow)
+    packed = pack_weights(
+        spread, w_query, key_weight, value_weight, w_out, w_gate, w_up, w_down
+    )
+    attention_full, gate_full, up_full, down_full = gather_weights(packed)
+    w_q = attention_full[:, :960]
+    w_k = attention_full[:, 960:1280]
+    w_v = attention_full[:, 1280:1600]
+    w_o = attention_full[:, 1664:]
+
+    def spread_vector(v):
+        return jnp.dot(v, spread.astype(wide), precision=highest)
+
+    gain_a, gain_f, routers = spread_vector(attn_gain), spread_vector(ffn_gain), spread_vector(router)
+
+    def rms_parts_padded(vectors, gain):
+        mean = jnp.sum(vectors * vectors, axis=-1, keepdims=True) / MODEL_WIDTH
+        inv_rms = lax.rsqrt(mean + epsilon)
+        normal_part = vectors * inv_rms
+        return (normal_part * gain, normal_part, inv_rms)
+
+    def rms_backward_padded(upstream, normal_part, inv_rms, gain):
+        gain_grad = jnp.sum(upstream * normal_part, axis=0)
+        scaled = upstream * gain
+        inner = jnp.sum(scaled * normal_part, axis=-1, keepdims=True) / MODEL_WIDTH
+        return (inv_rms * (scaled - normal_part * inner), gain_grad)
+
+    place_index = lax.axis_index("seq")
+    lengths = seq_spans[0]
+    seq_ends = jnp.cumsum(lengths)
+    span_ids = jnp.arange(chain, dtype=jnp.int32)
+    owners = jnp.sum((seq_ends[None, :] <= span_ids[:, None]).astype(jnp.int32), axis=1)
+    seq_starts = seq_ends - lengths
+    numbers = jnp.arange(lengths.shape[0], dtype=jnp.int32)
+    first_span = jnp.sum(
+        jnp.where(numbers[None, :] == owners[:, None], seq_starts[None, :], 0), axis=1
+    )
+    index_of_span = jnp.sum(jnp.where(span_ids == place_index, span_ids - first_span, 0))
+    positions = (index_of_span * count_of_rows + jnp.arange(count_of_rows, dtype=jnp.int32)).astype(
+        wide
+    )
+    cosine_table, sine_table = angle_tables(positions, HEAD_SIZE)
+    row_ids = jnp.arange(count_of_rows, dtype=jnp.int32)
+    col_ids = jnp.arange(window, dtype=jnp.int32)
+    offsets = most_spans - 1 - col_ids // count_of_rows
+    local_col = col_ids - (most_spans - 1) * count_of_rows
+    causal = jnp.where(offsets[None, :] == 0, local_col[None, :] <= row_ids[:, None], True)
+    diagonal = (offsets[None, :] == 0) & (local_col[None, :] == row_ids[:, None])
+    span_ok = (index_of_span >= offsets)[None, :]
+    active_all = (depths[0][None, :] > jnp.arange(RECUR, dtype=jnp.int32)[:, None]).astype(wide)
+    depth_win = depths[0].astype(narrow)
+    for level in range(depth_levels):
+        depth_win = jnp.concatenate([passed_along(depth_win, "seq", 1 << level), depth_win], axis=0)
+    hidden_state = unscaled_product(tokens[0], spread)
+    saved = []
+    for recursion in range(RECUR):
+        current_active = active_all[recursion]
+        normalized, normal_a, inv_a = rms_parts_padded(hidden_state, gain_a)
+        a_b = normalized.astype(narrow)
+        raw_query = unscaled_product(a_b, w_q).reshape(count_of_rows, QUERY_HEADS, HEAD_SIZE)
+        query_b = (
+            apply_rotation(raw_query, cosine_table, sine_table)
+            .astype(narrow)
+            .reshape(count_of_rows, KEY_VALUE_HEADS, query_groupings, HEAD_SIZE)
+        )
+        unrotated_key = unscaled_product(a_b, w_k).reshape(
+            count_of_rows, KEY_VALUE_HEADS, HEAD_SIZE
+        )
+        key_b = apply_rotation(unrotated_key, cosine_table, sine_table).astype(narrow)
+        value_b = (
+            unscaled_product(a_b, w_v)
+            .astype(narrow)
+            .reshape(count_of_rows, KEY_VALUE_HEADS, HEAD_SIZE)
+        )
+        pair = jnp.concatenate([key_b, value_b], axis=1)
+        for level in range(depth_levels):
+            pair = jnp.concatenate([passed_along(pair, "seq", 1 << level), pair], axis=0)
+        keys_win, values_win = pair[:, :KEY_VALUE_HEADS], pair[:, KEY_VALUE_HEADS:]
+        allowed = span_ok & causal & ((depth_win > recursion)[None, :] | diagonal)
+        scores = masked_scores(query_b, keys_win, allowed)
+        row_max = jnp.max(scores, axis=-1, keepdims=True)
+        expon = jnp.exp(scores - row_max)
+        row_total = jnp.sum(expon, axis=-1, keepdims=True)
+        probs_b = (expon / row_total).astype(narrow)
+        log_total = row_max + jnp.log(row_total)
+        attended_b = (
+            jnp.einsum("gjqk,kgd->qgjd", probs_b, values_win, preferred_element_type=wide)
+            .astype(narrow)
+            .reshape(count_of_rows, QUERY_HEADS * HEAD_SIZE)
+        )
+        attended_b = unscaled_product(attended_b, spread).astype(narrow)
+        branch = unscaled_product(attended_b, w_o)
+        middle = hidden_state + branch
+        second, normal_z, inv_z = rms_parts_padded(middle, gain_f)
+        second_b = second.astype(narrow)
+        gate_value = unscaled_product(second_b, gate_full)
+        up_value = unscaled_product(second_b, up_full)
+        hidden_b = (jax.nn.silu(gate_value) * up_value).astype(narrow)
+        ffn_out = unscaled_product(hidden_b, down_full)
+        weight_gate = jax.nn.sigmoid(jnp.dot(hidden_state, routers[recursion], precision=highest))
+        saved.append(
+            (
+                hidden_state,
+                a_b,
+                normal_a,
+                inv_a,
+                query_b,
+                keys_win,
+                values_win,
+                allowed,
+                log_total,
+                attended_b,
+                branch,
+                normal_z,
+                inv_z,
+                second_b,
+                gate_value,
+                up_value,
+                hidden_b,
+                ffn_out,
+                weight_gate,
+                current_active,
+            )
+        )
+        hidden_state = hidden_state + (current_active * weight_gate)[:, None] * (branch + ffn_out)
+    output = right_product(hidden_state.astype(narrow), spread).astype(narrow)
+    gain_a_total = jnp.zeros((PADDED_WIDTH,), wide)
+    gain_f_total = jnp.zeros((PADDED_WIDTH,), wide)
+    router_rows = [None] * RECUR
+    factors = []
+    grad_state = unscaled_product(cotangent[0], spread)
+    for recursion in reversed(range(RECUR)):
+        (
+            state_in,
+            a_b,
+            normal_a,
+            inv_a,
+            query_b,
+            keys_win,
+            values_win,
+            allowed,
+            log_total,
+            attended_b,
+            branch,
+            normal_z,
+            inv_z,
+            second_b,
+            gate_value,
+            up_value,
+            hidden_b,
+            ffn_out,
+            weight_gate,
+            current_active,
+        ) = saved[recursion]
+        mixing = current_active * weight_gate
+        grad_delta = mixing[:, None] * grad_state
+        grad_mix = jnp.sum(grad_state * (branch + ffn_out), axis=-1)
+        grad_logit = current_active * grad_mix * weight_gate * (1.0 - weight_gate)
+        router_rows[recursion] = jnp.dot(grad_logit, state_in, precision=highest)
+        grad_next = grad_state + grad_logit[:, None] * routers[recursion][None, :]
+        ffn_grad_b = grad_delta.astype(narrow)
+        grad_hidden = right_product(ffn_grad_b, down_full)
+        sigmoid_gate = jax.nn.sigmoid(gate_value)
+        grad_gate_b = (
+            grad_hidden * up_value * sigmoid_gate * (1.0 + gate_value * (1.0 - sigmoid_gate))
+        ).astype(narrow)
+        grad_up_b = (grad_hidden * gate_value * sigmoid_gate).astype(narrow)
+        grad_second = right_product(grad_gate_b, gate_full) + right_product(grad_up_b, up_full)
+        grad_middle, gain_f_part = rms_backward_padded(grad_second, normal_z, inv_z, gain_f)
+        gain_f_total = gain_f_total + gain_f_part
+        grad_branch_b = (grad_delta + grad_middle).astype(narrow)
+        grad_attended_b = right_product(
+            right_product(grad_branch_b, w_o).astype(narrow), spread
+        ).astype(narrow).reshape(count_of_rows, KEY_VALUE_HEADS, query_groupings, HEAD_SIZE)
+        grad_next = grad_next + grad_middle
+        scores = masked_scores(query_b, keys_win, allowed)
+        probs = jnp.exp(scores - log_total)
+        probs_b = probs.astype(narrow)
+        grad_probs = jnp.einsum(
+            "qgjd,kgd->gjqk", grad_attended_b, values_win, preferred_element_type=wide
+        )
+        row_dot = jnp.sum(probs * grad_probs, axis=-1, keepdims=True)
+        grad_scores_b = (probs * (grad_probs - row_dot)).astype(narrow)
+        grad_queries = (
+            jnp.einsum("gjqk,kgd->qgjd", grad_scores_b, keys_win, preferred_element_type=wide)
+            * 0.125
+        )
+        grad_keys = (
+            jnp.einsum("gjqk,qgjd->kgd", grad_scores_b, query_b, preferred_element_type=wide)
+            * 0.125
+        )
+        grad_values = jnp.einsum(
+            "gjqk,qgjd->kgd", probs_b, grad_attended_b, preferred_element_type=wide
+        )
+        local_pair = jnp.concatenate(
+            [
+                jnp.zeros((extra_rows, 2 * KEY_VALUE_HEADS, HEAD_SIZE), wide),
+                jnp.concatenate([grad_keys, grad_values], axis=1),
+            ],
+            axis=0,
+        )
+        for level in reversed(range(depth_levels)):
+            older_rows = (1 << level) * count_of_rows
+            back = passed_along(for_sending(local_pair[:older_rows]), "seq", -(1 << level))
+            local_pair = local_pair[older_rows:] + back
+        grad_query_b = (
+            apply_rotation(
+                grad_queries.reshape(count_of_rows, QUERY_HEADS, HEAD_SIZE),
+                cosine_table,
+                -sine_table,
+            )
+            .astype(narrow)
+            .reshape(count_of_rows, QUERY_HEADS * HEAD_SIZE)
+        )
+        grad_key_b = (
+            apply_rotation(local_pair[:, :KEY_VALUE_HEADS], cosine_table, -sine_table)
+            .astype(narrow)
+            .reshape(count_of_rows, KEY_VALUE_HEADS * HEAD_SIZE)
+        )
+        grad_value_b = (
+            local_pair[:, KEY_VALUE_HEADS:]
+            .astype(narrow)
+            .reshape(count_of_rows, KEY_VALUE_HEADS * HEAD_SIZE)
+        )
+        grad_qkv_b = jnp.concatenate([grad_query_b, grad_key_b, grad_value_b], axis=1)
+        grad_normed = right_product(grad_qkv_b, attention_full[:, :1600])
+        grad_input, gain_a_part = rms_backward_padded(grad_normed, normal_a, inv_a, gain_a)
+        gain_a_total = gain_a_total + gain_a_part
+        grad_state = grad_next + grad_input
+        factors.append(
+            (a_b, grad_qkv_b, attended_b, grad_branch_b, second_b, grad_gate_b, grad_up_b, hidden_b, ffn_grad_b)
+        )
+    a_all, qkv_all, o_all, t_all, b_all, gate_all, up_all, hidden_all, f_all = (
+        jnp.concatenate(parts, axis=0) for parts in zip(*factors)
+    )
+    d_qkv = left_product(a_all, jnp.pad(qkv_all, ((0, 0), (0, 64))))
+    partials = (
+        jnp.concatenate([d_qkv, left_product(o_all, t_all)], axis=1).astype(narrow),
+        left_product(b_all, gate_all).astype(narrow),
+        left_product(b_all, up_all).astype(narrow),
+        left_product(hidden_all, f_all).astype(narrow),
+    )
+    small = jnp.concatenate(
+        [jnp.stack([gain_a_total, gain_f_total]), jnp.stack(router_rows), jnp.zeros((3, PADDED_WIDTH), wide)]
+    )
+    attention_sum, gate_sum, up_sum, down_sum, small_sum = reduce_gradients(partials, small)
+
+    def gather_columns(x):
+        return x.reshape(x.shape[0], 32, PADDED_ROWS)[:, :, :OWN_ROWS].reshape(x.shape[0], MODEL_WIDTH)
+
+    small_natural = gather_columns(small_sum)
+    own = attention_sum[:OWN_ROWS]
+    return (
+        output[None],
+        gather_columns(grad_state)[None],
+        own[:, :960].reshape(-1),
+        own[:, 960:1280].reshape(-1),
+        own[:, 1280:1600].reshape(-1),
+        gather_columns(own[:, 1664:]).reshape(-1),
+        gate_sum[:OWN_ROWS].reshape(-1),
+        up_sum[:OWN_ROWS].reshape(-1),
+        gather_columns(down_sum).reshape(-1),
+        small_natural[0],
+        small_natural[1],
+        small_natural[2:5],
+    )
+
+
+def pack_weights(spread, w_query, key_weight, value_weight, w_out, w_gate, w_up, w_down):
+    narrow = jnp.bfloat16
+
+    def rows(flat):
+        return flat.astype(narrow).reshape(OWN_ROWS, -1)
+
+    attention = jnp.concatenate(
+        [
+            rows(w_query),
+            rows(key_weight),
+            rows(value_weight),
+            jnp.zeros((OWN_ROWS, 64), narrow),
+            unscaled_product(rows(w_out), spread).astype(narrow),
+        ],
+        axis=1,
+    )
+    extra = ((0, PADDED_ROWS - OWN_ROWS), (0, 0))
+    return (
+        jnp.pad(attention, extra),
+        jnp.pad(rows(w_gate), extra),
+        jnp.pad(rows(w_up), extra),
+        unscaled_product(w_down.astype(narrow).reshape(-1, MODEL_WIDTH), spread).astype(narrow),
+    )
+
+
 def solution(mesh):
+    fits = mesh.shape["seq"] == 8 and mesh.shape["rep"] == 4
     placed = (
         P("rep", "seq", None),
         P("rep", "seq"),
@@ -434,7 +1334,7 @@
         P(),
     )
     return jax.shard_map(
-        per_device,
+        per_device_fast if fits else per_device,
         mesh=mesh,
         in_specs=placed,
         out_specs=(

time: 1280 us -> 488 us (0.38)
  waiting for transfers between devices: 606 us -> 36.7 us
  Pallas kernels: 0 us -> 214 us
  blocking collectives: 143 us -> 0 us
  other arithmetic: 126 us -> 23.6 us
  local copies, waits for them, and re-layouts: 131 us -> 39.9 us
  matrix products: 178 us -> 120 us
  starting transfers between devices: 67.3 us -> 39.9 us
  between operations: 17.8 us -> 4.96 us
    unnamed x7 -> x0, waiting for transfers between devices: 526 us -> none
    pallas_call x0 -> x2, Pallas kernels: none -> 214 us  [the longest x1 132 us: reduce_gradients(): pl.pallas_call(reduce_kernel, out_shape=[jax.ShapeDtypeStruct(shape, jnp....]
    all_gather x4 -> x0, other arithmetic: 89 us -> none  [the longest x1 40.9 us: per_device(): lax.all_gather(w_out.astype(narrow_float_type), ('seq', 'rep'), axis=0, t...]
    all_gather x2 -> x0, blocking collectives: 88.5 us -> none  [the longest x1 44.4 us: per_device(): lax.all_gather(key_weight.astype(narrow_float_type), ('seq', 'rep'), axis...]
    dot_general x21 -> x5, matrix products: 90.5 us -> 19.4 us  [left_product(): lax.dot_general(left, right, (((0,), (0,)), ((), ())), preferred_element_...]
    add x10 -> x0, local copies, waits for them, and re-layouts: 64.8 us -> none  [per_device(): old_share + new_share]
    all_gather x5 -> x0, waiting for transfers between devices: 62.9 us -> none  [the longest x1 49 us: per_device(): lax.all_gather(w_down.astype(narrow_float_type), ('seq', 'rep'), axis=0,...]
    psum x1 -> x0, blocking collectives: 54.4 us -> none  [per_device(): lax.psum((gain_a_total, gain_f_total, router_grad), ('seq', 'rep'))]
  transfers between devices with their start and end apart: 36 -> 14, of which waited for: 14 -> 11; matrix products, arithmetic and copies ran while one was open for 24% -> 5% of each run, Pallas kernels for 0% -> 0%
where the time goes in v1:
time: 488 us; the launch traced here: 479 us
  Pallas kernels  214 us (44%)
  matrix products  120 us (25%)
  local copies, waits for them, and re-layouts  39.9 us (8%)
  starting transfers between devices  39.9 us (8%)
  waiting for transfers between devices  36.7 us (8%)
  other arithmetic  23.6 us (5%)
  between operations  4.96 us (1%)
    pallas_call x1, Pallas kernels, reduce_gradients(): pl.pallas_call(reduce_kernel, out_shape=[jax.ShapeDtypeStruct(shape, jnp....  132 us
    pallas_call x1, Pallas kernels, gather_weights(): pl.pallas_call(gather_kernel, out_shape=[jax.ShapeDtypeStruct((32 * rows,...  82.4 us
    ppermute x14, starting transfers between devices, passed_along(): lax.ppermute(value, axis, [(source, source + steps) for source in range(i...  39.9 us
    ppermute x14, waiting for transfers between devices, passed_along(): lax.ppermute(value, axis, [(source, source + steps) for source in range(i...  36.7 us
    dot_general x28, matrix products, unscaled_product(): return jnp.dot(left, right, preferred_element_type=jnp.float32)  36.2 us
    dot_general x16, matrix products, right_product(): lax.dot_general(left, right, (((1,), (1,)), ((), ())), preferred_element_...  33.9 us
    unnamed x372, local copies, waits for them, and re-layouts  19.9 us
    dot_general x5, matrix products, left_product(): lax.dot_general(left, right, (((0,), (0,)), ((), ())), preferred_element_...  19.4 us
  transfers between devices with their start and end apart: 14, of which 11 were waited for; matrix products, arithmetic and copies ran while one was open for 5% of the time, Pallas kernels for 0%

profile of v1, /device:TPU:1, one launch (start us, length us, event | category | flops | bytes accessed | tf_op | source)
XLA Modules:
  0.0 479.4 jit_solution(8922201721912510926)
XLA Ops:
  0.7 2.5 multiply_reduce_fusion.20
  11.8 82.4 %gather_weights.1 = (bf16[1024,2688]{1,0:T(8,128)(2,1)S(1)}, bf16[1024,2560]{1,0:T(8,128)(2,1)S(1)}, bf16[1024,2560]{1,0:T(8,128)(2,1)S(1)}, bf16[2560,1024]{1,0:T(8,128)(2,1)S(1)}) custom-call(bf16[32,2688]{1,0:T(8,128)(2,1)S(1)} %pad.15.refs_0_, bf16[32,2560]{1,0:T(8,128)(2,1)S(1)} %pad.16.refs_1_, bf16[32,2560]{1,0:T(8,128)(2,1)S(1)} %pad.17.refs_2_, ...), custom_call_target="tpu_custom_call" | custom-call | tf_op jit(solution)/shard_map/gather_weights/pallas_call | solution.py:626
  106.2 3.1 collective-permute-start
  109.4 3.4 collective-permute-start.2
  112.8 2.5 fusion.89
  119.8 3.3 collective-permute-start.3
  123.9 3.6 collective-permute-start.1
  128.1 4.5 collective-permute-done.1
  137.1 2.8 slice-done.19
  144.6 2.7 multiply_reduce_fusion.18
  149.8 3.2 collective-permute-start.4
  155.3 6.1 %collective-permute-start.5 = (bf16[256,10,64]{0,2,1:T(8,128)(2,1)S(1)}, bf16[256,10,64]{0,2,1:T(8,128)(2,1)S(1)}, u32[]{:S(2)}, u32[]{:S(2)}) collective-permute-start(bf16[256,10,64]{0,2,1:T(8,128)(2,1)S(1)} %maximum_maximum_fusion.4), channel_id=1, source_target_pairs={{0,8},{4,12},{8,16},{12,20},{16,24},{20,28},{1,9},{5,13},{9,17},{1... | collective-permute-start | bytes 983048 | tf_op jit(solution)/shard_map/ppermute | solution.py:28
  172.9 2.7 multiply_reduce_fusion.16
  183.6 6.5 %collective-permute-start.7 = (bf16[256,10,64]{0,2,1:T(8,128)(2,1)S(1)}, bf16[256,10,64]{0,2,1:T(8,128)(2,1)S(1)}, u32[]{:S(2)}, u32[]{:S(2)}) collective-permute-start(bf16[256,10,64]{0,2,1:T(8,128)(2,1)S(1)} %maximum_maximum_fusion.5), channel_id=1, source_target_pairs={{0,8},{4,12},{8,16},{12,20},{16,24},{20,28},{1,9},{5,13},{9,17},{1... | collective-permute-start | bytes 983048 | tf_op jit(solution)/shard_map/ppermute | solution.py:28
  207.3 3.7 multiply_reduce_fusion.14
  211.1 3.0 fusion.142
  214.1 3.2 fusion.6
  223.9 5.0 %collective-permute-done.8 = bf16[256,10,64]{0,2,1:T(8,128)(2,1)S(1)} collective-permute-done((bf16[256,10,64]{0,2,1:T(8,128)(2,1)S(1)}, bf16[256,10,64]{0,2,1:T(8,128)(2,1)S(1)}, u32[]{:S(2)}, u32[]{:S(2)}) %collective-permute-start.8) | collective-permute-done | bytes 327712 | tf_op jit(solution)/shard_map/ppermute | solution.py:28
  231.9 3.5 collective-permute-done.9
  246.9 3.1 fusion.143
  250.1 3.3 fusion.3
  259.6 4.7 collective-permute-done.10
  266.0 6.1 %collective-permute-done.11 = bf16[128,10,64]{0,2,1:T(8,128)(2,1)S(1)} collective-permute-done((bf16[128,10,64]{0,2,1:T(8,128)(2,1)S(1)}, bf16[128,10,64]{0,2,1:T(8,128)(2,1)S(1)}, u32[]{:S(2)}, u32[]{:S(2)}) %collective-permute-start.11) | collective-permute-done | bytes 163872 | tf_op jit(solution)/shard_map/ppermute | solution.py:28
  283.5 3.1 fusion.144
  286.6 3.2 fusion
  293.3 4.8 %convolution_convert_fusion.2.refs_1_ = bf16[1024,2560]{1,0:T(8,128)(2,1)} fusion(bf16[128,2560]{1,0:T(8,128)(2,1)S(1)} %copy-done.55, bf16[128,2560]{1,0:T(8,128)(2,1)S(1)} %copy-done.51, bf16[128,2560]{1,0:T(8,128)(2,1)S(1)} %copy-done.47, bf16[128,1024]{0,1:T(8,128)(2,1)S(1)} %copy-done.21, bf16[128,1024]{0,1:T(8,128)(2,1)S(1)} %copy-done.23, ...), kind=kOutput, calls=%fused_computation.2 | convolution fusion | flops 2024144896 | bytes 7995392 | tf_op jit(solution)/shard_map/dot_general | solution.py:44
  298.3 4.7 convolution_convert_fusion.refs_3_
  305.7 4.7 convolution_convert_fusion.1.refs_2_
  314.0 4.5 collective-permute-done.13
  320.6 3.9 convolution_convert_fusion.3
  324.5 2.8 pad_maximum_fusion.refs_0_
  328.0 131.7 %reduce_gradients.1 = (f32[32,2688]{1,0:T(8,128)}, f32[32,2560]{1,0:T(8,128)}, f32[32,2560]{1,0:T(8,128)}, f32[80,1024]{1,0:T(8,128)}, f32[8,1024]{1,0:T(8,128)}) custom-call(bf16[1024,2688]{1,0:T(8,128)(2,1)} %pad_maximum_fusion.refs_0_, bf16[1024,2560]{1,0:T(8,128)(2,1)} %convolution_convert_fusion.2.refs_1_, ...), custom_call_target="tpu_custom_call" | custom-call | tf_op jit(solution)/shard_map/reduce_gradients/pallas_call | solution.py:984
  (600 shorter events, 146.3 us)
Async XLA Ops:
  0.6 190.1 %copy-start = (bf16[1,128,960]{1,2,0:T(8,128)(2,1)S(1)}, bf16[1,128,960]{1,2,0:T(8,128)(2,1)}, u32[]{:S(2)}) copy-start(bf16[1,128,960]{1,2,0:T(8,128)(2,1)} %param.17) | copy-start | bytes 737284
  0.7 167.1 %copy-start.128 = (s32[960]{0:T(1024)}, s32[960]{0:T(1024)S(1)}, u32[]{:S(2)}) copy-start(s32[960]{0:T(1024)S(1)} %fusion.252) | copy-start | bytes 11524
  10.3 94.1 %copy-start.157 = (s32[1,3]{1,0:T(1,128)S(1)}, s32[1,3]{1,0:T(1,128)}, u32[]{:S(2)}) copy-start(s32[1,3]{1,0:T(1,128)} %param.16) | copy-start | bytes 40
  10.3 99.0 %copy-start.154 = (s32[1,128]{1,0:T(1,128)S(1)}, s32[1,128]{1,0:T(1,128)}, u32[]{:S(2)}) copy-start(s32[1,128]{1,0:T(1,128)} %param.15) | copy-start | bytes 1540
  11.6 103.8 %copy-start.155 = (f32[3,960]{1,0:T(4,128)S(1)}, f32[3,960]{1,0:T(4,128)}, u32[]{:S(2)}) copy-start(f32[3,960]{1,0:T(4,128)} %param.27) | copy-start | bytes 34564
  11.8 104.9 %copy-start.77 = (bf16[128,1024]{0,1:T(8,128)(2,1)}, bf16[128,1024]{0,1:T(8,128)(2,1)S(1)}, u32[]{:S(2)}) copy-start(bf16[128,1024]{0,1:T(8,128)(2,1)S(1)} %multiply_convert_fusion.14) | copy-start | bytes 786436
  103.5 14.9 %copy-start.156 = (f32[960]{0:T(1024)S(1)}, f32[960]{0:T(1024)}, u32[]{:S(2)}) copy-start(f32[960]{0:T(1024)} %param.26) | copy-start | bytes 11524
  106.2 17.6 %collective-permute-start = (bf16[128,10,64]{0,2,1:T(8,128)(2,1)S(1)}, bf16[128,10,64]{0,2,1:T(8,128)(2,1)S(1)}, u32[]{:S(2)}, u32[]{:S(2)}) collective-permute-start(bf16[128,10,64]{0,2,1:T(8,128)(2,1)S(1)} %pad_maximum_fusion.13), channel_id=1, source_target_pairs={{0,4},{4,8},{8,12},{12,16},{16,20},{20,24},{24,28},{1,5},{5,9},{9,... | collective-permute-start | bytes 491528 | tf_op jit(solution)/shard_map/ppermute | solution.py:28
  109.4 10.4 %collective-permute-start.2 = (bf16[128]{0:T(256)(128)(2,1)S(1)}, bf16[128]{0:T(256)(128)(2,1)S(1)}, u32[]{:S(2)}, u32[]{:S(2)}) collective-permute-start(bf16[128]{0:T(256)(128)(2,1)S(1)} %get-tuple-element.106), channel_id=1, source_target_pairs={{0,4},{4,8},{8,12},{12,16},{16,20},{20,24},{24,28},{1,5},{5,9},{9,... | collective-permute-start | bytes 776 | tf_op jit(solution)/shard_map/ppermute | solution.py:28
  115.3 60.3 %copy-start.107 = (f32[3,128]{1,0:T(4,128)}, f32[3,128]{1,0:T(4,128)S(1)}, u32[]{:S(2)}) copy-start(f32[3,128]{1,0:T(4,128)S(1)} %fusion.261) | copy-start | bytes 4612
  118.3 25.9 %copy-start.124 = (f32[128]{0:T(128)}, f32[128]{0:T(128)S(1)}, u32[]{:S(2)}) copy-start(f32[128]{0:T(128)S(1)} %get-tuple-element.115) | copy-start | bytes 1540
  118.4 15.7 %copy-start.57 = (bf16[128,15,32]{0,2,1:T(8,128)(2,1)}, bf16[128,15,32]{0,2,1:T(8,128)(2,1)S(1)}, u32[]{:S(2)}) copy-start(bf16[128,15,32]{0,2,1:T(8,128)(2,1)S(1)} %get-tuple-element.78) | copy-start | bytes 368644
  119.8 4.0 collective-permute-start.3
  123.9 8.8 %collective-permute-start.1 = (bf16[256,10,64]{0,2,1:T(8,128)(2,1)S(1)}, bf16[256,10,64]{0,2,1:T(8,128)(2,1)S(1)}, u32[]{:S(2)}, u32[]{:S(2)}) collective-permute-start(bf16[256,10,64]{0,2,1:T(8,128)(2,1)S(1)} %maximum_maximum_fusion.3), channel_id=1, source_target_pairs={{0,8},{4,12},{8,16},{12,20},{16,24},{20,28},{1,9},{5,13},{9,17},{1... | collective-permute-start | bytes 983048 | tf_op jit(solution)/shard_map/ppermute | solution.py:28
  149.8 5.4 %collective-permute-start.4 = (bf16[128,10,64]{0,2,1:T(8,128)(2,1)S(1)}, bf16[128,10,64]{0,2,1:T(8,128)(2,1)S(1)}, u32[]{:S(2)}, u32[]{:S(2)}) collective-permute-start(bf16[128,10,64]{0,2,1:T(8,128)(2,1)S(1)} %pad_maximum_fusion.14), channel_id=1, source_target_pairs={{0,4},{4,8},{8,12},{12,16},{16,20},{20,24},{24,28},{1,5},{5,9},{9,... | collective-permute-start | bytes 491528 | tf_op jit(solution)/shard_map/ppermute | solution.py:28
  155.3 9.7 %collective-permute-start.5 = (bf16[256,10,64]{0,2,1:T(8,128)(2,1)S(1)}, bf16[256,10,64]{0,2,1:T(8,128)(2,1)S(1)}, u32[]{:S(2)}, u32[]{:S(2)}) collective-permute-start(bf16[256,10,64]{0,2,1:T(8,128)(2,1)S(1)} %maximum_maximum_fusion.4), channel_id=1, source_target_pairs={{0,8},{4,12},{8,16},{12,20},{16,24},{20,28},{1,9},{5,13},{9,17},{1... | collective-permute-start | bytes 983048 | tf_op jit(solution)/shard_map/ppermute | solution.py:28
  176.6 30.7 %copy-start.145 = (f32[128]{0:T(128)}, f32[128]{0:T(128)S(1)}, u32[]{:S(2)}) copy-start(f32[128]{0:T(128)S(1)} %get-tuple-element.128) | copy-start | bytes 1540
  179.1 4.5 collective-permute-start.6
  183.6 10.3 %collective-permute-start.7 = (bf16[256,10,64]{0,2,1:T(8,128)(2,1)S(1)}, bf16[256,10,64]{0,2,1:T(8,128)(2,1)S(1)}, u32[]{:S(2)}, u32[]{:S(2)}) collective-permute-start(bf16[256,10,64]{0,2,1:T(8,128)(2,1)S(1)} %maximum_maximum_fusion.5), channel_id=1, source_target_pairs={{0,8},{4,12},{8,16},{12,20},{16,24},{20,28},{1,9},{5,13},{9,17},{1... | collective-permute-start | bytes 983048 | tf_op jit(solution)/shard_map/ppermute | solution.py:28
  192.2 15.1 %copy-start.38 = (f32[128,1024]{0,1:T(8,128)}, f32[128,1024]{0,1:T(8,128)S(1)}, u32[]{:S(2)}) copy-start(f32[128,1024]{0,1:T(8,128)S(1)} %get-tuple-element.131) | copy-start | bytes 1572868
  219.2 16.3 %slice-start.20 = ((s8[5505024]{0:T(1024)(128)(4,1)}), s8[4194304]{0:T(1024)(128)(4,1)S(1)}, s32[]{:S(2)}) async-start(s8[5505024]{0:T(1024)(128)(4,1)} %bitcast.395), calls=%async_computation.20 | async-start | bytes 8388608
  220.5 8.4 %collective-permute-start.8 = (bf16[256,10,64]{0,2,1:T(8,128)(2,1)S(1)}, bf16[256,10,64]{0,2,1:T(8,128)(2,1)S(1)}, u32[]{:S(2)}, u32[]{:S(2)}) collective-permute-start(bf16[256,10,64]{0,2,1:T(8,128)(2,1)S(1)} %fusion.203), channel_id=1, source_target_pairs={{8,0},{12,4},{16,8},{20,12},{24,16},{28,20},{9,1},{13,5},{17,9},{2... | collective-permute-start | bytes 983048 | tf_op jit(solution)/shard_map/ppermute | solution.py:28
  222.8 14.7 %copy-start.91 = (bf16[128,15,64]{0,2,1:T(8,128)(2,1)}, bf16[128,15,64]{0,2,1:T(8,128)(2,1)S(1)}, u32[]{:S(2)}) copy-start(bf16[128,15,64]{0,2,1:T(8,128)(2,1)S(1)} %pad_maximum_fusion.10) | copy-start | bytes 737284
  229.0 6.4 %collective-permute-start.9 = (bf16[128,10,64]{0,2,1:T(8,128)(2,1)S(1)}, bf16[128,10,64]{0,2,1:T(8,128)(2,1)S(1)}, u32[]{:S(2)}, u32[]{:S(2)}) collective-permute-start(bf16[128,10,64]{0,2,1:T(8,128)(2,1)S(1)} %slice.522), channel_id=1, source_target_pairs={{4,0},{8,4},{12,8},{16,12},{20,16},{24,20},{28,24},{5,1},{9,5},{13... | collective-permute-start | bytes 491528 | tf_op jit(solution)/shard_map/ppermute | solution.py:28
  255.2 17.1 %slice-start.22 = ((s8[5505024]{0:T(1024)(128)(4,1)}), s8[4194304]{0:T(1024)(128)(4,1)S(1)}, s32[]{:S(2)}) async-start(s8[5505024]{0:T(1024)(128)(4,1)} %bitcast.397), calls=%async_computation.22 | async-start | bytes 8388608
  256.0 8.3 %collective-permute-start.10 = (bf16[256,10,64]{0,2,1:T(8,128)(2,1)S(1)}, bf16[256,10,64]{0,2,1:T(8,128)(2,1)S(1)}, u32[]{:S(2)}, u32[]{:S(2)}) collective-permute-start(bf16[256,10,64]{0,2,1:T(8,128)(2,1)S(1)} %fusion.202), channel_id=1, source_target_pairs={{8,0},{12,4},{16,8},{20,12},{24,16},{28,20},{9,1},{13,5},{17,9},{2... | collective-permute-start | bytes 983048 | tf_op jit(solution)/shard_map/ppermute | solution.py:28
  264.5 7.7 %collective-permute-start.11 = (bf16[128,10,64]{0,2,1:T(8,128)(2,1)S(1)}, bf16[128,10,64]{0,2,1:T(8,128)(2,1)S(1)}, u32[]{:S(2)}, u32[]{:S(2)}) collective-permute-start(bf16[128,10,64]{0,2,1:T(8,128)(2,1)S(1)} %slice.521), channel_id=1, source_target_pairs={{4,0},{8,4},{12,8},{16,12},{20,16},{24,20},{28,24},{5,1},{9,5},{13... | collective-permute-start | bytes 491528 | tf_op jit(solution)/shard_map/ppermute | solution.py:28
  303.0 7.8 %collective-permute-start.12 = (bf16[256,10,64]{0,2,1:T(8,128)(2,1)S(1)}, bf16[256,10,64]{0,2,1:T(8,128)(2,1)S(1)}, u32[]{:S(2)}, u32[]{:S(2)}) collective-permute-start(bf16[256,10,64]{0,2,1:T(8,128)(2,1)S(1)} %fusion.201), channel_id=1, source_target_pairs={{8,0},{12,4},{16,8},{20,12},{24,16},{28,20},{9,1},{13,5},{17,9},{2... | collective-permute-start | bytes 983048 | tf_op jit(solution)/shard_map/ppermute | solution.py:28
  311.0 7.4 %collective-permute-start.13 = (bf16[128,10,64]{0,2,1:T(8,128)(2,1)S(1)}, bf16[128,10,64]{0,2,1:T(8,128)(2,1)S(1)}, u32[]{:S(2)}, u32[]{:S(2)}) collective-permute-start(bf16[128,10,64]{0,2,1:T(8,128)(2,1)S(1)} %slice.520), channel_id=1, source_target_pairs={{4,0},{8,4},{12,8},{16,12},{20,16},{24,20},{28,24},{5,1},{9,5},{13... | collective-permute-start | bytes 491528 | tf_op jit(solution)/shard_map/ppermute | solution.py:28
  328.0 135.5 %copy-start.110 = (f32[1,1024]{1,0:T(1,128)S(1)}, f32[1,1024]{1,0:T(1,128)}, u32[]{:S(2)}) copy-start(f32[1,1024]{1,0:T(1,128)} %get-tuple-element.95) | copy-start | bytes 12292
  328.0 135.5 %copy-start.120 = (f32[128]{0:T(128)S(1)}, f32[128]{0:T(128)}, u32[]{:S(2)}) copy-start(f32[128]{0:T(128)} %copy-done.118) | copy-start | bytes 1540
  328.0 135.5 %copy-start.151 = (f32[128]{0:T(128)S(1)}, f32[128]{0:T(128)}, u32[]{:S(2)}) copy-start(f32[128]{0:T(128)} %copy-done.150) | copy-start | bytes 1540
  (168 other events, 742.2 us)

commit v2 on v1

--- a/solution.py
+++ b/solution.py
@@ -1,5 +1,6 @@
 import jax
 import jax.numpy as jnp
+import numpy as np
 from jax import lax
 from jax.experimental import pallas as pl
 from jax.experimental.pallas import tpu as pltpu
@@ -423,7 +424,7 @@
 
 MESH = pl.DeviceIdType.MESH
 N_Z = 4
-BLOCKS = ((32, 2688), (32, 2560), (32, 2560), (80, 1024))
+BLOCKS = ((32, 2816), (32, 2560), (32, 2560), (80, 1024))
 GATHER_ORDERS = ("uzw", "zuw", "uzw", "zuw")
 REDUCE_ORDERS = ("zuw", "uzw", "zuw", "uzw")
 
@@ -996,6 +997,558 @@
     )(*partials, small)
 
 
+Q_TILES = 9
+O_AT, KV_AT, KV_WIDTH = 1792, 1152, 640
+CHUNK = 512
+
+
+def dot_nn(left, right):
+    return jnp.dot(left, right, preferred_element_type=jnp.float32)
+
+
+def dot_nt(left, right):
+    return lax.dot_general(
+        left, right, (((1,), (1,)), ((), ())), preferred_element_type=jnp.float32
+    )
+
+
+def span_of_device():
+    seq = lax.axis_index("seq")
+    rep = lax.axis_index("rep")
+    z, x, y, core = seq // 2, seq % 2, rep // 2, rep % 2
+    return z, (2 * x + y + x * (1 - 2 * y)) * 2 + core
+
+
+def device_of_span(group, span):
+    chip = span // 2
+    x, y = chip // 2, (chip + 1) // 2 % 2
+    return (group * 2 + x, y * 2 + span % 2)
+
+
+def lanes(shape):
+    return lax.broadcasted_iota(jnp.int32, shape, 1)
+
+
+def rotated(value, cosine, sine):
+    first = lanes(value.shape) % 64 < 32
+    partner = jnp.where(first, pltpu.roll(value, 96, 1), pltpu.roll(value, 32, 1))
+    return value * cosine + partner * sine
+
+
+def block_kernel(*refs):
+    (tokens, cotangent, meta, rope, turn, gains, places, wa_in, wg_in, wu_in, wd_in) = refs[:11]
+    (output, input_grad, small, a_all, gqkv_all, o_all, gt_all, b_all, gg_all, gu_all, hidden_all, gf_all) = refs[11:23]
+    (
+        wa, wg, wu, wd, spread, o_spread, h_all, z_all, tf_all, gate_all, up_all, q_all, window,
+        got, sending, depth_win, depth_at, bias_at, cos_at, sin_at, stats, o_at, dkv, grad, acc, gg_at, gu_at,
+        load_sem, out_sem, kv_send, kv_recv, back_send, back_recv, depth_send, depth_recv,
+    ) = refs[23:]
+    narrow, wide = jnp.bfloat16, jnp.float32
+    group, span = span_of_device()
+
+    barrier = pltpu.get_barrier_semaphore()
+    for away in (1, 2, 3):
+
+        @pl.when(span + away < 8)
+        def _():
+            pl.semaphore_signal(
+                barrier, inc=1, device_id=device_of_span(group, span + away), device_id_type=MESH
+            )
+
+        @pl.when(span - away >= 0)
+        def _():
+            pl.semaphore_signal(
+                barrier, inc=1, device_id=device_of_span(group, span - away), device_id_type=MESH
+            )
+
+    loads = [
+        pltpu.make_async_copy(src, dst, load_sem.at[i])
+        for i, (src, dst) in enumerate(((wa_in, wa), (wg_in, wg), (wu_in, wu), (wd_in, wd)))
+    ]
+    for load in loads:
+        load.start()
+
+    depth_win[3] = jnp.broadcast_to(meta[0:1, :], (8, 128))
+    for away in (1, 2, 3):
+
+        @pl.when(span - away < 0)
+        def _():
+            depth_win[3 - away] = jnp.zeros((8, 128), wide)
+            for recursion in range(RECUR):
+                window[recursion, 3 - away] = jnp.zeros((128, KV_WIDTH), narrow)
+
+    pl.semaphore_wait(barrier, 3 + span + span // 4 * (7 - 2 * span))
+
+    def depth_copy(away, device):
+        return remote(
+            depth_win.at[3],
+            depth_win.at[3 - away],
+            depth_send.at[away - 1],
+            depth_recv.at[away - 1],
+            device,
+        )
+
+    def kv_copy(recursion, away, device):
+        return remote(
+            window.at[recursion, 3],
+            window.at[recursion, 3 - away],
+            kv_send.at[recursion, away - 1],
+            kv_recv.at[recursion, away - 1],
+            device,
+        )
+
+    def back_copy(recursion, away, device):
+        return remote(
+            sending.at[away - 1],
+            got.at[recursion, away - 1],
+            back_send.at[recursion, away - 1],
+            back_recv.at[recursion, away - 1],
+            device,
+        )
+
+    def stage_copies(recursion):
+        return [
+            pltpu.make_async_copy(gg_at, gg_all.at[recursion], out_sem.at[0]),
+            pltpu.make_async_copy(gu_at, gu_all.at[recursion], out_sem.at[1]),
+        ]
+
+    def to_later(copy):
+        for away in (1, 2, 3):
+
+            @pl.when(span + away < 8)
+            def _():
+                copy(away, device_of_span(group, span + away)).start()
+
+    def to_earlier(copy):
+        for away in (1, 2, 3):
+
+            @pl.when(span - away >= 0)
+            def _():
+                copy(away, device_of_span(group, span - away)).start()
+
+    def wait_each(valid, waiting):
+        for away in (1, 2, 3):
+
+            @pl.when(valid(away))
+            def _():
+                waiting(away)
+
+    def has_later(away):
+        return span + away < 8
+
+    def has_earlier(away):
+        return span - away >= 0
+
+    here = device_of_span(group, span)
+    to_later(depth_copy)
+
+    @pl.loop(0, MODEL_WIDTH // 64)
+    def _(i):
+        at = pl.multiple_of(i * 64, 64)
+        rows = lax.broadcasted_iota(jnp.int32, (64, 1024), 0) + at
+        spread[pl.ds(at, 64), :] = jnp.where(rows == places[0:1, :], 1.0, 0.0).astype(narrow)
+
+    for tile in range(Q_TILES):
+        at = lax.broadcasted_iota(jnp.int32, (128, 1024), 0)
+        pair, part = tile // 3, tile % 3
+        low, high = (6 * pair + part) * 64, (6 * pair + 3 + part) * 64 - 64
+        if pair == 2:
+            target = jnp.where(at < 64, -2, at + (12 + part) * 64 - 64)
+        else:
+            target = jnp.where(at < 64, at + low, at + high)
+        o_spread[pl.ds(tile * 128, 128), :] = jnp.where(
+            target == places[0:1, :], 1.0, 0.0
+        ).astype(narrow)
+
+    span_lane = meta[1:2, :]
+    turn_cos = jnp.zeros((1, 128), wide)
+    turn_sin = jnp.zeros((1, 128), wide)
+    for k in range(4):
+        turn_cos = turn_cos + jnp.where(span_lane == k, turn[k : k + 1, :], 0.0)
+        turn_sin = turn_sin + jnp.where(span_lane == k, turn[8 + k : 9 + k, :], 0.0)
+    cos_at[...] = turn_cos * rope[0] - turn_sin * rope[1]
+    sign = jnp.where(lanes((128, 128)) % 64 < 32, -1.0, 1.0)
+    sin_at[...] = sign * (turn_sin * rope[0] + turn_cos * rope[1])
+
+    h_all[0] = dot_nn(tokens[...], spread[...])
+    grad[...] = dot_nn(cotangent[...], spread[...])
+    small[...] = jnp.zeros((8, 1024), wide)
+
+    wait_each(has_earlier, lambda away: depth_copy(away, here).wait_recv())
+    row = lax.broadcasted_iota(jnp.int32, (128, 128), 0)
+    column = lanes((128, 128))
+    ones = jnp.ones((128, 128), wide)
+    for block in range(4):
+        held = depth_win[block]
+        depth_at[pl.ds(block * 128, 128), :] = dot_nn(
+            jnp.where(row == column, jnp.broadcast_to(held[0:1, :], (128, 128)), 0.0), ones
+        ).astype(narrow)
+
+    def set_bias(recursion):
+        level = recursion.astype(wide)
+        for block in range(4):
+            active = depth_at[pl.ds(block * 128, 128), :].astype(wide) > level
+            if block == 3:
+                allowed = (row == column) | (active & (row <= column))
+            else:
+                allowed = active & (span_lane >= 3 - block)
+            bias_at[pl.ds(block * 128, 128), :] = jnp.where(allowed, 0.0, masked_score)
+
+    def inverse_rms(value):
+        return lax.rsqrt(
+            jnp.sum(value * value, axis=-1, keepdims=True) / MODEL_WIDTH + epsilon
+        )
+
+    def active_column(recursion):
+        own = depth_at[384:512, :].astype(wide)[:, 0:1]
+        return jnp.where(own > recursion.astype(wide), 1.0, 0.0)
+
+    def mixing_gate(recursion):
+        logits = jnp.sum(
+            h_all[recursion] * gains[pl.ds(2 + recursion, 1), :], axis=-1, keepdims=True
+        )
+        return jax.nn.sigmoid(logits)
+
+    def halves(tile, pair, key_side):
+        low = lanes(tile.shape) < 64
+        zero = jnp.zeros_like(tile)
+        if pair == 2:
+            return jnp.where(low, tile, zero) if key_side else jnp.where(low, zero, tile)
+        return jnp.concatenate([jnp.where(low, tile, zero), jnp.where(low, zero, tile)], axis=0)
+
+    def key_tile(recursion, pair):
+        parts = [window[recursion, b, :, pair * 128 : pair * 128 + 128] for b in range(4)]
+        return jnp.concatenate(parts, axis=0)
+
+    def value_tile(recursion, pair):
+        at = 256 if pair == 2 else 384 + pair * 128
+        parts = [window[recursion, b, :, at : at + 128] for b in range(4)]
+        return jnp.concatenate(parts, axis=0)
+
+    def biased(scores):
+        bias = bias_at[...]
+        if scores.shape[1] == 128:
+            return scores + bias
+        return scores + jnp.concatenate([bias, bias], axis=1)
+
+    def joined(out, pair, key_side):
+        if pair == 2:
+            if key_side:
+                out = jnp.where(row < 64, out, 0.0)
+            return out.T
+        return jnp.where(row < 64, out[:, :128], out[:, 128:]).T
+
+    def attend(recursion):
+        for pair in range(3):
+            keys, values_t = key_tile(recursion, pair), value_tile(recursion, pair).T
+
+            @pl.loop(0, 3)
+            def _(part):
+                at = pl.multiple_of((pair * 3 + part) * 128, 128)
+                queries = halves(q_all[recursion, :, pl.ds(at, 128)], pair, True)
+                scores = biased(dot_nt(keys, queries))
+                top = jnp.max(scores, axis=0, keepdims=True)
+                weight = jnp.exp(scores - top)
+                inverse = 1.0 / jnp.sum(weight, axis=0, keepdims=True)
+                width = scores.shape[1]
+                stats[recursion, pair * 3 + part, 0:1, 0:width] = top
+                stats[recursion, pair * 3 + part, 1:2, 0:width] = inverse
+                out = dot_nn(values_t, (weight * inverse).astype(narrow))
+                o_at[:, pl.ds(at, 128)] = joined(out, pair, False).astype(narrow)
+
+    def attend_back(recursion):
+        for pair in range(3):
+            keys, values = key_tile(recursion, pair), value_tile(recursion, pair)
+            keys_t = keys.T
+            value_at = 256 if pair == 2 else 384 + pair * 128
+            dkv[:, pair * 128 : pair * 128 + 128] = jnp.zeros((512, 128), wide)
+            if pair < 2:
+                dkv[:, value_at : value_at + 128] = jnp.zeros((512, 128), wide)
+
+            @pl.loop(0, 3)
+            def _(part):
+                at = pl.multiple_of((pair * 3 + part) * 128, 128)
+                queries = halves(q_all[recursion, :, pl.ds(at, 128)], pair, True)
+                upstream = halves(o_at[:, pl.ds(at, 128)], pair, False)
+                scores = biased(dot_nt(keys, queries))
+                width = scores.shape[1]
+                top = stats[recursion, pair * 3 + part, 0:1, 0:width]
+                inverse = stats[recursion, pair * 3 + part, 1:2, 0:width]
+                probs = jnp.exp(scores - top) * inverse
+                grad_probs = dot_nt(values, upstream)
+                inner = jnp.sum(probs * grad_probs, axis=0, keepdims=True)
+                grad_scores = (probs * (grad_probs - inner)).astype(narrow)
+                dkv[:, pair * 128 : pair * 128 + 128] += dot_nn(grad_scores, queries)
+                dkv[:, value_at : value_at + 128] += dot_nn(probs.astype(narrow), upstream)
+                out = dot_nn(keys_t, grad_scores)
+                gqkv_all[recursion, :, pl.ds(at, 128)] = rotated(
+                    joined(out, pair, True), cos_at[...] * 0.125, sin_at[...] * -0.125
+                ).astype(narrow)
+
+    def rotate_keys(value, sine):
+        cosine = cos_at[...]
+        low = lanes((128, 128)) < 64
+        parts = []
+        for tile in range(5):
+            part = value[:, tile * 128 : tile * 128 + 128]
+            if tile < 2:
+                part = rotated(part, cosine, sine)
+            elif tile == 2:
+                part = jnp.where(low, rotated(part, cosine, sine), part)
+            parts.append(part)
+        return jnp.concatenate(parts, axis=1)
+
+    @pl.loop(0, RECUR)
+    def _(recursion):
+        state = h_all[recursion]
+        normal = state * inverse_rms(state)
+        a_b = (normal * gains[0:1, :]).astype(narrow)
+        a_all[recursion] = a_b
+
+        @pl.when(recursion == 0)
+        def _():
+            loads[0].wait()
+
+        pair_values = dot_nn(a_b, wa[:, KV_AT:O_AT])
+        window[recursion, 3] = rotate_keys(pair_values, sin_at[...]).astype(narrow)
+        to_later(lambda away, device: kv_copy(recursion, away, device))
+        cosine, sine = cos_at[...] * 0.125, sin_at[...] * 0.125
+        for first, width in ((0, 512), (512, 512), (1024, 128)):
+            queries = dot_nn(a_all[recursion], wa[:, first : first + width])
+            for at in range(0, width, 128):
+                q_all[recursion, :, first + at : first + at + 128] = rotated(
+                    queries[:, at : at + 128], cosine, sine
+                ).astype(narrow)
+        set_bias(recursion)
+        wait_each(has_earlier, lambda away: kv_copy(recursion, away, here).wait_recv())
+        attend(recursion)
+        o_pad = dot_nn(o_at[...], o_spread[...]).astype(narrow)
+        o_all[recursion] = o_pad
+        branch = dot_nn(o_pad, wa[:, O_AT:])
+        middle = h_all[recursion] + branch
+        z_all[recursion] = middle
+        b_b = (middle * inverse_rms(middle) * gains[1:2, :]).astype(narrow)
+        b_all[recursion] = b_b
+        acc[...] = branch
+
+        @pl.when(recursion == 0)
+        def _():
+            for load in loads[1:]:
+                load.wait()
+
+        @pl.loop(0, FEEDFORWARD_UNITS // CHUNK)
+        def _(j):
+            at = pl.ds(pl.multiple_of(j * CHUNK, CHUNK), CHUNK)
+            gate = dot_nn(b_all[recursion], wg[:, at])
+            up = dot_nn(b_all[recursion], wu[:, at])
+            gate_all[recursion, :, at] = gate
+            up_all[recursion, :, at] = up
+            hidden = (gate * jax.nn.sigmoid(gate) * up).astype(narrow)
+            hidden_all[recursion, :, at] = hidden
+            acc[...] += dot_nn(hidden, wd[at, :])
+
+        tf_all[recursion] = acc[...]
+        mixing = active_column(recursion) * mixing_gate(recursion)
+        following = h_all[recursion] + mixing * acc[...]
+
+        @pl.when(recursion < RECUR - 1)
+        def _():
+            h_all[recursion + 1] = following
+
+        @pl.when(recursion == RECUR - 1)
+        def _():
+            output[...] = dot_nt(following.astype(narrow), spread[...]).astype(narrow)
+
+    @pl.loop(0, RECUR)
+    def _(i):
+        recursion = RECUR - 1 - i
+        router_row = gains[pl.ds(2 + recursion, 1), :]
+        active, gate_value = active_column(recursion), mixing_gate(recursion)
+        upstream = grad[...]
+        grad_mix = jnp.sum(upstream * tf_all[recursion], axis=-1, keepdims=True)
+        grad_logit = active * grad_mix * gate_value * (1.0 - gate_value)
+        small[pl.ds(2 + recursion, 1), :] = jnp.sum(
+            grad_logit * h_all[recursion], axis=0, keepdims=True
+        )
+        delta = (active * gate_value) * upstream
+        gf_all[recursion] = delta.astype(narrow)
+        grad[...] = upstream + grad_logit * router_row
+        tf_all[recursion] = delta
+        acc[...] = jnp.zeros((128, 1024), wide)
+
+        @pl.when(recursion < RECUR - 1)
+        def _():
+            for copy in stage_copies(recursion + 1):
+                copy.wait()
+
+        @pl.loop(0, FEEDFORWARD_UNITS // CHUNK)
+        def _(j):
+            at = pl.ds(pl.multiple_of(j * CHUNK, CHUNK), CHUNK)
+            grad_hidden = dot_nt(gf_all[recursion], wd[at, :])
+            gate, up = gate_all[recursion, :, at], up_all[recursion, :, at]
+            sigmoid = jax.nn.sigmoid(gate)
+            grad_gate = (grad_hidden * up * sigmoid * (1.0 + gate * (1.0 - sigmoid))).astype(narrow)
+            grad_up = (grad_hidden * gate * sigmoid).astype(narrow)
+            gg_at[:, at] = grad_gate
+            gu_at[:, at] = grad_up
+            acc[...] += dot_nt(grad_gate, wg[:, at]) + dot_nt(grad_up, wu[:, at])
+
+        for copy in stage_copies(recursion):
+            copy.start()
+        middle = z_all[recursion]
+        inverse = inverse_rms(middle)
+        normal = middle * inverse
+        small[1:2, :] += jnp.sum(acc[...] * normal, axis=0, keepdims=True)
+        scaled = acc[...] * gains[1:2, :]
+        inner = jnp.sum(scaled * normal, axis=-1, keepdims=True) / MODEL_WIDTH
+        grad_middle = inverse * (scaled - normal * inner)
+        gt_b = (tf_all[recursion] + grad_middle).astype(narrow)
+        gt_all[recursion] = gt_b
+        grad[...] += grad_middle
+        go_pad = dot_nt(gt_b, wa[:, O_AT:]).astype(narrow)
+        o_at[...] = dot_nt(go_pad, o_spread[...]).astype(narrow)
+        set_bias(recursion)
+        attend_back(recursion)
+
+        @pl.when(recursion < RECUR - 1)
+        def _():
+            wait_each(has_earlier, lambda away: back_copy(recursion + 1, away, here).wait_send())
+
+        for away in (1, 2, 3):
+            sending[away - 1] = dkv[
+                (3 - away) * 128 : (4 - away) * 128, :
+            ].astype(narrow)
+        to_earlier(lambda away, device: back_copy(recursion, away, device))
+        acc[...] = dot_nt(gqkv_all[recursion, :, :KV_AT], wa[:, :KV_AT])
+
+        @pl.loop(1, 4)
+        def _(away):
+            @pl.when(span + away < 8)
+            def _():
+                back_copy(recursion, away, here).wait_recv()
+                dkv[384:512, :] += got[recursion, away - 1].astype(wide)
+
+        gqkv_all[recursion, :, KV_AT:] = rotate_keys(dkv[384:512, :], -sin_at[...]).astype(narrow)
+        grad_normed = acc[...] + dot_nt(gqkv_all[recursion, :, KV_AT:], wa[:, KV_AT:O_AT])
+        state = h_all[recursion]
+        inverse = inverse_rms(state)
+        normal = state * inverse
+        small[0:1, :] += jnp.sum(grad_normed * normal, axis=0, keepdims=True)
+        scaled = grad_normed * gains[0:1, :]
+        inner = jnp.sum(scaled * normal, axis=-1, keepdims=True) / MODEL_WIDTH
+        grad[...] += inverse * (scaled - normal * inner)
+
+    for copy in stage_copies(0):
+        copy.wait()
+    total = grad[...]
+    first = total.astype(narrow)
+    rest = total - first.astype(wide)
+    second = rest.astype(narrow)
+    third = (rest - second.astype(wide)).astype(narrow)
+    input_grad[...] = (
+        dot_nt(first, spread[...]) + dot_nt(second, spread[...]) + dot_nt(third, spread[...])
+    )
+
+    wait_each(has_later, lambda away: depth_copy(away, here).wait_send())
+    for recursion in range(RECUR):
+        wait_each(has_later, lambda away: kv_copy(recursion, away, here).wait_send())
+    wait_each(has_earlier, lambda away: back_copy(0, away, here).wait_send())
+
+
+def run_block(tokens, cotangent, meta, gains, weights):
+    narrow, wide, vmem, sems = jnp.bfloat16, jnp.float32, pltpu.VMEM, pltpu.SemaphoreType.DMA
+    half = HEAD_SIZE // 2
+    lane = np.arange(128) % half
+    frequency = 10000.0 ** (-lane / half)
+    angle = np.arange(128)[:, None] * frequency[None, :]
+    rope = np.stack([np.cos(angle), np.sin(angle)]).astype(np.float32)
+    jump = np.arange(4)[:, None] * 128.0 * frequency[None, :]
+    turn = np.zeros((16, 128), np.float32)
+    turn[:4], turn[8:12] = np.cos(jump), np.sin(jump)
+    padded = np.arange(1024)
+    natural = padded // PADDED_ROWS * OWN_ROWS + padded % PADDED_ROWS
+    natural = np.where(padded % PADDED_ROWS < OWN_ROWS, natural, -1)
+    places = np.broadcast_to(natural[None], (8, 1024)).astype(np.int32)
+    outs = [((128, MODEL_WIDTH), narrow), ((128, MODEL_WIDTH), wide), ((8, 1024), wide)]
+    outs += [
+        ((RECUR, 128, width), narrow)
+        for width in (1024, O_AT, 1024, 1024, 1024, 2560, 2560, 2560, 1024)
+    ]
+    scratch = [
+        vmem((1024, 2816), narrow),
+        vmem((1024, 2560), narrow),
+        vmem((1024, 2560), narrow),
+        vmem((2560, 1024), narrow),
+        vmem((MODEL_WIDTH, 1024), narrow),
+        vmem((KV_AT, 1024), narrow),
+        vmem((RECUR, 128, 1024), wide),
+        vmem((RECUR, 128, 1024), wide),
+        vmem((RECUR, 128, 1024), wide),
+        vmem((RECUR, 128, 2560), wide),
+        vmem((RECUR, 128, 2560), wide),
+        vmem((RECUR, 128, KV_AT), narrow),
+        vmem((RECUR, 4, 128, KV_WIDTH), narrow),
+        vmem((RECUR, 3, 128, KV_WIDTH), narrow),
+        vmem((3, 128, KV_WIDTH), narrow),
+        vmem((4, 8, 128), wide),
+        vmem((512, 128), narrow),
+        vmem((512, 128), wide),
+        vmem((128, 128), wide),
+        vmem((128, 128), wide),
+        vmem((RECUR, Q_TILES, 2, 256), wide),
+        vmem((128, KV_AT), narrow),
+        vmem((512, KV_WIDTH), wide),
+        vmem((128, 1024), wide),
+        vmem((128, 1024), wide),
+        vmem((128, 2560), narrow),
+        vmem((128, 2560), narrow),
+        sems((4,)),
+        sems((2,)),
+        sems((RECUR, 3)),
+        sems((RECUR, 3)),
+        sems((RECUR, 3)),
+        sems((RECUR, 3)),
+        sems((3,)),
+        sems((3,)),
+    ]
+    here = pl.BlockSpec(memory_space=vmem)
+    return pl.pallas_call(
+        block_kernel,
+        out_shape=[jax.ShapeDtypeStruct(shape, dtype) for shape, dtype in outs],
+        in_specs=[here] * 7 + [pl.BlockSpec(memory_space=pl.ANY)] * 4,
+        out_specs=[here] * 8 + [pl.BlockSpec(memory_space=pl.ANY)] * 2 + [here] * 2,
+        scratch_shapes=scratch,
+        compiler_params=pltpu.CompilerParams(
+            collective_id=3, has_side_effects=True, vmem_limit_bytes=59 * 2**20
+        ),
+        name="run_block",
+    )(tokens, cotangent, meta, rope, turn, gains, places, *weights)
+
+
+HEAD_ORDER = (0, 3, 1, 4, 2, 5, 6, 9, 7, 10, 8, 11, 12, -1, 13, -1, 14, -1)
+
+
+def moved(value, back=False):
+    pairs = []
+    for span in range(8):
+        for group in range(4):
+            seq, rep = device_of_span(group, span)
+            pairs.append((span * 4 + group, seq * 4 + rep))
+    if back:
+        pairs = [(there, here) for here, there in pairs]
+    return lax.ppermute(value, ("seq", "rep"), pairs)
+
+
+def span_index(seq_spans):
+    chain = lax.axis_size("seq")
+    lengths = seq_spans[0]
+    seq_ends = jnp.cumsum(lengths)
+    own = lax.axis_index("seq")
+    starts = seq_ends - lengths
+    inside = (starts <= own) & (own < seq_ends)
+    return own - jnp.sum(jnp.where(inside, starts, 0))
+
+
 def per_device_fast(
     tokens,
     depths,
@@ -1013,259 +1566,51 @@
     router,
 ):
     narrow, wide = jnp.bfloat16, jnp.float32
-    count_of_rows = tokens.shape[1]
-    query_groupings = QUERY_HEADS // KEY_VALUE_HEADS
-    chain = lax.axis_size("seq")
-    most_spans = min(2**LOGC, chain // 2)
-    depth_levels = (most_spans - 1).bit_length()
-    extra_rows = ((1 << depth_levels) - most_spans) * count_of_rows
-    window = most_spans * count_of_rows
     natural = jnp.arange(MODEL_WIDTH, dtype=jnp.int32)
     padded_at = (natural // OWN_ROWS) * PADDED_ROWS + natural % OWN_ROWS
     spread = (padded_at[:, None] == jnp.arange(PADDED_WIDTH, dtype=jnp.int32)[None, :]).astype(narrow)
     packed = pack_weights(
         spread, w_query, key_weight, value_weight, w_out, w_gate, w_up, w_down
     )
-    attention_full, gate_full, up_full, down_full = gather_weights(packed)
-    w_q = attention_full[:, :960]
-    w_k = attention_full[:, 960:1280]
-    w_v = attention_full[:, 1280:1600]
-    w_o = attention_full[:, 1664:]
-
-    def spread_vector(v):
-        return jnp.dot(v, spread.astype(wide), precision=highest)
-
-    gain_a, gain_f, routers = spread_vector(attn_gain), spread_vector(ffn_gain), spread_vector(router)
-
-    def rms_parts_padded(vectors, gain):
-        mean = jnp.sum(vectors * vectors, axis=-1, keepdims=True) / MODEL_WIDTH
-        inv_rms = lax.rsqrt(mean + epsilon)
-        normal_part = vectors * inv_rms
-        return (normal_part * gain, normal_part, inv_rms)
-
-    def rms_backward_padded(upstream, normal_part, inv_rms, gain):
-        gain_grad = jnp.sum(upstream * normal_part, axis=0)
-        scaled = upstream * gain
-        inner = jnp.sum(scaled * normal_part, axis=-1, keepdims=True) / MODEL_WIDTH
-        return (inv_rms * (scaled - normal_part * inner), gain_grad)
-
-    place_index = lax.axis_index("seq")
-    lengths = seq_spans[0]
-    seq_ends = jnp.cumsum(lengths)
-    span_ids = jnp.arange(chain, dtype=jnp.int32)
-    owners = jnp.sum((seq_ends[None, :] <= span_ids[:, None]).astype(jnp.int32), axis=1)
-    seq_starts = seq_ends - lengths
-    numbers = jnp.arange(lengths.shape[0], dtype=jnp.int32)
-    first_span = jnp.sum(
-        jnp.where(numbers[None, :] == owners[:, None], seq_starts[None, :], 0), axis=1
-    )
-    index_of_span = jnp.sum(jnp.where(span_ids == place_index, span_ids - first_span, 0))
-    positions = (index_of_span * count_of_rows + jnp.arange(count_of_rows, dtype=jnp.int32)).astype(
-        wide
-    )
-    cosine_table, sine_table = angle_tables(positions, HEAD_SIZE)
-    row_ids = jnp.arange(count_of_rows, dtype=jnp.int32)
-    col_ids = jnp.arange(window, dtype=jnp.int32)
-    offsets = most_spans - 1 - col_ids // count_of_rows
-    local_col = col_ids - (most_spans - 1) * count_of_rows
-    causal = jnp.where(offsets[None, :] == 0, local_col[None, :] <= row_ids[:, None], True)
-    diagonal = (offsets[None, :] == 0) & (local_col[None, :] == row_ids[:, None])
-    span_ok = (index_of_span >= offsets)[None, :]
-    active_all = (depths[0][None, :] > jnp.arange(RECUR, dtype=jnp.int32)[:, None]).astype(wide)
-    depth_win = depths[0].astype(narrow)
-    for level in range(depth_levels):
-        depth_win = jnp.concatenate([passed_along(depth_win, "seq", 1 << level), depth_win], axis=0)
-    hidden_state = unscaled_product(tokens[0], spread)
-    saved = []
-    for recursion in range(RECUR):
-        current_active = active_all[recursion]
-        normalized, normal_a, inv_a = rms_parts_padded(hidden_state, gain_a)
-        a_b = normalized.astype(narrow)
-        raw_query = unscaled_product(a_b, w_q).reshape(count_of_rows, QUERY_HEADS, HEAD_SIZE)
-        query_b = (
-            apply_rotation(raw_query, cosine_table, sine_table)
-            .astype(narrow)
-            .reshape(count_of_rows, KEY_VALUE_HEADS, query_groupings, HEAD_SIZE)
-        )
-        unrotated_key = unscaled_product(a_b, w_k).reshape(
-            count_of_rows, KEY_VALUE_HEADS, HEAD_SIZE
-        )
-        key_b = apply_rotation(unrotated_key, cosine_table, sine_table).astype(narrow)
-        value_b = (
-            unscaled_product(a_b, w_v)
-            .astype(narrow)
-            .reshape(count_of_rows, KEY_VALUE_HEADS, HEAD_SIZE)
-        )
-        pair = jnp.concatenate([key_b, value_b], axis=1)
-        for level in range(depth_levels):
-            pair = jnp.concatenate([passed_along(pair, "seq", 1 << level), pair], axis=0)
-        keys_win, values_win = pair[:, :KEY_VALUE_HEADS], pair[:, KEY_VALUE_HEADS:]
-        allowed = span_ok & causal & ((depth_win > recursion)[None, :] | diagonal)
-        scores = masked_scores(query_b, keys_win, allowed)
-        row_max = jnp.max(scores, axis=-1, keepdims=True)
-        expon = jnp.exp(scores - row_max)
-        row_total = jnp.sum(expon, axis=-1, keepdims=True)
-        probs_b = (expon / row_total).astype(narrow)
-        log_total = row_max + jnp.log(row_total)
-        attended_b = (
-            jnp.einsum("gjqk,kgd->qgjd", probs_b, values_win, preferred_element_type=wide)
-            .astype(narrow)
-            .reshape(count_of_rows, QUERY_HEADS * HEAD_SIZE)
-        )
-        attended_b = unscaled_product(attended_b, spread).astype(narrow)
-        branch = unscaled_product(attended_b, w_o)
-        middle = hidden_state + branch
-        second, normal_z, inv_z = rms_parts_padded(middle, gain_f)
-        second_b = second.astype(narrow)
-        gate_value = unscaled_product(second_b, gate_full)
-        up_value = unscaled_product(second_b, up_full)
-        hidden_b = (jax.nn.silu(gate_value) * up_value).astype(narrow)
-        ffn_out = unscaled_product(hidden_b, down_full)
-        weight_gate = jax.nn.sigmoid(jnp.dot(hidden_state, routers[recursion], precision=highest))
-        saved.append(
-            (
-                hidden_state,
-                a_b,
-                normal_a,
-                inv_a,
-                query_b,
-                keys_win,
-                values_win,
-                allowed,
-                log_total,
-                attended_b,
-                branch,
-                normal_z,
-                inv_z,
-                second_b,
-                gate_value,
-                up_value,
-                hidden_b,
-                ffn_out,
-                weight_gate,
-                current_active,
-            )
-        )
-        hidden_state = hidden_state + (current_active * weight_gate)[:, None] * (branch + ffn_out)
-    output = right_product(hidden_state.astype(narrow), spread).astype(narrow)
-    gain_a_total = jnp.zeros((PADDED_WIDTH,), wide)
-    gain_f_total = jnp.zeros((PADDED_WIDTH,), wide)
-    router_rows = [None] * RECUR
-    factors = []
-    grad_state = unscaled_product(cotangent[0], spread)
-    for recursion in reversed(range(RECUR)):
-        (
-            state_in,
-            a_b,
-            normal_a,
-            inv_a,
-            query_b,
-            keys_win,
-            values_win,
-            allowed,
-            log_total,
-            attended_b,
-            branch,
-            normal_z,
-            inv_z,
-            second_b,
-            gate_value,
-            up_value,
-            hidden_b,
-            ffn_out,
-            weight_gate,
-            current_active,
-        ) = saved[recursion]
-        mixing = current_active * weight_gate
-        grad_delta = mixing[:, None] * grad_state
-        grad_mix = jnp.sum(grad_state * (branch + ffn_out), axis=-1)
-        grad_logit = current_active * grad_mix * weight_gate * (1.0 - weight_gate)
-        router_rows[recursion] = jnp.dot(grad_logit, state_in, precision=highest)
-        grad_next = grad_state + grad_logit[:, None] * routers[recursion][None, :]
-        ffn_grad_b = grad_delta.astype(narrow)
-        grad_hidden = right_product(ffn_grad_b, down_full)
-        sigmoid_gate = jax.nn.sigmoid(gate_value)
-        grad_gate_b = (
-            grad_hidden * up_value * sigmoid_gate * (1.0 + gate_value * (1.0 - sigmoid_gate))
+    weights = gather_weights(packed)
+    gains = jnp.concatenate([attn_gain[None], ffn_gain[None], router], axis=0)
+    gains = jnp.pad(
+        gains.reshape(5, 32, OWN_ROWS), ((0, 3), (0, 0), (0, PADDED_ROWS - OWN_ROWS))
+    ).reshape(8, PADDED_WIDTH)
+    index = span_index(seq_spans)
+    meta = jnp.concatenate(
+        [
+            depths.astype(wide),
+            jnp.broadcast_to(index.astype(wide), (1, 128)),
+            jnp.zeros((6, 128), wide),
+        ],
+        axis=0,
+    )
+    (
+        output,
+        input_grad,
+        small,
+        a_all,
+        qkv_all,
+        o_all,
+        t_all,
+        b_all,
+        gate_all,
+        up_all,
+        hidden_all,
+        f_all,
+    ) = run_block(moved(tokens[0]), moved(cotangent[0]), moved(meta), gains, weights)
+
+    def contracted(left, right):
+        return left_product(
+            left.reshape(RECUR * 128, -1), right.reshape(RECUR * 128, -1)
         ).astype(narrow)
-        grad_up_b = (grad_hidden * gate_value * sigmoid_gate).astype(narrow)
-        grad_second = right_product(grad_gate_b, gate_full) + right_product(grad_up_b, up_full)
-        grad_middle, gain_f_part = rms_backward_padded(grad_second, normal_z, inv_z, gain_f)
-        gain_f_total = gain_f_total + gain_f_part
-        grad_branch_b = (grad_delta + grad_middle).astype(narrow)
-        grad_attended_b = right_product(
-            right_product(grad_branch_b, w_o).astype(narrow), spread
-        ).astype(narrow).reshape(count_of_rows, KEY_VALUE_HEADS, query_groupings, HEAD_SIZE)
-        grad_next = grad_next + grad_middle
-        scores = masked_scores(query_b, keys_win, allowed)
-        probs = jnp.exp(scores - log_total)
-        probs_b = probs.astype(narrow)
-        grad_probs = jnp.einsum(
-            "qgjd,kgd->gjqk", grad_attended_b, values_win, preferred_element_type=wide
-        )
-        row_dot = jnp.sum(probs * grad_probs, axis=-1, keepdims=True)
-        grad_scores_b = (probs * (grad_probs - row_dot)).astype(narrow)
-        grad_queries = (
-            jnp.einsum("gjqk,kgd->qgjd", grad_scores_b, keys_win, preferred_element_type=wide)
-            * 0.125
-        )
-        grad_keys = (
-            jnp.einsum("gjqk,qgjd->kgd", grad_scores_b, query_b, preferred_element_type=wide)
-            * 0.125
-        )
-        grad_values = jnp.einsum(
-            "gjqk,qgjd->kgd", probs_b, grad_attended_b, preferred_element_type=wide
-        )
-        local_pair = jnp.concatenate(
-            [
-                jnp.zeros((extra_rows, 2 * KEY_VALUE_HEADS, HEAD_SIZE), wide),
-                jnp.concatenate([grad_keys, grad_values], axis=1),
-            ],
-            axis=0,
-        )
-        for level in reversed(range(depth_levels)):
-            older_rows = (1 << level) * count_of_rows
-            back = passed_along(for_sending(local_pair[:older_rows]), "seq", -(1 << level))
-            local_pair = local_pair[older_rows:] + back
-        grad_query_b = (
-            apply_rotation(
-                grad_queries.reshape(count_of_rows, QUERY_HEADS, HEAD_SIZE),
-                cosine_table,
-                -sine_table,
-            )
-            .astype(narrow)
-            .reshape(count_of_rows, QUERY_HEADS * HEAD_SIZE)
-        )
-        grad_key_b = (
-            apply_rotation(local_pair[:, :KEY_VALUE_HEADS], cosine_table, -sine_table)
-            .astype(narrow)
-            .reshape(count_of_rows, KEY_VALUE_HEADS * HEAD_SIZE)
-        )
-        grad_value_b = (
-            local_pair[:, KEY_VALUE_HEADS:]
-            .astype(narrow)
-            .reshape(count_of_rows, KEY_VALUE_HEADS * HEAD_SIZE)
-        )
-        grad_qkv_b = jnp.concatenate([grad_query_b, grad_key_b, grad_value_b], axis=1)
-        grad_normed = right_product(grad_qkv_b, attention_full[:, :1600])
-        grad_input, gain_a_part = rms_backward_padded(grad_normed, normal_a, inv_a, gain_a)
-        gain_a_total = gain_a_total + gain_a_part
-        grad_state = grad_next + grad_input
-        factors.append(
-            (a_b, grad_qkv_b, attended_b, grad_branch_b, second_b, grad_gate_b, grad_up_b, hidden_b, ffn_grad_b)
-        )
-    a_all, qkv_all, o_all, t_all, b_all, gate_all, up_all, hidden_all, f_all = (
-        jnp.concatenate(parts, axis=0) for parts in zip(*factors)
-    )
-    d_qkv = left_product(a_all, jnp.pad(qkv_all, ((0, 0), (0, 64))))
+
     partials = (
-        jnp.concatenate([d_qkv, left_product(o_all, t_all)], axis=1).astype(narrow),
-        left_product(b_all, gate_all).astype(narrow),
-        left_product(b_all, up_all).astype(narrow),
-        left_product(hidden_all, f_all).astype(narrow),
-    )
-    small = jnp.concatenate(
-        [jnp.stack([gain_a_total, gain_f_total]), jnp.stack(router_rows), jnp.zeros((3, PADDED_WIDTH), wide)]
+        jnp.concatenate([contracted(a_all, qkv_all), contracted(o_all, t_all)], axis=1),
+        contracted(b_all, gate_all),
+        contracted(b_all, up_all),
+        contracted(hidden_all, f_all),
     )
     attention_sum, gate_sum, up_sum, down_sum, small_sum = reduce_gradients(partials, small)
 
@@ -1274,13 +1619,16 @@
 
     small_natural = gather_columns(small_sum)
     own = attention_sum[:OWN_ROWS]
+    heads = own[:, :KV_AT].reshape(OWN_ROWS, 18, HEAD_SIZE)
+    d_query = jnp.stack([heads[:, HEAD_ORDER.index(head)] for head in range(QUERY_HEADS)], axis=1)
+    d_value = jnp.concatenate([own[:, 1536:1792], own[:, 1472:1536]], axis=1)
     return (
-        output[None],
-        gather_columns(grad_state)[None],
-        own[:, :960].reshape(-1),
-        own[:, 960:1280].reshape(-1),
-        own[:, 1280:1600].reshape(-1),
-        gather_columns(own[:, 1664:]).reshape(-1),
+        moved(output, True)[None],
+        moved(input_grad, True)[None],
+        d_query.reshape(-1),
+        own[:, 1152:1472].reshape(-1),
+        d_value.reshape(-1),
+        gather_columns(own[:, O_AT:]).reshape(-1),
         gate_sum[:OWN_ROWS].reshape(-1),
         up_sum[:OWN_ROWS].reshape(-1),
         gather_columns(down_sum).reshape(-1),
@@ -1296,12 +1644,16 @@
     def rows(flat):
         return flat.astype(narrow).reshape(OWN_ROWS, -1)
 
+    heads = rows(w_query).reshape(OWN_ROWS, QUERY_HEADS, HEAD_SIZE)
+    empty = jnp.zeros((OWN_ROWS, HEAD_SIZE), narrow)
+    queries = [heads[:, head] if head >= 0 else empty for head in HEAD_ORDER]
+    values = rows(value_weight)
     attention = jnp.concatenate(
-        [
-            rows(w_query),
+        queries
+        + [
             rows(key_weight),
-            rows(value_weight),
-            jnp.zeros((OWN_ROWS, 64), narrow),
+            values[:, 256:],
+            values[:, :256],
             unscaled_product(rows(w_out), spread).astype(narrow),
         ],
         axis=1,

time: 488 us -> 475 us (0.973)
  Pallas kernels: 214 us -> 348 us
  matrix products: 120 us -> 21.6 us
  starting transfers between devices: 39.9 us -> 16.3 us
  other arithmetic: 23.6 us -> 8.67 us
    pallas_call x0 -> x1, Pallas kernels: none -> 145 us  [run_block(): pl.pallas_call(block_kernel, out_shape=[jax.ShapeDtypeStruct(shape, dtype...]
    dot_general x43 -> x0, matrix products: 64.7 us -> none  [the longest x16 33.9 us: right_product(): lax.dot_general(left, right, (((1,), (1,)), ((), ())), preferred_element_...]
    dot_general x28 -> x2, matrix products: 36.2 us -> 1.58 us  [unscaled_product(): return jnp.dot(left, right, preferred_element_type=jnp.float32)]
    ppermute x14 -> x5, starting transfers between devices: 39.9 us -> 16.3 us  [moved(): return lax.ppermute(value, ('seq', 'rep'), pairs)]
    pallas_call x1, Pallas kernels: 132 us -> 121 us  [reduce_gradients(): pl.pallas_call(reduce_kernel, out_shape=[jax.ShapeDtypeStruct(shape, jnp....]
    unnamed x372 -> x49, local copies, waits for them, and re-layouts: 19.9 us -> 14.5 us
    ppermute x14 -> x5, waiting for transfers between devices: 36.7 us -> 35.4 us  [moved(): return lax.ppermute(value, ('seq', 'rep'), pairs)]
  transfers between devices with their start and end apart: 14 -> 5, of which waited for: 11 -> 2; matrix products, arithmetic and copies ran while one was open for 5% -> 6% of each run, Pallas kernels for 0% -> 18%
where the time goes in v2:
time: 475 us; the launch traced here: 469 us
  Pallas kernels  348 us (73%)
  local copies, waits for them, and re-layouts  37 us (8%)
  waiting for transfers between devices  35.4 us (7%)
  matrix products  21.6 us (5%)
  starting transfers between devices  16.3 us (3%)
  other arithmetic  8.67 us (2%)
    pallas_call x1, Pallas kernels, run_block(): pl.pallas_call(block_kernel, out_shape=[jax.ShapeDtypeStruct(shape, dtype...  145 us
    pallas_call x1, Pallas kernels, reduce_gradients(): pl.pallas_call(reduce_kernel, out_shape=[jax.ShapeDtypeStruct(shape, jnp....  121 us
    pallas_call x1, Pallas kernels, gather_weights(): pl.pallas_call(gather_kernel, out_shape=[jax.ShapeDtypeStruct((32 * rows,...  82.7 us
    ppermute x5, waiting for transfers between devices, moved(): return lax.ppermute(value, ('seq', 'rep'), pairs)  35.4 us
    dot_general x5, matrix products, left_product(): lax.dot_general(left, right, (((0,), (0,)), ((), ())), preferred_element_...  20 us
    ppermute x5, starting transfers between devices, moved(): return lax.ppermute(value, ('seq', 'rep'), pairs)  16.3 us
    unnamed x49, local copies, waits for them, and re-layouts  14.5 us
  transfers between devices with their start and end apart: 5, of which 2 were waited for; matrix products, arithmetic and copies ran while one was open for 6% of the time, Pallas kernels for 18%

profile of v2, /device:TPU:1, one launch (start us, length us, event | category | flops | bytes accessed | tf_op | source)
XLA Modules:
  0.0 469.5 jit_solution(381776954862083657)
XLA Ops:
  2.2 1.3 fusion.17
  4.4 4.6 collective-permute-start.2
  9.0 1.1 copy.40
  10.1 3.3 collective-permute-start.1
  13.4 1.1 copy.39
  14.5 4.6 collective-permute-start
  23.8 1.0 convert_element_type.71
  28.3 82.7 %gather_weights.1 = (bf16[1024,2816]{1,0:T(8,128)(2,1)S(1)}, bf16[1024,2560]{1,0:T(8,128)(2,1)S(1)}, bf16[1024,2560]{1,0:T(8,128)(2,1)S(1)}, bf16[2560,1024]{1,0:T(8,128)(2,1)S(1)}) custom-call(bf16[32,2816]{1,0:T(8,128)(2,1)S(1)} %pad.16.refs_0_, bf16[32,2560]{1,0:T(8,128)(2,1)S(1)} %pad.17.refs_1_, bf16[32,2560]{1,0:T(8,128)(2,1)S(1)} %pad.18.refs_2_, ...), custom_call_target="tpu_custom_call" | custom-call | tf_op jit(solution)/shard_map/gather_weights/pallas_call | solution.py:627
  111.0 2.5 copy-done
  113.5 2.4 copy-done.1
  115.9 2.3 copy-done.2
  118.2 2.3 copy-done.3
  121.2 145.0 %run_block.1 = (bf16[128,960]{1,0:T(8,128)(2,1)}, f32[128,960]{1,0:T(8,128)}, f32[8,1024]{1,0:T(8,128)}, bf16[3,128,1024]{2,1,0:T(8,128)(2,1)}, bf16[3,128,1792]...) custom-call(bf16[128,960]{1,0:T(8,128)(2,1)} %copy-done.8, ...), custom_call_target="tpu_custom_call" | custom-call | tf_op jit(solution)/shard_map/run_block/pallas_call | solution.py:1515
  266.3 7.3 %bitcast_convert_fusion.2.refs_1_ = bf16[1024,2560]{1,0:T(8,128)(2,1)} fusion(bf16[3,128,1024]{2,1,0:T(8,128)(2,1)} %get-tuple-element.43, bf16[3,128,2560]{2,1,0:T(8,128)(2,1)} %get-tuple-element.44), kind=kOutput, calls=%fused_computation.2 | convolution fusion | flops 2015887360 | bytes 7995392 | tf_op jit(solution)/shard_map/dot_general | solution.py:45
  273.6 4.7 %bitcast_convert_fusion.1.refs_2_ = bf16[1024,2560]{1,0:T(8,128)(2,1)} fusion(bf16[3,128,1024]{2,1,0:T(8,128)(2,1)S(1)} %copy-done.19, bf16[3,128,2560]{2,1,0:T(8,128)(2,1)S(1)} %copy-done.13), kind=kOutput, calls=%fused_computation.1 | convolution fusion | flops 2015887360 | bytes 7995392 | tf_op jit(solution)/shard_map/dot_general | solution.py:45
  278.3 1.3 bitcast_convert_fusion.4
  279.8 2.1 bitcast_convert_fusion.3
  282.0 2.9 pad_maximum_fusion.refs_0_
  284.9 4.7 bitcast_convert_fusion.refs_3_
  289.5 120.5 %reduce_gradients.1 = (f32[32,2816]{1,0:T(8,128)}, f32[32,2560]{1,0:T(8,128)}, f32[32,2560]{1,0:T(8,128)}, f32[80,1024]{1,0:T(8,128)}, f32[8,1024]{1,0:T(8,128)}) custom-call(bf16[1024,2816]{1,0:T(8,128)(2,1)} %pad_maximum_fusion.refs_0_, bf16[1024,2560]{1,0:T(8,128)(2,1)} %bitcast_convert_fusion.2.refs_1_, ...), custom_call_target="tpu_custom_call" | custom-call | tf_op jit(solution)/shard_map/reduce_gradients/pallas_call | solution.py:985
  411.7 0.9 slice.162
  412.6 1.9 collective-permute-start.3
  414.6 1.9 collective-permute-start.4
  418.4 0.9 slice.179
  419.3 1.7 reshape.154
  421.0 1.7 reshape.155
  427.5 1.0 reshape_reshape.10
  428.7 1.2 copy.63
  429.9 1.9 reshape_reshape.11
  431.8 25.0 %collective-permute-done.3 = bf16[128,960]{1,0:T(8,128)(2,1)S(1)} collective-permute-done((bf16[128,960]{1,0:T(8,128)(2,1)S(1)}, bf16[128,960]{1,0:T(8,128)(2,1)S(1)}, u32[]{:S(2)}, u32[]{:S(2)}) %collective-permute-start.3) | collective-permute-done | bytes 245792 | tf_op jit(solution)/shard_map/ppermute | solution.py:1539
  457.7 10.4 %collective-permute-done.4 = f32[128,960]{1,0:T(8,128)S(1)} collective-permute-done((f32[128,960]{1,0:T(8,128)S(1)}, f32[128,960]{1,0:T(8,128)S(1)}, u32[]{:S(2)}, u32[]{:S(2)}) %collective-permute-start.4) | collective-permute-done | bytes 491552 | tf_op jit(solution)/shard_map/ppermute | solution.py:1539
  468.0 1.0 copy.65
  (106 shorter events, 20.1 us)
Async XLA Ops:
  0.6 26.0 %copy-start.9 = (f32[9600]{0:T(1024)S(1)}, f32[9600]{0:T(1024)}, u32[]{:S(2)}) copy-start(f32[9600]{0:T(1024)} %param.23) | copy-start | bytes 115204
  0.7 26.1 %copy-start.10 = (f32[9600]{0:T(1024)S(1)}, f32[9600]{0:T(1024)}, u32[]{:S(2)}) copy-start(f32[9600]{0:T(1024)} %param.22) | copy-start | bytes 115204
  0.7 27.1 %copy-start.5 = (f32[76800]{0:T(1024)S(1)}, f32[76800]{0:T(1024)}, u32[]{:S(2)}) copy-start(f32[76800]{0:T(1024)} %param.25) | copy-start | bytes 921604
  4.4 116.1 %collective-permute-start.2 = (f32[8,128]{1,0:T(8,128)S(1)}, f32[8,128]{1,0:T(8,128)S(1)}, u32[]{:S(2)}, u32[]{:S(2)}) collective-permute-start(f32[8,128]{1,0:T(8,128)S(1)} %maximum_maximum_fusion), channel_id=1, source_target_pairs={{0,0},{1,8},{2,16},{3,24},{4,1},{5,9},{6,17},{7,25},{8,2},{9,10},{... | collective-permute-start | bytes 12296 | tf_op jit(solution)/shard_map/ppermute | solution.py:1539
  10.1 110.4 %collective-permute-start.1 = (bf16[128,960]{1,0:T(8,128)(2,1)S(1)}, bf16[128,960]{1,0:T(8,128)(2,1)S(1)}, u32[]{:S(2)}, u32[]{:S(2)}) collective-permute-start(bf16[128,960]{1,0:T(8,128)(2,1)S(1)} %bitcast.81), channel_id=1, source_target_pairs={{0,0},{1,8},{2,16},{3,24},{4,1},{5,9},{6,17},{7,25},{8,2},{9,10},{... | collective-permute-start | bytes 737288 | tf_op jit(solution)/shard_map/ppermute | solution.py:1539
  14.5 13.6 %copy-start.6 = (f32[76800]{0:T(1024)S(1)}, f32[76800]{0:T(1024)}, u32[]{:S(2)}) copy-start(f32[76800]{0:T(1024)} %param.26) | copy-start | bytes 921604
  14.5 106.0 %collective-permute-start = (bf16[128,960]{1,0:T(8,128)(2,1)S(1)}, bf16[128,960]{1,0:T(8,128)(2,1)S(1)}, u32[]{:S(2)}, u32[]{:S(2)}) collective-permute-start(bf16[128,960]{1,0:T(8,128)(2,1)S(1)} %bitcast.82), channel_id=1, source_target_pairs={{0,0},{1,8},{2,16},{3,24},{4,1},{5,9},{6,17},{7,25},{8,2},{9,10},{... | collective-permute-start | bytes 737288 | tf_op jit(solution)/shard_map/ppermute | solution.py:1539
  111.0 2.5 copy-start
  113.5 2.4 copy-start.1
  115.9 2.3 copy-start.2
  118.2 2.3 copy-start.3
  120.4 0.6 copy-start.11
  120.5 0.7 copy-start.7
  120.5 0.8 copy-start.8
  266.3 7.3 %copy-start.13 = (bf16[3,128,2560]{2,1,0:T(8,128)(2,1)S(1)}, bf16[3,128,2560]{2,1,0:T(8,128)(2,1)}, u32[]{:S(2)}) copy-start(bf16[3,128,2560]{2,1,0:T(8,128)(2,1)} %get-tuple-element.45) | copy-start | bytes 5898244
  266.3 7.3 %copy-start.19 = (bf16[3,128,1024]{2,1,0:T(8,128)(2,1)S(1)}, bf16[3,128,1024]{2,1,0:T(8,128)(2,1)}, u32[]{:S(2)}) copy-start(bf16[3,128,1024]{2,1,0:T(8,128)(2,1)} %get-tuple-element.43) | copy-start | bytes 2359300
  273.6 4.7 %copy-start.17 = (bf16[3,128,1024]{2,1,0:T(8,128)(2,1)S(1)}, bf16[3,128,1024]{2,1,0:T(8,128)(2,1)}, u32[]{:S(2)}) copy-start(bf16[3,128,1024]{2,1,0:T(8,128)(2,1)} %get-tuple-element.41) | copy-start | bytes 2359300
  273.6 4.7 %copy-start.18 = (bf16[3,128,1024]{2,1,0:T(8,128)(2,1)S(1)}, bf16[3,128,1024]{2,1,0:T(8,128)(2,1)}, u32[]{:S(2)}) copy-start(bf16[3,128,1024]{2,1,0:T(8,128)(2,1)} %get-tuple-element.42) | copy-start | bytes 2359300
  278.3 1.3 copy-start.14
  278.3 1.5 copy-start.16
  282.0 2.9 copy-start.12
  282.0 2.9 copy-start.15
  289.5 123.1 %copy-start.21 = (bf16[128,960]{1,0:T(8,128)(2,1)S(1)}, bf16[128,960]{1,0:T(8,128)(2,1)}, u32[]{:S(2)}) copy-start(bf16[128,960]{1,0:T(8,128)(2,1)} %get-tuple-element.37) | copy-start | bytes 737284
  289.5 125.0 %copy-start.20 = (f32[128,960]{1,0:T(8,128)S(1)}, f32[128,960]{1,0:T(8,128)}, u32[]{:S(2)}) copy-start(f32[128,960]{1,0:T(8,128)} %get-tuple-element.38) | copy-start | bytes 1474564
  410.1 18.4 %copy-start.4 = (f32[80,1024]{1,0:T(8,128)S(1)}, f32[80,1024]{1,0:T(8,128)}, u32[]{:S(2)}) copy-start(f32[80,1024]{1,0:T(8,128)} %get-tuple-element.52) | copy-start | bytes 983044
  412.6 44.2 %collective-permute-start.3 = (bf16[128,960]{1,0:T(8,128)(2,1)S(1)}, bf16[128,960]{1,0:T(8,128)(2,1)S(1)}, u32[]{:S(2)}, u32[]{:S(2)}) collective-permute-start(bf16[128,960]{1,0:T(8,128)(2,1)S(1)} %copy-done.21), channel_id=1, source_target_pairs={{0,0},{8,1},{16,2},{24,3},{1,4},{9,5},{17,6},{25,7},{2,8},{10,9},{... | collective-permute-start | bytes 737288 | tf_op jit(solution)/shard_map/ppermute | solution.py:1539
  414.6 53.5 %collective-permute-start.4 = (f32[128,960]{1,0:T(8,128)S(1)}, f32[128,960]{1,0:T(8,128)S(1)}, u32[]{:S(2)}, u32[]{:S(2)}) collective-permute-start(f32[128,960]{1,0:T(8,128)S(1)} %copy-done.20), channel_id=1, source_target_pairs={{0,0},{8,1},{16,2},{24,3},{1,4},{9,5},{17,6},{25,7},{2,8},{10,9},{... | collective-permute-start | bytes 1474568 | tf_op jit(solution)/shard_map/ppermute | solution.py:1539

commit v3 on v2

--- a/solution.py
+++ b/solution.py
@@ -426,7 +426,7 @@
 N_Z = 4
 BLOCKS = ((32, 2816), (32, 2560), (32, 2560), (80, 1024))
 GATHER_ORDERS = ("uzw", "zuw", "uzw", "zuw")
-REDUCE_ORDERS = ("zuw", "uzw", "zuw", "uzw")
+REDUCE_ORDERS = ("uzw", "zuw", "uzw", "zuw")
 
 
 def place():
@@ -483,19 +483,75 @@
     return events
 
 
+def move_partners():
+    seq, rep = lax.axis_index("seq"), lax.axis_index("rep")
+    return device_of_span(rep, seq), span_of_device()[::-1], (seq * 4 + rep + 31) // 32
+
+
+def start_moves(leaving, arriving, send_sem, recv_sem, target, moves):
+    for i, (src, dst) in enumerate(zip(leaving, arriving)):
+
+        @pl.when(moves == 1)
+        def _():
+            remote(src, dst, send_sem.at[i], recv_sem.at[i], target).start()
+
+        @pl.when(moves == 0)
+        def _():
+            pltpu.make_async_copy(src, dst, recv_sem.at[i]).start()
+
+
+def wait_moves(leaving, arriving, send_sem, recv_sem, target, moves):
+    for i, (src, dst) in enumerate(zip(leaving, arriving)):
+
+        @pl.when(moves == 1)
+        def _():
+            remote(src, dst, send_sem.at[i], recv_sem.at[i], target).wait()
+
+        @pl.when(moves == 0)
+        def _():
+            pltpu.make_async_copy(src, dst, recv_sem.at[i]).wait()
+
+
+def set_meta(meta, depths, spans):
+    own = lax.axis_index("seq")
+    first, end = 0, 0
+    for sequence in range(spans.shape[1]):
+        end = end + spans[0, sequence]
+        first = jnp.where(end <= own, end, first)
+    row = lax.broadcasted_iota(jnp.int32, (8, 128), 0)
+    values = jnp.where(row == 0, depths[...], jnp.where(row == 1, own - first, 0))
+    meta[...] = values.astype(jnp.float32)
+
+
 def gather_kernel(*refs):
-    own, full = refs[:4], refs[4:8]
-    recv_sem, z_sem, u_sem, w_sem, core_sem, local_sem = refs[8:]
+    flat_in, tokens, depths, spans, places = refs[:7], refs[7], refs[8], refs[9], refs[10]
+    full, arriving = refs[11:15], refs[15:17]
+    flat, own, meta = refs[17:24], refs[24:28], refs[28]
+    spread, tiles, natural, long_rows = refs[29:33]
+    recv_sem, z_sem, u_sem, w_sem, core_sem, local_sem, move_send, move_recv, flat_sem = refs[33:]
+    leaving = (tokens, meta)
     z, u, w, core = place()
     me = block_of(z, u, w, core)
+    target, source, moves = move_partners()
     above, below = device_of(z + 1, u, w, core), device_of(z - 1, u, w, core)
     across_u, across_w = device_of(z, 1 - u, w, core), device_of(z, u, 1 - w, core)
     sibling = device_of(z, w, u, 1 - core)
 
+    loads = [
+        pltpu.make_async_copy(src, dst, flat_sem.at[i])
+        for i, (src, dst) in enumerate(zip(flat_in, flat))
+    ]
+    for copy in loads:
+        copy.start()
     barrier = pltpu.get_barrier_semaphore()
     for device in (across_u, across_w, sibling):
         pl.semaphore_signal(barrier, inc=1, device_id=device, device_id_type=MESH)
 
+    @pl.when(moves == 1)
+    def _():
+        pl.semaphore_signal(barrier, inc=1, device_id=target, device_id_type=MESH)
+        pl.semaphore_signal(barrier, inc=1, device_id=source, device_id_type=MESH)
+
     @pl.when(z < N_Z - 1)
     def _():
         pl.semaphore_signal(barrier, inc=1, device_id=above, device_id_type=MESH)
@@ -504,7 +560,12 @@
     def _():
         pl.semaphore_signal(barrier, inc=1, device_id=below, device_id_type=MESH)
 
-    pl.semaphore_wait(barrier, 4 + (z + 1) // 2 - z // 3 * 2)
+    fill_spread(spread, places)
+    set_meta(meta, depths, spans)
+    for copy in loads:
+        copy.wait()
+    pack_own(flat, own, spread, places, tiles, natural, long_rows)
+    pl.semaphore_wait(barrier, 4 + (z + 1) // 2 - z // 3 * 2 + 2 * moves)
 
     def rows(group, block):
         count = BLOCKS[group][0]
@@ -594,7 +655,10 @@
 
     actions = {"own": own_event, "first": first_event, "z": z_event, "u": u_event, "w": w_event}
     for event in gather_events():
+        if event == ("z", 0, 1, 0):
+            start_moves(leaving, arriving, move_send, move_recv, target, moves)
         actions[event[0]](*event[1:])
+    wait_moves(leaving, arriving, move_send, move_recv, target, moves)
 
     for group in range(4):
         z_first = GATHER_ORDERS[group] == "zuw"
@@ -622,76 +686,125 @@
                     copy(group, me, own[group], z_sem.at[group, 1, slot], below).wait_send()
 
 
-def gather_weights(packed):
-    sems = pltpu.SemaphoreType.DMA
+def gather_weights(flat, tokens, depths, spans):
+    narrow, wide, vmem, sems = jnp.bfloat16, jnp.float32, pltpu.VMEM, pltpu.SemaphoreType.DMA
+    anywhere, here = pl.BlockSpec(memory_space=pl.ANY), pl.BlockSpec(memory_space=vmem)
+    flat = [x.reshape(-1, 128) for x in flat]
     return pl.pallas_call(
         gather_kernel,
-        out_shape=[
-            jax.ShapeDtypeStruct((32 * rows, columns), jnp.bfloat16) for rows, columns in BLOCKS
-        ],
-        in_specs=[pl.BlockSpec(memory_space=pl.ANY)] * 4,
-        out_specs=[pl.BlockSpec(memory_space=pl.ANY)] * 4,
-        scratch_shapes=[
+        out_shape=[jax.ShapeDtypeStruct((32 * rows, columns), narrow) for rows, columns in BLOCKS]
+        + [jax.ShapeDtypeStruct(tokens.shape, narrow), jax.ShapeDtypeStruct((8, 128), wide)],
+        in_specs=[anywhere] * 8 + [here, pl.BlockSpec(memory_space=pltpu.SMEM), here],
+        out_specs=[anywhere] * 6,
+        scratch_shapes=[vmem(x.shape, wide) for x in flat]
+        + [vmem(shape, narrow) for shape in BLOCKS]
+        + [
+            vmem((8, 128), wide),
+            vmem((MODEL_WIDTH, 1024), narrow),
+            vmem((20, 32, 128), wide),
+            vmem((8, 32, 128), wide),
+            vmem((8, 80, 128), wide),
             sems((4, 32)),
             sems((4, 2, 8)),
             sems((4,)),
             sems((4,)),
             sems((4,)),
             sems((4,)),
+            sems((2,)),
+            sems((2,)),
+            sems((7,)),
         ],
         compiler_params=pltpu.CompilerParams(
-            collective_id=1, has_side_effects=True, vmem_limit_bytes=16 * 2**20
+            collective_id=1, has_side_effects=True, vmem_limit_bytes=59 * 2**20
         ),
         name="gather_weights",
-    )(*packed)
-
-
-def reduce_events():
-    events = [("small", -1)]
-
-    def entry(group):
-        return [("core", group, plane) for plane in range(4)] + [
-            ("w", group, step) for step in (3, 2, 1, 0)
-        ]
-
-    def middle(group):
-        kind = "u" if REDUCE_ORDERS[group] == "zuw" else "z_early"
-        return [(kind, group, step) for step in (3, 2, 1, 0)]
-
-    def last(group):
-        if REDUCE_ORDERS[group] == "zuw":
-            return [("z_late", group, step) for step in (3, 2, 1, 0)]
-        return [("u_late", group)]
-
-    for stage in (
-        entry(0),
-        entry(1),
-        [("small", 0)],
-        middle(0),
-        entry(2),
-        [("small", 1)],
-        middle(1),
-        last(0),
-        [("small", 2)],
-        entry(3),
-        middle(2),
-        [("small", 3)],
-        last(1),
-        middle(3),
-        [("small", 4)],
-        last(2),
-        last(3),
-    ):
-        events += stage
-    return events
+    )(*flat, tokens, depths, spans, natural_places())
+
+
+REDUCE_STEPS = (
+    ("make", 0, 3),
+    ("make", 1, 3),
+    ("w", 0, 3),
+    ("make", 0, 2),
+    ("make", 1, 1),
+    ("z_early", 0, 3, 1),
+    ("w", 1, 3),
+    ("w", 0, 2),
+    ("make", 2, 3),
+    ("z_early", 0, 3, 0),
+    ("make", 0, 0),
+    ("w", 1, 1),
+    ("make", 1, 0),
+    ("make", 3, 3),
+    ("w", 1, 0),
+    ("w", 2, 3),
+    ("make", 0, 1),
+    ("z_early", 0, 2, 1),
+    ("make", 1, 2),
+    ("w", 0, 1),
+    ("make", 2, 0),
+    ("z_early", 0, 2, 0),
+    ("z_early", 2, 3, 1),
+    ("u", 1, 3),
+    ("w", 1, 2),
+    ("z_early", 2, 3, 0),
+    ("make", 3, 1),
+    ("u", 1, 1),
+    ("w", 3, 3),
+    ("make", 2, 2),
+    ("make", 2, 1),
+    ("z_early", 0, 1, 0),
+    ("w", 2, 2),
+    ("z_late", 1, 3),
+    ("u", 1, 0),
+    ("make", 3, 0),
+    ("make", 3, 2),
+    ("u", 1, 2),
+    ("small", -1),
+    ("z_early", 0, 1, 1),
+    ("w", 2, 1),
+    ("small", 0),
+    ("w", 3, 1),
+    ("w", 3, 2),
+    ("u", 3, 3),
+    ("z_early", 2, 2, 0),
+    ("w", 2, 0),
+    ("w", 0, 0),
+    ("z_late", 1, 2),
+    ("z_early", 2, 2, 1),
+    ("z_early", 2, 1, 0),
+    ("z_late", 1, 1),
+    ("z_early", 2, 1, 1),
+    ("z_early", 2, 0, 0),
+    ("small", 1),
+    ("u", 3, 1),
+    ("u", 3, 2),
+    ("z_late", 3, 3),
+    ("z_early", 2, 0, 1),
+    ("small", 2),
+    ("z_early", 0, 0, 1),
+    ("z_late", 1, 0),
+    ("z_late", 3, 2),
+    ("w", 3, 0),
+    ("z_early", 0, 0, 0),
+    ("u_late", 2),
+    ("small", 3),
+    ("z_late", 3, 1),
+    ("u", 3, 0),
+    ("u_late", 0),
+    ("small", 4),
+    ("z_late", 3, 0),
+)
 
 
 def reduce_kernel(*refs):
-    partial, small_in, final, small_out = refs[:4], refs[4], refs[5:9], refs[9]
-    part, from_core, from_w, from_u, from_z = (refs[10 + 4 * i : 14 + 4 * i] for i in range(5))
-    small_held, small_got = refs[30:32]
+    factors_in, small_in, leaving = refs[:9], refs[9], refs[10:11]
+    final, small_out, arriving = refs[11:15], refs[15], refs[16:17]
+    part, from_core, from_w, from_u, from_z = (refs[17 + 4 * i : 21 + 4 * i] for i in range(5))
+    factors, turned = refs[37:46], refs[46]
+    small_held, small_got = refs[47:49]
     (
-        local_sem,
+        load_sem,
         core_send,
         core_recv,
         w_send,
@@ -702,7 +815,10 @@
         z_recv,
         small_send,
         small_recv,
-    ) = refs[32:]
+        move_send,
+        move_recv,
+    ) = refs[49:]
+    source, target, moves = move_partners()
     z, u, w, core = place()
     me = block_of(z, u, w, core)
     above, below = device_of(z + 1, u, w, core), device_of(z - 1, u, w, core)
@@ -722,28 +838,25 @@
     for device in partners:
         pl.semaphore_signal(barrier, inc=1, device_id=device, device_id_type=MESH)
 
+    @pl.when(moves == 1)
+    def _():
+        pl.semaphore_signal(barrier, inc=1, device_id=target, device_id_type=MESH)
+        pl.semaphore_signal(barrier, inc=1, device_id=source, device_id_type=MESH)
+
     @pl.when(middle_z)
     def _():
         pl.semaphore_signal(
             barrier, inc=1, device_id=device_of(3 - z, u, w, core), device_id_type=MESH
         )
 
-    def plane_rows(group, ref, plane):
-        count = 8 * BLOCKS[group][0]
-        return ref.at[pl.ds(plane * count, count)]
-
-    def load(group, plane):
-        return pltpu.make_async_copy(
-            plane_rows(group, partial[group], plane),
-            plane_rows(group, part[group], plane),
-            local_sem.at[group, plane],
-        )
-
-    for group in range(4):
-        for plane in range(4):
-            load(group, plane).start()
-
-    pl.semaphore_wait(barrier, 5 + (z + 1) // 2 - z // 3 * 2)
+    def load(i):
+        return pltpu.make_async_copy(factors_in[i], factors[i], load_sem.at[i])
+
+    loaded = set()
+    for i in LOAD_ORDER:
+        load(i).start()
+
+    pl.semaphore_wait(barrier, 5 + (z + 1) // 2 - z // 3 * 2 + 2 * moves)
 
     def rows(group, block):
         count = BLOCKS[group][0]
@@ -770,18 +883,42 @@
         else:
             small_out[...] = total
 
-    def core_event(group, plane):
-        load(group, plane).wait()
-        for column in (0, 1):
-            for line in (0, 1):
-                slot = slot_of(plane, column, line)
-                remote(
-                    rows(group, block_of(plane, column, line, 1 - core)),
-                    from_core[group].at[slot],
-                    core_send.at[group],
-                    core_recv.at[group, slot],
-                    sibling,
-                ).start()
+    def product(group, plane, left, right, first, width, chunk):
+        count = 8 * BLOCKS[group][0]
+        at = pl.multiple_of(plane * count, 128)
+        turned[0:count, :] = factors[left][:, pl.ds(at, count)].T
+
+        @pl.loop(0, width // chunk)
+        def _(j):
+            here = pl.multiple_of(j * chunk, 128)
+            there = pl.multiple_of(first + j * chunk, 128)
+            part[group][pl.ds(at, count), pl.ds(there, chunk)] = jnp.dot(
+                turned[0:count, :],
+                factors[right][:, pl.ds(here, chunk)],
+                preferred_element_type=jnp.float32,
+            ).astype(jnp.bfloat16)
+
+    def make_event(group, step):
+        for i in NEEDED[group]:
+            if i not in loaded:
+                load(i).wait()
+                loaded.add(i)
+
+        def action(plane, way):
+            for left, right, first, width, chunk in PRODUCTS[group]:
+                product(group, plane, left, right, first, width, chunk)
+            for column in (0, 1):
+                for line in (0, 1):
+                    slot = slot_of(plane, column, line)
+                    remote(
+                        rows(group, block_of(plane, column, line, 1 - core)),
+                        from_core[group].at[slot],
+                        core_send.at[group],
+                        core_recv.at[group, slot],
+                        sibling,
+                    ).start()
+
+        at_distance(step, action)
 
     def wait_core(group, slot):
         held = from_core[group].at[slot]
@@ -854,33 +991,34 @@
     def z_copy(group, block, way, slot):
         return remote(
             rows(group, block),
-            from_z[group].at[way, slot],
+            from_z[group].at[slot],
             z_send.at[group, way, slot],
-            z_recv.at[group, way, slot],
+            z_recv.at[group, slot],
             below if way else above,
         )
 
     def z_take(group, block, way, slot):
         z_copy(group, block, way, slot).wait_recv()
-        accumulate(group, block, [(from_z[group].at[way], slot)])
+        accumulate(group, block, [(from_z[group], slot)])
 
     def z_step(group, step, column, z_slot, terms_of):
         def action(far, way):
-            block, slot = block_of(far, column, w, core), z_slot(far)
+            block = block_of(far, column, w, core)
             accumulate(group, block, terms_of(far))
             if way >= 0:
 
                 @pl.when(z > 0)
                 def _():
-                    z_take(group, block, 0, slot)
+                    z_take(group, block, 0, z_slot(far))
 
             if way <= 0:
 
                 @pl.when(z < N_Z - 1)
                 def _():
-                    z_take(group, block, 1, slot)
+                    z_take(group, block, 1, z_slot(far if way else 4))
 
             if way:
+                slot = z_slot(4 if way < 0 and step == 1 else far)
                 z_copy(group, block, 0 if way > 0 else 1, slot).start()
 
         at_distance(step, action)
@@ -901,17 +1039,17 @@
         if step == 0:
             finish(group)
 
-    def z_early_event(group, step):
-        for column in (1 - u, u):
-            z_step(
-                group,
-                step,
-                column,
-                lambda far: far * 2 + column,
-                lambda far: gathered(group, far, column),
-            )
-            if step == 0 and column is not u:
-                u_copy(group, rows(group, block_of(z, 1 - u, w, core)), 0).start()
+    def z_early_event(group, step, other):
+        column = 1 - u if other else u
+        z_step(
+            group,
+            step,
+            column,
+            lambda far: far * 2 + column,
+            lambda far: gathered(group, far, column),
+        )
+        if step == 0 and other:
+            u_copy(group, rows(group, block_of(z, 1 - u, w, core)), 0).start()
 
     def u_late_event(group):
         u_copy(group, from_u[group].at[0], 0).wait_recv()
@@ -920,15 +1058,18 @@
 
     actions = {
         "small": small_event,
-        "core": core_event,
+        "make": make_event,
         "w": w_event,
         "u": u_event,
         "z_early": z_early_event,
         "z_late": z_late_event,
         "u_late": u_late_event,
     }
-    for event in reduce_events():
+    for event in REDUCE_STEPS:
         actions[event[0]](*event[1:])
+        if event == REDUCE_STEPS[20]:
+            start_moves(leaving, arriving, move_send, move_recv, target, moves)
+    wait_moves(leaving, arriving, move_send, move_recv, target, moves)
 
     for group in range(4):
         z_first = REDUCE_ORDERS[group] == "zuw"
@@ -946,60 +1087,82 @@
                 def _():
                     z_copy(group, me, 0, slot).wait_send()
 
-                @pl.when(z > far)
+                @pl.when(z > far + 1)
                 def _():
                     z_copy(group, me, 1, slot).wait_send()
 
+        for column in (0,) if z_first else (0, 1):
+
+            @pl.when(z > 0)
+            def _():
+                z_copy(group, me, 1, 4 if z_first else 8 + column).wait_send()
+
     for i in range(5):
         small_copy(i).wait_send()
 
 
-def reduce_gradients(partials, small):
-    narrow, sems = jnp.bfloat16, pltpu.SemaphoreType.DMA
+LOAD_ORDER = (0, 1, 2, 3, 4, 5, 6, 7, 8)
+NEEDED = ((0, 1, 2, 3), (4, 5), (4, 6), (7, 8))
+PRODUCTS = (
+    ((0, 1, 0, 1792, 256), (2, 3, 1792, 1024, 512)),
+    ((4, 5, 0, 2560, 512),),
+    ((4, 6, 0, 2560, 512),),
+    ((7, 8, 0, 1024, 512),),
+)
+
+
+def reduce_gradients(factors, small, leaving):
+    narrow, sems, vmem = jnp.bfloat16, pltpu.SemaphoreType.DMA, pltpu.VMEM
     z_first = [order == "zuw" for order in REDUCE_ORDERS]
-    scratch = [pltpu.VMEM((32 * rows, columns), narrow) for rows, columns in BLOCKS]
-    scratch += [pltpu.VMEM((16, rows, columns), narrow) for rows, columns in BLOCKS]
-    scratch += [pltpu.VMEM((8, rows, columns), narrow) for rows, columns in BLOCKS]
+    scratch = [vmem((32 * rows, columns), narrow) for rows, columns in BLOCKS]
+    scratch += [vmem((16, rows, columns), narrow) for rows, columns in BLOCKS]
+    scratch += [vmem((8, rows, columns), narrow) for rows, columns in BLOCKS]
     scratch += [
-        pltpu.VMEM((4 if first else 1, rows, columns), narrow)
+        vmem((4 if first else 1, rows, columns), narrow)
         for (rows, columns), first in zip(BLOCKS, z_first)
     ]
     scratch += [
-        pltpu.VMEM((2, 4 if first else 8, rows, columns), narrow)
+        vmem((5 if first else 10, rows, columns), narrow)
         for (rows, columns), first in zip(BLOCKS, z_first)
     ]
-    scratch += [pltpu.VMEM((5, 8, 1024), jnp.float32)] * 2
+    scratch += [vmem(x.shape, narrow) for x in factors]
+    scratch += [vmem((640, RECUR * 128), narrow)]
+    scratch += [vmem((5, 8, 1024), jnp.float32)] * 2
     scratch += [
-        sems((4, 4)),
+        sems((9,)),
         sems((4,)),
         sems((4, 16)),
         sems((4,)),
         sems((4, 8)),
         sems((4,)),
         sems((4, 4)),
-        sems((4, 2, 8)),
-        sems((4, 2, 8)),
+        sems((4, 2, 10)),
+        sems((4, 10)),
         sems((5,)),
         sems((5,)),
+        sems((1,)),
+        sems((1,)),
     ]
+    anywhere, here = pl.BlockSpec(memory_space=pl.ANY), pl.BlockSpec(memory_space=vmem)
     return pl.pallas_call(
         reduce_kernel,
         out_shape=[jax.ShapeDtypeStruct(shape, jnp.float32) for shape in BLOCKS]
-        + [jax.ShapeDtypeStruct((8, 1024), jnp.float32)],
-        in_specs=[pl.BlockSpec(memory_space=pl.ANY)] * 4
-        + [pl.BlockSpec(memory_space=pltpu.VMEM)],
-        out_specs=[pl.BlockSpec(memory_space=pltpu.VMEM)] * 5,
+        + [jax.ShapeDtypeStruct((8, 1024), jnp.float32)]
+        + [jax.ShapeDtypeStruct(x.shape, x.dtype) for x in leaving],
+        in_specs=[anywhere] * 9 + [here, anywhere],
+        out_specs=[here] * 5 + [anywhere],
         scratch_shapes=scratch,
         compiler_params=pltpu.CompilerParams(
-            collective_id=2, has_side_effects=True, vmem_limit_bytes=58 * 2**20
+            collective_id=2, has_side_effects=True, vmem_limit_bytes=60 * 2**20
         ),
         name="reduce_gradients",
-    )(*partials, small)
+    )(*factors, small, *leaving)
 
 
 Q_TILES = 9
 O_AT, KV_AT, KV_WIDTH = 1792, 1152, 640
 CHUNK = 512
+SUB = 64
 
 
 def dot_nn(left, right):
@@ -1036,15 +1199,18 @@
 
 
 def block_kernel(*refs):
-    (tokens, cotangent, meta, rope, turn, gains, places, wa_in, wg_in, wu_in, wd_in) = refs[:11]
-    (output, input_grad, small, a_all, gqkv_all, o_all, gt_all, b_all, gg_all, gu_all, hidden_all, gf_all) = refs[11:23]
+    (tokens, cotangent, meta, rope, turn, gain_a, gain_f, routers, wa_in, wg_in, wu_in, wd_in) = refs[:12]
+    (output, input_grad, small, a_all, gqkv_all, o_all, gt_all, b_all, gg_all, gu_all, hidden_all, gf_all) = refs[12:24]
     (
-        wa, wg, wu, wd, spread, o_spread, h_all, z_all, tf_all, gate_all, up_all, q_all, window,
-        got, sending, depth_win, depth_at, bias_at, cos_at, sin_at, stats, o_at, dkv, grad, acc, gg_at, gu_at,
+        wa, wg, wu, wd, gains, natural_at, padded_at, cotangent_at, leaving, h_all, z_all, tf_all, gate_all, up_all, q_all, window,
+        got, sending, depth_win, depth_at, bias_at, cos_at, sin_at, stats, dkv, grad, acc, gg_at, gu_at,
+        keys_at, s_at, gp_at, p_at, gs_at, qs_at, us_at, move_send, move_recv,
         load_sem, out_sem, kv_send, kv_recv, back_send, back_recv, depth_send, depth_recv,
-    ) = refs[23:]
+    ) = refs[24:]
     narrow, wide = jnp.bfloat16, jnp.float32
     group, span = span_of_device()
+    core = span % 2
+    target, source, moves = move_partners()
 
     barrier = pltpu.get_barrier_semaphore()
     for away in (1, 2, 3):
@@ -1060,6 +1226,11 @@
             pl.semaphore_signal(
                 barrier, inc=1, device_id=device_of_span(group, span - away), device_id_type=MESH
             )
+
+    @pl.when(moves == 1)
+    def _():
+        pl.semaphore_signal(barrier, inc=1, device_id=target, device_id_type=MESH)
+        pl.semaphore_signal(barrier, inc=1, device_id=source, device_id_type=MESH)
 
     loads = [
         pltpu.make_async_copy(src, dst, load_sem.at[i])
@@ -1077,7 +1248,8 @@
             for recursion in range(RECUR):
                 window[recursion, 3 - away] = jnp.zeros((128, KV_WIDTH), narrow)
 
-    pl.semaphore_wait(barrier, 3 + span + span // 4 * (7 - 2 * span))
+    pl.semaphore_wait(barrier, 3 + span + span // 4 * (7 - 2 * span) + 2 * moves)
+    start_moves((cotangent,), (cotangent_at,), move_send.at[pl.ds(0, 1)], move_recv.at[pl.ds(0, 1)], target, moves)
 
     def depth_copy(away, device):
         return remote(
@@ -1088,21 +1260,21 @@
             device,
         )
 
-    def kv_copy(recursion, away, device):
+    def kv_copy(recursion, slot, to_slot, sent, device):
         return remote(
-            window.at[recursion, 3],
-            window.at[recursion, 3 - away],
-            kv_send.at[recursion, away - 1],
-            kv_recv.at[recursion, away - 1],
+            window.at[recursion, slot],
+            window.at[recursion, to_slot],
+            kv_send.at[recursion, sent],
+            kv_recv.at[recursion, to_slot],
             device,
         )
 
-    def back_copy(recursion, away, device):
+    def back_copy(recursion, slot, device):
         return remote(
-            sending.at[away - 1],
-            got.at[recursion, away - 1],
-            back_send.at[recursion, away - 1],
-            back_recv.at[recursion, away - 1],
+            sending.at[slot],
+            got.at[recursion, slot],
+            back_send.at[recursion, slot],
+            back_recv.at[recursion, slot],
             device,
         )
 
@@ -1112,53 +1284,94 @@
             pltpu.make_async_copy(gu_at, gu_all.at[recursion], out_sem.at[1]),
         ]
 
-    def to_later(copy):
-        for away in (1, 2, 3):
-
-            @pl.when(span + away < 8)
-            def _():
-                copy(away, device_of_span(group, span + away)).start()
-
-    def to_earlier(copy):
-        for away in (1, 2, 3):
-
-            @pl.when(span - away >= 0)
-            def _():
-                copy(away, device_of_span(group, span - away)).start()
-
-    def wait_each(valid, waiting):
-        for away in (1, 2, 3):
-
-            @pl.when(valid(away))
-            def _():
-                waiting(away)
-
-    def has_later(away):
-        return span + away < 8
-
-    def has_earlier(away):
-        return span - away >= 0
+    def neighbour(away):
+        return device_of_span(group, span + away)
+
+    sibling = neighbour(1 - 2 * core)
+
+    def when(condition, action):
+        @pl.when(condition)
+        def _():
+            action()
+
+    def send_keys(recursion):
+        when(span + 2 < 8, lambda: kv_copy(recursion, 3, 1, 0, neighbour(2)).start())
+        when(core == 0, lambda: kv_copy(recursion, 3, 2, 1, sibling).start())
+        when(
+            (core == 1) & (span + 3 < 8),
+            lambda: kv_copy(recursion, 3, 0, 1, neighbour(3)).start(),
+        )
+
+    def pass_keys_on(recursion):
+        @pl.when(span >= 2)
+        def _():
+            kv_copy(recursion, 3, 1, 0, sibling).wait_recv()
+            kv_copy(recursion, 1, 2 * core, 2, sibling).start()
+
+    def wait_keys(recursion):
+        when(span >= 1, lambda: kv_copy(recursion, 3, 2, 1, sibling).wait_recv())
+        when(span >= 3, lambda: kv_copy(recursion, 3, 0, 1, sibling).wait_recv())
+
+    def wait_keys_sent(recursion):
+        when(span + 2 < 8, lambda: kv_copy(recursion, 3, 1, 0, sibling).wait_send())
+        when(core == 0, lambda: kv_copy(recursion, 3, 2, 1, sibling).wait_send())
+        when(
+            (core == 1) & (span + 3 < 8),
+            lambda: kv_copy(recursion, 3, 0, 1, sibling).wait_send(),
+        )
+        when(span >= 2, lambda: kv_copy(recursion, 1, 2, 2, sibling).wait_send())
+
+    def send_back(recursion):
+        @pl.when(span >= 2)
+        def _():
+            sending[0] = dkv[pl.ds(pl.multiple_of(256 * (1 - core), 128), 128), :].astype(narrow)
+            back_copy(recursion, 0, sibling).start()
+
+        sending[2] = dkv[pl.ds(pl.multiple_of(256 * core, 128), 128), :].astype(narrow)
+        when(core == 1, lambda: back_copy(recursion, 2, sibling).start())
+        when(
+            (core == 0) & (span >= 3),
+            lambda: back_copy(recursion, 2, neighbour(-3)).start(),
+        )
+
+    def pass_back_on(recursion):
+        @pl.when(span >= 2)
+        def _():
+            back_copy(recursion, 0, sibling).wait_recv()
+            sending[1] = (dkv[128:256, :] + got[recursion, 0].astype(wide)).astype(narrow)
+            back_copy(recursion, 1, neighbour(-2)).start()
+
+    def take_back(recursion):
+        @pl.when((core == 0) | (span + 3 < 8))
+        def _():
+            back_copy(recursion, 2, sibling).wait_recv()
+            dkv[384:512, :] += got[recursion, 2].astype(wide)
+
+        @pl.when(span + 2 < 8)
+        def _():
+            back_copy(recursion, 1, sibling).wait_recv()
+            dkv[384:512, :] += got[recursion, 1].astype(wide)
+
+    def wait_back_sent(recursion):
+        when(span >= 2, lambda: back_copy(recursion, 0, sibling).wait_send())
+        when(span >= 2, lambda: back_copy(recursion, 1, sibling).wait_send())
+        when((core == 1) | (span >= 3), lambda: back_copy(recursion, 2, sibling).wait_send())
+
+    def add_pads():
+        for block in range(32):
+            padded_at[block * PADDED_ROWS : block * PADDED_ROWS + OWN_ROWS, :] = natural_at[
+                block * OWN_ROWS : block * OWN_ROWS + OWN_ROWS, :
+            ]
+
+    def drop_pads():
+        for block in range(32):
+            natural_at[block * OWN_ROWS : block * OWN_ROWS + OWN_ROWS, :] = padded_at[
+                block * PADDED_ROWS : block * PADDED_ROWS + OWN_ROWS, :
+            ]
 
     here = device_of_span(group, span)
-    to_later(depth_copy)
-
-    @pl.loop(0, MODEL_WIDTH // 64)
-    def _(i):
-        at = pl.multiple_of(i * 64, 64)
-        rows = lax.broadcasted_iota(jnp.int32, (64, 1024), 0) + at
-        spread[pl.ds(at, 64), :] = jnp.where(rows == places[0:1, :], 1.0, 0.0).astype(narrow)
-
-    for tile in range(Q_TILES):
-        at = lax.broadcasted_iota(jnp.int32, (128, 1024), 0)
-        pair, part = tile // 3, tile % 3
-        low, high = (6 * pair + part) * 64, (6 * pair + 3 + part) * 64 - 64
-        if pair == 2:
-            target = jnp.where(at < 64, -2, at + (12 + part) * 64 - 64)
-        else:
-            target = jnp.where(at < 64, at + low, at + high)
-        o_spread[pl.ds(tile * 128, 128), :] = jnp.where(
-            target == places[0:1, :], 1.0, 0.0
-        ).astype(narrow)
+    for away in (1, 2, 3):
+        when(span + away < 8, lambda: depth_copy(away, neighbour(away)).start())
 
     span_lane = meta[1:2, :]
     turn_cos = jnp.zeros((1, 128), wide)
@@ -1170,11 +1383,20 @@
     sign = jnp.where(lanes((128, 128)) % 64 < 32, -1.0, 1.0)
     sin_at[...] = sign * (turn_sin * rope[0] + turn_cos * rope[1])
 
-    h_all[0] = dot_nn(tokens[...], spread[...])
-    grad[...] = dot_nn(cotangent[...], spread[...])
+    padded_at[...] = jnp.zeros((1024, 128), wide)
+    vectors = jnp.concatenate(
+        [gain_a[...], gain_f[...], routers[...], jnp.zeros((123, MODEL_WIDTH), wide)], axis=0
+    )
+    natural_at[...] = vectors.T
+    add_pads()
+    gains[...] = padded_at[...].T[0:8, :]
+    natural_at[...] = tokens[...].astype(wide)
+    add_pads()
+    h_all[0] = padded_at[...].T
     small[...] = jnp.zeros((8, 1024), wide)
 
-    wait_each(has_earlier, lambda away: depth_copy(away, here).wait_recv())
+    for away in (1, 2, 3):
+        when(span - away >= 0, lambda: depth_copy(away, here).wait_recv())
     row = lax.broadcasted_iota(jnp.int32, (128, 128), 0)
     column = lanes((128, 128))
     ones = jnp.ones((128, 128), wide)
@@ -1192,7 +1414,7 @@
                 allowed = (row == column) | (active & (row <= column))
             else:
                 allowed = active & (span_lane >= 3 - block)
-            bias_at[pl.ds(block * 128, 128), :] = jnp.where(allowed, 0.0, masked_score)
+            bias_at[pl.ds(block * 128, 128), :] = jnp.where(allowed, 0.0, masked_score).astype(narrow)
 
     def inverse_rms(value):
         return lax.rsqrt(
@@ -1209,80 +1431,126 @@
         )
         return jax.nn.sigmoid(logits)
 
-    def halves(tile, pair, key_side):
+    def halves(tile, pair):
         low = lanes(tile.shape) < 64
         zero = jnp.zeros_like(tile)
         if pair == 2:
-            return jnp.where(low, tile, zero) if key_side else jnp.where(low, zero, tile)
+            return jnp.where(low, tile, zero)
         return jnp.concatenate([jnp.where(low, tile, zero), jnp.where(low, zero, tile)], axis=0)
 
-    def key_tile(recursion, pair):
-        parts = [window[recursion, b, :, pair * 128 : pair * 128 + 128] for b in range(4)]
-        return jnp.concatenate(parts, axis=0)
+    def set_keys(recursion, pair):
+        for block in range(4):
+            at = pl.ds(block * 128, 128)
+            keys_at[at, 0:128] = window[recursion, block, :, pair * 128 : pair * 128 + 128]
+            keys_at[at, 128:256] = bias_at[at, :]
 
     def value_tile(recursion, pair):
         at = 256 if pair == 2 else 384 + pair * 128
         parts = [window[recursion, b, :, at : at + 128] for b in range(4)]
         return jnp.concatenate(parts, axis=0)
 
-    def biased(scores):
-        bias = bias_at[...]
-        if scores.shape[1] == 128:
-            return scores + bias
-        return scores + jnp.concatenate([bias, bias], axis=1)
-
-    def joined(out, pair, key_side):
+    def set_scores(recursion, pair, part, buffer):
+        at = (pair * 3 + part) * 128
+        queries = halves(q_all[recursion, :, at : at + 128], pair)
+        width = queries.shape[0]
+        same = jnp.where(row == column, 1.0, 0.0).astype(narrow)
+        same = same if width == 128 else jnp.concatenate([same, same], axis=0)
+        both = jnp.concatenate([queries, same], axis=1)
+        s_at[buffer, :, 0:width] = dot_nt(keys_at[...], both)
+        return queries, width
+
+    def rows_of_eight(value, join):
+        return join(value.reshape(value.shape[0] // 8, 8, value.shape[1]), axis=0)
+
+    def joined(out, pair):
         if pair == 2:
-            if key_side:
-                out = jnp.where(row < 64, out, 0.0)
-            return out.T
+            return jnp.where(row < 64, out, 0.0).T
         return jnp.where(row < 64, out[:, :128], out[:, 128:]).T
 
     def attend(recursion):
         for pair in range(3):
-            keys, values_t = key_tile(recursion, pair), value_tile(recursion, pair).T
-
-            @pl.loop(0, 3)
-            def _(part):
-                at = pl.multiple_of((pair * 3 + part) * 128, 128)
-                queries = halves(q_all[recursion, :, pl.ds(at, 128)], pair, True)
-                scores = biased(dot_nt(keys, queries))
-                top = jnp.max(scores, axis=0, keepdims=True)
-                weight = jnp.exp(scores - top)
-                inverse = 1.0 / jnp.sum(weight, axis=0, keepdims=True)
-                width = scores.shape[1]
-                stats[recursion, pair * 3 + part, 0:1, 0:width] = top
-                stats[recursion, pair * 3 + part, 1:2, 0:width] = inverse
-                out = dot_nn(values_t, (weight * inverse).astype(narrow))
-                o_at[:, pl.ds(at, 128)] = joined(out, pair, False).astype(narrow)
+            set_keys(recursion, pair)
+            values_t = value_tile(recursion, pair).T
+            for part in range(3):
+                buffer = part % 2
+                _, width = set_scores(recursion, pair, part, buffer)
+                top = jnp.full((8, width), masked_score, wide)
+                for sub in range(0, 512, SUB):
+                    scores = s_at[buffer, sub : sub + SUB, 0:width]
+                    top = jnp.maximum(top, rows_of_eight(scores, jnp.max))
+                top = jnp.max(top, axis=0, keepdims=True)
+                total = jnp.zeros((8, width), wide)
+                for sub in range(0, 512, SUB):
+                    weight = jnp.exp(s_at[buffer, sub : sub + SUB, 0:width] - top)
+                    total = total + rows_of_eight(weight, jnp.sum)
+                    p_at[sub : sub + SUB, part * 256 : part * 256 + width] = weight.astype(narrow)
+                total = jnp.sum(total, axis=0, keepdims=True)
+                stats[recursion, pair * 3 + part, 0:1, 0:width] = top + jnp.log(total)
+                out = dot_nn(values_t, p_at[:, part * 256 : part * 256 + width]) / total
+                if pair == 2:
+                    head = (12 + part) * HEAD_SIZE
+                    natural_at[head : head + 64, :] = out[64:, :]
+                else:
+                    head = (6 * pair + part) * HEAD_SIZE
+                    natural_at[head : head + 64, :] = out[:64, :128]
+                    head = (6 * pair + 3 + part) * HEAD_SIZE
+                    natural_at[head : head + 64, :] = out[64:, 128:]
+
+    def upstream_of(pair, part):
+        zero = jnp.zeros((64, 128), narrow)
+
+        def head(number):
+            return natural_at[number * 64 : number * 64 + 64, :].astype(narrow)
+
+        if pair == 2:
+            return jnp.concatenate([zero, head(12 + part)], axis=0)
+        low = jnp.concatenate([head(6 * pair + part), zero], axis=1)
+        high = jnp.concatenate([zero, head(6 * pair + 3 + part)], axis=1)
+        return jnp.concatenate([low, high], axis=0)
 
     def attend_back(recursion):
         for pair in range(3):
-            keys, values = key_tile(recursion, pair), value_tile(recursion, pair)
-            keys_t = keys.T
-            value_at = 256 if pair == 2 else 384 + pair * 128
-            dkv[:, pair * 128 : pair * 128 + 128] = jnp.zeros((512, 128), wide)
-            if pair < 2:
-                dkv[:, value_at : value_at + 128] = jnp.zeros((512, 128), wide)
-
-            @pl.loop(0, 3)
-            def _(part):
-                at = pl.multiple_of((pair * 3 + part) * 128, 128)
-                queries = halves(q_all[recursion, :, pl.ds(at, 128)], pair, True)
-                upstream = halves(o_at[:, pl.ds(at, 128)], pair, False)
-                scores = biased(dot_nt(keys, queries))
-                width = scores.shape[1]
-                top = stats[recursion, pair * 3 + part, 0:1, 0:width]
-                inverse = stats[recursion, pair * 3 + part, 1:2, 0:width]
-                probs = jnp.exp(scores - top) * inverse
-                grad_probs = dot_nt(values, upstream)
-                inner = jnp.sum(probs * grad_probs, axis=0, keepdims=True)
-                grad_scores = (probs * (grad_probs - inner)).astype(narrow)
-                dkv[:, pair * 128 : pair * 128 + 128] += dot_nn(grad_scores, queries)
-                dkv[:, value_at : value_at + 128] += dot_nn(probs.astype(narrow), upstream)
-                out = dot_nn(keys_t, grad_scores)
-                gqkv_all[recursion, :, pl.ds(at, 128)] = rotated(
-                    joined(out, pair, True), cos_at[...] * 0.125, sin_at[...] * -0.125
+            set_keys(recursion, pair)
+            values = value_tile(recursion, pair)
+            keys_t = keys_at[:, 0:128].T
+            width = 128 if pair == 2 else 256
+            for part in range(3):
+                buffer = part % 2
+                queries, _ = set_scores(recursion, pair, part, buffer)
+                upstream = upstream_of(pair, part)
+                qs_at[part * width : part * width + width, :] = queries
+                us_at[:, part * width : part * width + width] = upstream
+                gp_at[buffer, :, 0:width] = dot_nn(values, upstream)
+                log_total = stats[recursion, pair * 3 + part, 0:1, 0:width]
+                inner = jnp.zeros((8, width), wide)
+                where = slice(part * width, part * width + width)
+                for sub in range(0, 512, SUB):
+                    probs = jnp.exp(s_at[buffer, sub : sub + SUB, 0:width] - log_total)
+                    s_at[buffer, sub : sub + SUB, 0:width] = probs
+                    p_at[sub : sub + SUB, where] = probs.astype(narrow)
+                    inner = inner + rows_of_eight(
+                        probs * gp_at[buffer, sub : sub + SUB, 0:width], jnp.sum
+                    )
+                inner = jnp.sum(inner, axis=0, keepdims=True)
+                for sub in range(0, 512, SUB):
+                    rows = slice(sub, sub + SUB)
+                    gs_at[rows, where] = (
+                        s_at[buffer, rows, 0:width] * (gp_at[buffer, rows, 0:width] - inner)
+                    ).astype(narrow)
+            grad_keys = dot_nn(gs_at[:, 0 : 3 * width], qs_at[0 : 3 * width, :])
+            grad_values = dot_nt(p_at[:, 0 : 3 * width], us_at[:, 0 : 3 * width])
+            if pair == 2:
+                dkv[:, 256:384] = grad_keys + grad_values
+            else:
+                dkv[:, pair * 128 : pair * 128 + 128] = grad_keys
+                dkv[:, 384 + pair * 128 : 512 + pair * 128] = grad_values
+            out = dot_nn(keys_t, gs_at[:, 0 : 3 * width])
+            for part in range(3):
+                at = (pair * 3 + part) * 128
+                gqkv_all[recursion, :, at : at + 128] = rotated(
+                    joined(out[:, part * width : part * width + width], pair),
+                    cos_at[...] * 0.125,
+                    sin_at[...] * -0.125,
                 ).astype(narrow)
 
     def rotate_keys(value, sine):
@@ -1311,7 +1579,7 @@
 
         pair_values = dot_nn(a_b, wa[:, KV_AT:O_AT])
         window[recursion, 3] = rotate_keys(pair_values, sin_at[...]).astype(narrow)
-        to_later(lambda away, device: kv_copy(recursion, away, device))
+        send_keys(recursion)
         cosine, sine = cos_at[...] * 0.125, sin_at[...] * 0.125
         for first, width in ((0, 512), (512, 512), (1024, 128)):
             queries = dot_nn(a_all[recursion], wa[:, first : first + width])
@@ -1320,9 +1588,11 @@
                     queries[:, at : at + 128], cosine, sine
                 ).astype(narrow)
         set_bias(recursion)
-        wait_each(has_earlier, lambda away: kv_copy(recursion, away, here).wait_recv())
+        pass_keys_on(recursion)
+        wait_keys(recursion)
         attend(recursion)
-        o_pad = dot_nn(o_at[...], o_spread[...]).astype(narrow)
+        add_pads()
+        o_pad = padded_at[...].T.astype(narrow)
         o_all[recursion] = o_pad
         branch = dot_nn(o_pad, wa[:, O_AT:])
         middle = h_all[recursion] + branch
@@ -1357,7 +1627,15 @@
 
         @pl.when(recursion == RECUR - 1)
         def _():
-            output[...] = dot_nt(following.astype(narrow), spread[...]).astype(narrow)
+            padded_at[...] = following.astype(narrow).astype(wide).T
+            drop_pads()
+            leaving[...] = natural_at[...].astype(narrow)
+
+    start_moves((leaving,), (output,), move_send.at[pl.ds(1, 1)], move_recv.at[pl.ds(1, 1)], source, moves)
+    wait_moves((cotangent,), (cotangent_at,), move_send.at[pl.ds(0, 1)], move_recv.at[pl.ds(0, 1)], target, moves)
+    natural_at[...] = cotangent_at[...].astype(wide)
+    add_pads()
+    grad[...] = padded_at[...].T
 
     @pl.loop(0, RECUR)
     def _(i):
@@ -1405,29 +1683,20 @@
         gt_b = (tf_all[recursion] + grad_middle).astype(narrow)
         gt_all[recursion] = gt_b
         grad[...] += grad_middle
-        go_pad = dot_nt(gt_b, wa[:, O_AT:]).astype(narrow)
-        o_at[...] = dot_nt(go_pad, o_spread[...]).astype(narrow)
+        padded_at[...] = dot_nt(gt_b, wa[:, O_AT:]).T
+        drop_pads()
         set_bias(recursion)
         attend_back(recursion)
 
         @pl.when(recursion < RECUR - 1)
         def _():
-            wait_each(has_earlier, lambda away: back_copy(recursion + 1, away, here).wait_send())
-
-        for away in (1, 2, 3):
-            sending[away - 1] = dkv[
-                (3 - away) * 128 : (4 - away) * 128, :
-            ].astype(narrow)
-        to_earlier(lambda away, device: back_copy(recursion, away, device))
+            wait_back_sent(recursion + 1)
+
+        send_back(recursion)
+        pass_back_on(recursion)
         acc[...] = dot_nt(gqkv_all[recursion, :, :KV_AT], wa[:, :KV_AT])
 
-        @pl.loop(1, 4)
-        def _(away):
-            @pl.when(span + away < 8)
-            def _():
-                back_copy(recursion, away, here).wait_recv()
-                dkv[384:512, :] += got[recursion, away - 1].astype(wide)
-
+        take_back(recursion)
         gqkv_all[recursion, :, KV_AT:] = rotate_keys(dkv[384:512, :], -sin_at[...]).astype(narrow)
         grad_normed = acc[...] + dot_nt(gqkv_all[recursion, :, KV_AT:], wa[:, KV_AT:O_AT])
         state = h_all[recursion]
@@ -1440,19 +1709,16 @@
 
     for copy in stage_copies(0):
         copy.wait()
-    total = grad[...]
-    first = total.astype(narrow)
-    rest = total - first.astype(wide)
-    second = rest.astype(narrow)
-    third = (rest - second.astype(wide)).astype(narrow)
-    input_grad[...] = (
-        dot_nt(first, spread[...]) + dot_nt(second, spread[...]) + dot_nt(third, spread[...])
-    )
-
-    wait_each(has_later, lambda away: depth_copy(away, here).wait_send())
+    padded_at[...] = grad[...].T
+    drop_pads()
+    input_grad[...] = natural_at[...].astype(narrow)
+
+    wait_moves((leaving,), (output,), move_send.at[pl.ds(1, 1)], move_recv.at[pl.ds(1, 1)], source, moves)
+    for away in (1, 2, 3):
+        when(span + away < 8, lambda: depth_copy(away, here).wait_send())
     for recursion in range(RECUR):
-        wait_each(has_later, lambda away: kv_copy(recursion, away, here).wait_send())
-    wait_each(has_earlier, lambda away: back_copy(0, away, here).wait_send())
+        wait_keys_sent(recursion)
+    wait_back_sent(0)
 
 
 def run_block(tokens, cotangent, meta, gains, weights):
@@ -1465,11 +1731,7 @@
     jump = np.arange(4)[:, None] * 128.0 * frequency[None, :]
     turn = np.zeros((16, 128), np.float32)
     turn[:4], turn[8:12] = np.cos(jump), np.sin(jump)
-    padded = np.arange(1024)
-    natural = padded // PADDED_ROWS * OWN_ROWS + padded % PADDED_ROWS
-    natural = np.where(padded % PADDED_ROWS < OWN_ROWS, natural, -1)
-    places = np.broadcast_to(natural[None], (8, 1024)).astype(np.int32)
-    outs = [((128, MODEL_WIDTH), narrow), ((128, MODEL_WIDTH), wide), ((8, 1024), wide)]
+    outs = [((MODEL_WIDTH, 128), narrow), ((MODEL_WIDTH, 128), narrow), ((8, 1024), wide)]
     outs += [
         ((RECUR, 128, width), narrow)
         for width in (1024, O_AT, 1024, 1024, 1024, 2560, 2560, 2560, 1024)
@@ -1479,8 +1741,11 @@
         vmem((1024, 2560), narrow),
         vmem((1024, 2560), narrow),
         vmem((2560, 1024), narrow),
-        vmem((MODEL_WIDTH, 1024), narrow),
-        vmem((KV_AT, 1024), narrow),
+        vmem((8, 1024), wide),
+        vmem((MODEL_WIDTH, 128), wide),
+        vmem((1024, 128), wide),
+        vmem((MODEL_WIDTH, 128), narrow),
+        vmem((MODEL_WIDTH, 128), narrow),
         vmem((RECUR, 128, 1024), wide),
         vmem((RECUR, 128, 1024), wide),
         vmem((RECUR, 128, 1024), wide),
@@ -1492,16 +1757,24 @@
         vmem((3, 128, KV_WIDTH), narrow),
         vmem((4, 8, 128), wide),
         vmem((512, 128), narrow),
-        vmem((512, 128), wide),
+        vmem((512, 128), narrow),
         vmem((128, 128), wide),
         vmem((128, 128), wide),
         vmem((RECUR, Q_TILES, 2, 256), wide),
-        vmem((128, KV_AT), narrow),
         vmem((512, KV_WIDTH), wide),
         vmem((128, 1024), wide),
         vmem((128, 1024), wide),
         vmem((128, 2560), narrow),
         vmem((128, 2560), narrow),
+        vmem((512, 256), narrow),
+        vmem((2, 512, 256), wide),
+        vmem((2, 512, 256), wide),
+        vmem((512, 768), narrow),
+        vmem((512, 768), narrow),
+        vmem((768, 128), narrow),
+        vmem((128, 768), narrow),
+        sems((2,)),
+        sems((2,)),
         sems((4,)),
         sems((2,)),
         sems((RECUR, 3)),
@@ -1511,42 +1784,196 @@
         sems((3,)),
         sems((3,)),
     ]
-    here = pl.BlockSpec(memory_space=vmem)
+    here, anywhere = pl.BlockSpec(memory_space=vmem), pl.BlockSpec(memory_space=pl.ANY)
     return pl.pallas_call(
         block_kernel,
         out_shape=[jax.ShapeDtypeStruct(shape, dtype) for shape, dtype in outs],
-        in_specs=[here] * 7 + [pl.BlockSpec(memory_space=pl.ANY)] * 4,
-        out_specs=[here] * 8 + [pl.BlockSpec(memory_space=pl.ANY)] * 2 + [here] * 2,
+        in_specs=[here, anywhere] + [here] * 6 + [anywhere] * 4,
+        out_specs=[here] * 8 + [anywhere] * 2 + [here] * 2,
         scratch_shapes=scratch,
         compiler_params=pltpu.CompilerParams(
-            collective_id=3, has_side_effects=True, vmem_limit_bytes=59 * 2**20
+            collective_id=3, has_side_effects=True, vmem_limit_bytes=60 * 2**20
         ),
         name="run_block",
-    )(tokens, cotangent, meta, rope, turn, gains, places, *weights)
-
-
-HEAD_ORDER = (0, 3, 1, 4, 2, 5, 6, 9, 7, 10, 8, 11, 12, -1, 13, -1, 14, -1)
-
-
-def moved(value, back=False):
-    pairs = []
-    for span in range(8):
-        for group in range(4):
-            seq, rep = device_of_span(group, span)
-            pairs.append((span * 4 + group, seq * 4 + rep))
-    if back:
-        pairs = [(there, here) for here, there in pairs]
-    return lax.ppermute(value, ("seq", "rep"), pairs)
-
-
-def span_index(seq_spans):
-    chain = lax.axis_size("seq")
-    lengths = seq_spans[0]
-    seq_ends = jnp.cumsum(lengths)
-    own = lax.axis_index("seq")
-    starts = seq_ends - lengths
-    inside = (starts <= own) & (own < seq_ends)
-    return own - jnp.sum(jnp.where(inside, starts, 0))
+    )(tokens, cotangent, meta, rope, turn, *gains, *weights)
+
+
+HEAD_TILES = tuple(
+    (6 * (tile // 3) + tile % 3, 6 * (tile // 3) + 3 + tile % 3) if tile < 6 else (6 + tile, -1)
+    for tile in range(9)
+)
+NATURAL_TILES = tuple((2 * tile, 2 * tile + 1 if tile < 7 else -1) for tile in range(8))
+
+
+def fill_spread(spread, places):
+    @pl.loop(0, MODEL_WIDTH // 64)
+    def _(i):
+        at = pl.multiple_of(i * 64, 64)
+        rows = lax.broadcasted_iota(jnp.int32, (64, 1024), 0) + at
+        spread[pl.ds(at, 64), :] = jnp.where(rows == places[0:1, :], 1.0, 0.0).astype(jnp.bfloat16)
+
+
+def chunk_rows(flat, units, pairs, parity, unit):
+    where = units * parity + unit
+    return flat[pl.ds(where // 2, pairs, stride=units), :], where % 2
+
+
+def placed_half(found, low):
+    value, half = found
+    return value if half == (0 if low else 1) else pltpu.roll(value, 64, 1)
+
+
+def pack_tiles(flat, out, first, tiles, units, pairs):
+    low = lax.broadcasted_iota(jnp.int32, (pairs, 128), 1) < 64
+    zero = jnp.zeros((pairs, 128), jnp.float32)
+    for parity in (0, 1):
+        for tile, (left, right) in enumerate(tiles):
+            one = placed_half(chunk_rows(flat, units, pairs, parity, left), True) if left >= 0 else zero
+            two = (
+                placed_half(chunk_rows(flat, units, pairs, parity, right), False)
+                if right >= 0
+                else zero
+            )
+            out[first + tile, pl.ds(parity, pairs, stride=2), :] = jnp.where(low, one, two)
+
+
+def pack_own(flat, own, spread, places, tiles, natural, long_rows):
+    w_query, w_key, w_value, w_out, w_gate, w_up, w_down = flat
+    attention, gate, up, down = own
+    narrow = jnp.bfloat16
+    tiles[...] = jnp.zeros(tiles.shape, jnp.float32)
+    natural[...] = jnp.zeros(natural.shape, jnp.float32)
+    pack_tiles(w_query, tiles, 0, HEAD_TILES, 15, 15)
+    pack_tiles(w_key, tiles, 9, ((0, 1), (2, 3), (4, -1)), 5, 15)
+    pack_tiles(w_value, tiles, 12, ((0, 1), (2, 3), (-1, 4)), 5, 15)
+    low = lax.broadcasted_iota(jnp.int32, (32, 128), 1) < 64
+    tiles[11] = jnp.where(low, tiles[11], tiles[14])
+    for tile in range(14):
+        attention[:, tile * 128 : tile * 128 + 128] = tiles[tile].astype(narrow)
+    pack_tiles(w_out, natural, 0, NATURAL_TILES, 15, 15)
+    for source, out in ((w_gate, gate), (w_up, up)):
+        for tile in range(20):
+            tiles[tile, 0:OWN_ROWS] = source[pl.ds(tile, OWN_ROWS, stride=20), :]
+            tiles[tile, OWN_ROWS:] = jnp.zeros((PADDED_ROWS - OWN_ROWS, 128), jnp.float32)
+            out[:, tile * 128 : tile * 128 + 128] = tiles[tile].astype(narrow)
+    pack_tiles(w_down, long_rows, 0, NATURAL_TILES, 15, 40)
+    both = jnp.concatenate([side_by_side(natural), side_by_side(long_rows)], axis=0)
+    both = dot_nn(both.astype(narrow), spread[...]).astype(narrow)
+    attention[:, 1792:], down[...] = both[0:32], both[32:112]
+
+
+def side_by_side(tiles):
+    return jnp.concatenate([tiles[tile] for tile in range(8)], axis=1)[:, 0:MODEL_WIDTH]
+
+
+def natural_places():
+    padded = np.arange(1024)
+    natural = padded // PADDED_ROWS * OWN_ROWS + padded % PADDED_ROWS
+    natural = np.where(padded % PADDED_ROWS < OWN_ROWS, natural, -1)
+    return np.broadcast_to(natural[None], (8, 1024)).astype(np.int32)
+
+
+def unpack_tiles(packed, first, tiles, units, pairs, out):
+    spots = {}
+    for tile, heads in enumerate(tiles):
+        for half, unit in enumerate(heads):
+            if unit >= 0:
+                spots[unit] = (tile, half)
+    low = lax.broadcasted_iota(jnp.int32, (pairs, 128), 1) < 64
+
+    def unit_at(where, is_low):
+        parity, unit = where // units, where % units
+        tile, half = spots[unit]
+        value = packed[first + tile, pl.ds(parity, pairs, stride=2), :]
+        return placed_half((value, half), is_low)
+
+    for chunk in range(units):
+        out[pl.ds(chunk, pairs, stride=units), :] = jnp.where(
+            low, unit_at(2 * chunk, True), unit_at(2 * chunk + 1, False)
+        )
+
+
+def exact_gathered(value, spread):
+    first = value.astype(jnp.bfloat16)
+    rest = value - first.astype(jnp.float32)
+    second = rest.astype(jnp.bfloat16)
+    third = (rest - second.astype(jnp.float32)).astype(jnp.bfloat16)
+    summed = dot_nt(jnp.concatenate([first, second, third], axis=0), spread[...])
+    rows = value.shape[0]
+    return summed[0:rows] + summed[rows : 2 * rows] + summed[2 * rows :]
+
+
+def split_tiles(value, tiles):
+    for tile in range(7):
+        tiles[tile] = value[:, tile * 128 : tile * 128 + 128]
+    tiles[7, :, 0:64] = value[:, 896:960]
+
+
+def unpack_kernel(*refs):
+    inside, places = refs[:7], refs[7]
+    d_query, d_key, d_value, d_out, d_gate, d_up, d_down = refs[8:15]
+    d_attn, d_ffn, d_router, output, input_grad = refs[15:20]
+    held, (spread, tiles, natural, long_rows, sems) = refs[20:26], refs[26:]
+    copies = [
+        pltpu.make_async_copy(src, dst, sems.at[i])
+        for i, (src, dst) in enumerate(zip(inside, held + (output,)))
+    ]
+    for copy in copies:
+        copy.start()
+    fill_spread(spread, places)
+    for copy in copies[:6]:
+        copy.wait()
+    attention, gate, up, down, small, moved_grad = held
+    input_grad[...] = moved_grad[...].astype(jnp.float32)
+    for tile in range(14):
+        tiles[tile] = attention[:, tile * 128 : tile * 128 + 128]
+    unpack_tiles(tiles, 0, HEAD_TILES, 15, 15, d_query)
+    unpack_tiles(tiles, 9, ((0, 1), (2, 3), (4, -1)), 5, 15, d_key)
+    unpack_tiles(tiles, 11, ((-1, 4), (0, 1), (2, 3)), 5, 15, d_value)
+    for packed, out in ((gate, d_gate), (up, d_up)):
+        for tile in range(20):
+            out[pl.ds(tile, OWN_ROWS, stride=20), :] = packed[
+                0:OWN_ROWS, tile * 128 : tile * 128 + 128
+            ]
+    gathered = exact_gathered(
+        jnp.concatenate([attention[:, 1792:], down[...], small[...]], axis=0), spread
+    )
+    split_tiles(gathered[0:32], natural)
+    unpack_tiles(natural, 0, NATURAL_TILES, 15, 15, d_out)
+    split_tiles(gathered[32:112], long_rows)
+    unpack_tiles(long_rows, 0, NATURAL_TILES, 15, 40, d_down)
+    d_attn[...], d_ffn[...], d_router[...] = gathered[112:113], gathered[113:114], gathered[114:117]
+    copies[6].wait()
+
+
+def unpack_gradients(sums, small, input_grad, output):
+    narrow, wide, vmem = jnp.bfloat16, jnp.float32, pltpu.VMEM
+    here, anywhere = pl.BlockSpec(memory_space=vmem), pl.BlockSpec(memory_space=pl.ANY)
+    flat = (225, 75, 75, 225, 600, 600, 600)
+    inside = (*sums, small, input_grad, output)
+    return pl.pallas_call(
+        unpack_kernel,
+        out_shape=[jax.ShapeDtypeStruct((rows, 128), wide) for rows in flat]
+        + [
+            jax.ShapeDtypeStruct((1, MODEL_WIDTH), wide),
+            jax.ShapeDtypeStruct((1, MODEL_WIDTH), wide),
+            jax.ShapeDtypeStruct((RECUR, MODEL_WIDTH), wide),
+            jax.ShapeDtypeStruct((MODEL_WIDTH, 128), narrow),
+            jax.ShapeDtypeStruct((MODEL_WIDTH, 128), wide),
+        ],
+        in_specs=[anywhere] * 7 + [here],
+        out_specs=[here] * 10 + [anywhere, here],
+        scratch_shapes=[vmem(x.shape, x.dtype) for x in inside[:6]]
+        + [
+            vmem((MODEL_WIDTH, 1024), narrow),
+            vmem((14, 32, 128), wide),
+            vmem((8, 32, 128), wide),
+            vmem((8, 80, 128), wide),
+            pltpu.SemaphoreType.DMA((7,)),
+        ],
+        compiler_params=pltpu.CompilerParams(vmem_limit_bytes=59 * 2**20),
+        name="unpack_gradients",
+    )(*inside, natural_places())
 
 
 def per_device_fast(
@@ -1565,105 +1992,28 @@
     ffn_gain,
     router,
 ):
-    narrow, wide = jnp.bfloat16, jnp.float32
-    natural = jnp.arange(MODEL_WIDTH, dtype=jnp.int32)
-    padded_at = (natural // OWN_ROWS) * PADDED_ROWS + natural % OWN_ROWS
-    spread = (padded_at[:, None] == jnp.arange(PADDED_WIDTH, dtype=jnp.int32)[None, :]).astype(narrow)
-    packed = pack_weights(
-        spread, w_query, key_weight, value_weight, w_out, w_gate, w_up, w_down
-    )
-    weights = gather_weights(packed)
-    gains = jnp.concatenate([attn_gain[None], ffn_gain[None], router], axis=0)
-    gains = jnp.pad(
-        gains.reshape(5, 32, OWN_ROWS), ((0, 3), (0, 0), (0, PADDED_ROWS - OWN_ROWS))
-    ).reshape(8, PADDED_WIDTH)
-    index = span_index(seq_spans)
-    meta = jnp.concatenate(
-        [
-            depths.astype(wide),
-            jnp.broadcast_to(index.astype(wide), (1, 128)),
-            jnp.zeros((6, 128), wide),
-        ],
-        axis=0,
-    )
-    (
-        output,
-        input_grad,
-        small,
-        a_all,
-        qkv_all,
-        o_all,
-        t_all,
-        b_all,
-        gate_all,
-        up_all,
-        hidden_all,
-        f_all,
-    ) = run_block(moved(tokens[0]), moved(cotangent[0]), moved(meta), gains, weights)
-
-    def contracted(left, right):
-        return left_product(
-            left.reshape(RECUR * 128, -1), right.reshape(RECUR * 128, -1)
-        ).astype(narrow)
-
-    partials = (
-        jnp.concatenate([contracted(a_all, qkv_all), contracted(o_all, t_all)], axis=1),
-        contracted(b_all, gate_all),
-        contracted(b_all, up_all),
-        contracted(hidden_all, f_all),
-    )
-    attention_sum, gate_sum, up_sum, down_sum, small_sum = reduce_gradients(partials, small)
-
-    def gather_columns(x):
-        return x.reshape(x.shape[0], 32, PADDED_ROWS)[:, :, :OWN_ROWS].reshape(x.shape[0], MODEL_WIDTH)
-
-    small_natural = gather_columns(small_sum)
-    own = attention_sum[:OWN_ROWS]
-    heads = own[:, :KV_AT].reshape(OWN_ROWS, 18, HEAD_SIZE)
-    d_query = jnp.stack([heads[:, HEAD_ORDER.index(head)] for head in range(QUERY_HEADS)], axis=1)
-    d_value = jnp.concatenate([own[:, 1536:1792], own[:, 1472:1536]], axis=1)
+    *weights, own_tokens, own_meta = gather_weights(
+        (w_query, key_weight, value_weight, w_out, w_gate, w_up, w_down),
+        tokens[0].T,
+        depths,
+        seq_spans,
+    )
+    output, input_grad, small, *factors = run_block(
+        own_tokens, cotangent[0].T, own_meta, (attn_gain[None], ffn_gain[None], router), weights
+    )
+    *sums, small_sum, input_grad = reduce_gradients(
+        [x.reshape(RECUR * 128, -1) for x in factors], small, (input_grad,)
+    )
+    *gradients, d_attn, d_ffn, d_router, output, input_grad = unpack_gradients(
+        sums, small_sum, input_grad, output
+    )
     return (
-        moved(output, True)[None],
-        moved(input_grad, True)[None],
-        d_query.reshape(-1),
-        own[:, 1152:1472].reshape(-1),
-        d_value.reshape(-1),
-        gather_columns(own[:, O_AT:]).reshape(-1),
-        gate_sum[:OWN_ROWS].reshape(-1),
-        up_sum[:OWN_ROWS].reshape(-1),
-        gather_columns(down_sum).reshape(-1),
-        small_natural[0],
-        small_natural[1],
-        small_natural[2:5],
-    )
-
-
-def pack_weights(spread, w_query, key_weight, value_weight, w_out, w_gate, w_up, w_down):
-    narrow = jnp.bfloat16
-
-    def rows(flat):
-        return flat.astype(narrow).reshape(OWN_ROWS, -1)
-
-    heads = rows(w_query).reshape(OWN_ROWS, QUERY_HEADS, HEAD_SIZE)
-    empty = jnp.zeros((OWN_ROWS, HEAD_SIZE), narrow)
-    queries = [heads[:, head] if head >= 0 else empty for head in HEAD_ORDER]
-    values = rows(value_weight)
-    attention = jnp.concatenate(
-        queries
-        + [
-            rows(key_weight),
-            values[:, 256:],
-            values[:, :256],
-            unscaled_product(rows(w_out), spread).astype(narrow),
-        ],
-        axis=1,
-    )
-    extra = ((0, PADDED_ROWS - OWN_ROWS), (0, 0))
-    return (
-        jnp.pad(attention, extra),
-        jnp.pad(rows(w_gate), extra),
-        jnp.pad(rows(w_up), extra),
-        unscaled_product(w_down.astype(narrow).reshape(-1, MODEL_WIDTH), spread).astype(narrow),
+        output.T[None],
+        input_grad.T[None],
+        *[x.reshape(-1) for x in gradients],
+        d_attn[0],
+        d_ffn[0],
+        d_router,
     )
 
 

time: 475 us -> 322 us (0.68)
  local copies, waits for them, and re-layouts: 37 us -> 0 us
  waiting for transfers between devices: 35.4 us -> 0 us
  Pallas kernels: 348 us -> 320 us
  matrix products: 21.6 us -> 0 us
  starting transfers between devices: 16.3 us -> 0 us
  other arithmetic: 8.67 us -> 0 us
    ppermute x5 -> x0, waiting for transfers between devices: 35.4 us -> none  [moved(): return lax.ppermute(value, ('seq', 'rep'), pairs)]
    pallas_call x1, Pallas kernels: 145 us -> 115 us  [run_block(): pl.pallas_call(block_kernel, out_shape=[jax.ShapeDtypeStruct(shape, dtype...]
    dot_general x7 -> x0, matrix products: 21.6 us -> none  [the longest x5 20 us: left_product(): lax.dot_general(left, right, (((0,), (0,)), ((), ())), preferred_element_...]
    pallas_call x1, Pallas kernels: 121 us -> 103 us  [reduce_gradients(): pl.pallas_call(reduce_kernel, out_shape=[jax.ShapeDtypeStruct(shape, jnp....]
    ppermute x5 -> x0, starting transfers between devices: 16.3 us -> none  [moved(): return lax.ppermute(value, ('seq', 'rep'), pairs)]
    unnamed x49 -> x0, local copies, waits for them, and re-layouts: 14.5 us -> none
    pallas_call x0 -> x1, Pallas kernels: none -> 10.6 us  [unpack_gradients(): pl.pallas_call(unpack_kernel, out_shape=[jax.ShapeDtypeStruct((rows, 128)...]
    pallas_call x1, Pallas kernels: 82.7 us -> 91.9 us  [gather_weights(): pl.pallas_call(gather_kernel, out_shape=[jax.ShapeDtypeStruct((32 * rows,...]
  transfers between devices with their start and end apart: 5 -> 0, of which waited for: 2 -> 0; matrix products, arithmetic and copies ran while one was open for 6% -> 0% of each run, Pallas kernels for 18% -> 0%
where the time goes in v3:
time: 322 us; the launch traced here: 321 us
  Pallas kernels  320 us (99%)
    pallas_call x1, Pallas kernels, run_block(): pl.pallas_call(block_kernel, out_shape=[jax.ShapeDtypeStruct(shape, dtype...  115 us
    pallas_call x1, Pallas kernels, reduce_gradients(): pl.pallas_call(reduce_kernel, out_shape=[jax.ShapeDtypeStruct(shape, jnp....  103 us
    pallas_call x1, Pallas kernels, gather_weights(): pl.pallas_call(gather_kernel, out_shape=[jax.ShapeDtypeStruct((32 * rows,...  91.9 us
    pallas_call x1, Pallas kernels, unpack_gradients(): pl.pallas_call(unpack_kernel, out_shape=[jax.ShapeDtypeStruct((rows, 128)...  10.6 us

profile of v3, /device:TPU:1, one launch (start us, length us, event | category | flops | bytes accessed | tf_op | source)
XLA Modules:
  0.0 321.1 jit_solution(11159305228681003827)
XLA Ops:
  0.6 91.9 %gather_weights.1 = (bf16[1024,2816]{1,0:T(8,128)(2,1)}, bf16[1024,2560]{1,0:T(8,128)(2,1)}, bf16[1024,2560]{1,0:T(8,128)(2,1)}, bf16[2560,1024]{1,0:T(8,128)(2,...) custom-call(f32[225,128]{1,0:T(8,128)} %bitcast.53, f32[75,128]{1,0:T(8,128)} %bitcast.55, f32[75,128]{1,0:T(8,128)} %bitcast.56, ...), custom_call_target="tpu_custom_call" | custom-call | tf_op jit(solution)/shard_map/gather_weights/pallas_call | solution.py:693
  92.6 114.6 %run_block.1 = (bf16[960,128]{1,0:T(8,128)(2,1)}, bf16[960,128]{1,0:T(8,128)(2,1)}, f32[8,1024]{1,0:T(8,128)}, bf16[3,128,1024]{2,1,0:T(8,128)(2,1)}, bf16[3,128...) custom-call(bf16[960,128]{1,0:T(8,128)(2,1)} %get-tuple-element.48.r, ...), custom_call_target="tpu_custom_call" | custom-call | tf_op jit(solution)/shard_map/run_block/pallas_call | solution.py:1788
  207.2 103.2 %reduce_gradients.1 = (f32[32,2816]{1,0:T(8,128)}, f32[32,2560]{1,0:T(8,128)}, f32[32,2560]{1,0:T(8,128)}, f32[80,1024]{1,0:T(8,128)}, f32[8,1024]{1,0:T(8,128)}, /*index=5*/bf16[960,128]{1,0:T(8,128)(2,1)}) custom-call(bf16[384,1024]{1,0:T(8,128)(2,1)} %bitcast.43, bf16[384,1792]{1,0:T(8,128)(2,1)} %bitcast.42, bf16[384,1024]{1,0:T(8,128)(2,1)} %bitcast.44, ...), custom_call_target="tpu_custom_call" | custom-call | tf_op jit(solution)/shard_map/reduce_gradients/pallas_call | solution.py:1147
  310.4 10.6 %unpack_gradients.1 = (f32[225,128]{1,0:T(8,128)}, f32[75,128]{1,0:T(8,128)}, f32[75,128]{1,0:T(8,128)}, f32[225,128]{1,0:T(8,128)}, f32[600,128]{1,0:T(8,128)},...) custom-call(f32[32,2816]{1,0:T(8,128)} %get-tuple-element.65.refs_0_, ...), custom_call_target="tpu_custom_call" | custom-call | tf_op jit(solution)/shard_map/unpack_gradients/pallas_call | solution.py:1954

commit v4 on v3

--- a/solution.py
+++ b/solution.py
@@ -426,7 +426,7 @@
 N_Z = 4
 BLOCKS = ((32, 2816), (32, 2560), (32, 2560), (80, 1024))
 GATHER_ORDERS = ("uzw", "zuw", "uzw", "zuw")
-REDUCE_ORDERS = ("uzw", "zuw", "uzw", "zuw")
+REDUCE_ORDERS = ("uzw", "uzw", "zuw", "zuw")
 
 
 def place():
@@ -458,7 +458,7 @@
 
 
 def gather_events():
-    events = [("own", group) for group in range(4)]
+    events = [("own", group) for group in (1, 2, 0, 3)]
     for step in range(6):
         for group in range(4):
             if GATHER_ORDERS[group] == "zuw":
@@ -485,7 +485,8 @@
 
 def move_partners():
     seq, rep = lax.axis_index("seq"), lax.axis_index("rep")
-    return device_of_span(rep, seq), span_of_device()[::-1], (seq * 4 + rep + 31) // 32
+    apart = (seq * 4 + rep) * (seq * 4 + rep - 13)
+    return device_of_span(rep, seq), span_of_device()[::-1], (apart * apart + 999999) // 1000000
 
 
 def start_moves(leaving, arriving, send_sem, recv_sem, target, moves):
@@ -560,11 +561,10 @@
     def _():
         pl.semaphore_signal(barrier, inc=1, device_id=below, device_id_type=MESH)
 
-    fill_spread(spread, places)
     set_meta(meta, depths, spans)
     for copy in loads:
         copy.wait()
-    pack_own(flat, own, spread, places, tiles, natural, long_rows)
+    pack_wide(flat, own, tiles)
     pl.semaphore_wait(barrier, 4 + (z + 1) // 2 - z // 3 * 2 + 2 * moves)
 
     def rows(group, block):
@@ -655,6 +655,9 @@
 
     actions = {"own": own_event, "first": first_event, "z": z_event, "u": u_event, "w": w_event}
     for event in gather_events():
+        if event == ("own", 0):
+            fill_spread(spread, places)
+            pack_rest(flat, own, spread, tiles, natural, long_rows)
         if event == ("z", 0, 1, 0):
             start_moves(leaving, arriving, move_send, move_recv, target, moves)
         actions[event[0]](*event[1:])
@@ -722,77 +725,77 @@
 
 
 REDUCE_STEPS = (
-    ("make", 0, 3),
-    ("make", 1, 3),
-    ("w", 0, 3),
-    ("make", 0, 2),
-    ("make", 1, 1),
-    ("z_early", 0, 3, 1),
-    ("w", 1, 3),
-    ("w", 0, 2),
-    ("make", 2, 3),
-    ("z_early", 0, 3, 0),
-    ("make", 0, 0),
-    ("w", 1, 1),
-    ("make", 1, 0),
-    ("make", 3, 3),
-    ("w", 1, 0),
-    ("w", 2, 3),
-    ("make", 0, 1),
-    ("z_early", 0, 2, 1),
-    ("make", 1, 2),
-    ("w", 0, 1),
-    ("make", 2, 0),
-    ("z_early", 0, 2, 0),
-    ("z_early", 2, 3, 1),
-    ("u", 1, 3),
-    ("w", 1, 2),
-    ("z_early", 2, 3, 0),
-    ("make", 3, 1),
-    ("u", 1, 1),
-    ("w", 3, 3),
     ("make", 2, 2),
     ("make", 2, 1),
+    ("small", -1),
+    ("w", 2, 2),
+    ("make", 0, 3),
+    ("w", 0, 3),
+    ("make", 1, 3),
+    ("make", 2, 3),
+    ("w", 1, 3),
+    ("u", 2, 2),
+    ("make", 0, 2),
+    ("w", 2, 1),
+    ("z_early", 1, 3, 1),
+    ("make", 3, 3),
+    ("w", 0, 2),
+    ("z_early", 1, 3, 0),
+    ("w", 3, 3),
+    ("w", 2, 3),
+    ("z_early", 0, 3, 1),
+    ("make", 0, 1),
+    ("make", 1, 1),
+    ("z_early", 0, 3, 0),
+    ("make", 3, 1),
+    ("small", 0),
+    ("w", 0, 1),
+    ("w", 1, 1),
+    ("z_early", 0, 2, 0),
+    ("make", 1, 2),
+    ("z_early", 0, 2, 1),
+    ("make", 3, 2),
+    ("u", 2, 1),
+    ("u", 2, 3),
     ("z_early", 0, 1, 0),
-    ("w", 2, 2),
-    ("z_late", 1, 3),
-    ("u", 1, 0),
+    ("w", 1, 2),
+    ("z_early", 0, 1, 1),
+    ("small", 1),
+    ("w", 3, 1),
+    ("z_early", 1, 2, 1),
+    ("z_late", 2, 3),
+    ("u", 3, 3),
+    ("w", 3, 2),
+    ("make", 2, 0),
+    ("u", 3, 1),
+    ("make", 1, 0),
+    ("z_late", 2, 2),
+    ("z_early", 1, 1, 1),
+    ("w", 2, 0),
+    ("make", 0, 0),
+    ("w", 1, 0),
     ("make", 3, 0),
-    ("make", 3, 2),
-    ("u", 1, 2),
-    ("small", -1),
-    ("z_early", 0, 1, 1),
-    ("w", 2, 1),
-    ("small", 0),
-    ("w", 3, 1),
-    ("w", 3, 2),
-    ("u", 3, 3),
-    ("z_early", 2, 2, 0),
-    ("w", 2, 0),
+    ("z_early", 1, 2, 0),
     ("w", 0, 0),
-    ("z_late", 1, 2),
-    ("z_early", 2, 2, 1),
-    ("z_early", 2, 1, 0),
-    ("z_late", 1, 1),
-    ("z_early", 2, 1, 1),
-    ("z_early", 2, 0, 0),
-    ("small", 1),
-    ("u", 3, 1),
+    ("z_late", 2, 1),
+    ("small", 2),
+    ("z_early", 1, 1, 0),
     ("u", 3, 2),
+    ("z_early", 0, 0, 1),
     ("z_late", 3, 3),
-    ("z_early", 2, 0, 1),
-    ("small", 2),
-    ("z_early", 0, 0, 1),
-    ("z_late", 1, 0),
+    ("small", 3),
+    ("z_early", 0, 0, 0),
+    ("z_early", 1, 0, 1),
+    ("z_early", 1, 0, 0),
+    ("w", 3, 0),
+    ("u", 2, 0),
     ("z_late", 3, 2),
-    ("w", 3, 0),
-    ("z_early", 0, 0, 0),
-    ("u_late", 2),
-    ("small", 3),
+    ("u_late", 1),
+    ("u", 3, 0),
     ("z_late", 3, 1),
-    ("u", 3, 0),
+    ("small", 4),
     ("u_late", 0),
-    ("small", 4),
+    ("z_late", 2, 0),
     ("z_late", 3, 0),
 )
 
@@ -904,21 +907,19 @@
                 load(i).wait()
                 loaded.add(i)
 
-        def action(plane, way):
-            for left, right, first, width, chunk in PRODUCTS[group]:
-                product(group, plane, left, right, first, width, chunk)
-            for column in (0, 1):
-                for line in (0, 1):
-                    slot = slot_of(plane, column, line)
-                    remote(
-                        rows(group, block_of(plane, column, line, 1 - core)),
-                        from_core[group].at[slot],
-                        core_send.at[group],
-                        core_recv.at[group, slot],
-                        sibling,
-                    ).start()
-
-        at_distance(step, action)
+        plane = (z, z + 1 - 2 * (z % 2), (z + 2) % 4, 3 - z)[step]
+        for left, right, first, width, chunk in PRODUCTS[group]:
+            product(group, plane, left, right, first, width, chunk)
+        for column in (0, 1):
+            for line in (0, 1):
+                slot = slot_of(plane, column, line)
+                remote(
+                    rows(group, block_of(plane, column, line, 1 - core)),
+                    from_core[group].at[slot],
+                    core_send.at[group],
+                    core_recv.at[group, slot],
+                    sibling,
+                ).start()
 
     def wait_core(group, slot):
         held = from_core[group].at[slot]
@@ -1101,7 +1102,7 @@
         small_copy(i).wait_send()
 
 
-LOAD_ORDER = (0, 1, 2, 3, 4, 5, 6, 7, 8)
+LOAD_ORDER = (4, 6, 0, 1, 2, 3, 5, 7, 8)
 NEEDED = ((0, 1, 2, 3), (4, 5), (4, 6), (7, 8))
 PRODUCTS = (
     ((0, 1, 0, 1792, 256), (2, 3, 1792, 1024, 512)),
@@ -1161,7 +1162,7 @@
 
 Q_TILES = 9
 O_AT, KV_AT, KV_WIDTH = 1792, 1152, 640
-CHUNK = 512
+CHUNK = 1280
 SUB = 64
 
 
@@ -1179,12 +1180,12 @@
     seq = lax.axis_index("seq")
     rep = lax.axis_index("rep")
     z, x, y, core = seq // 2, seq % 2, rep // 2, rep % 2
-    return z, (2 * x + y + x * (1 - 2 * y)) * 2 + core
+    return z, (2 * y + x + y * (1 - 2 * x)) * 2 + core
 
 
 def device_of_span(group, span):
     chip = span // 2
-    x, y = chip // 2, (chip + 1) // 2 % 2
+    x, y = (chip + 1) // 2 % 2, chip // 2
     return (group * 2 + x, y * 2 + span % 2)
 
 
@@ -1200,11 +1201,12 @@
 
 def block_kernel(*refs):
     (tokens, cotangent, meta, rope, turn, gain_a, gain_f, routers, wa_in, wg_in, wu_in, wd_in) = refs[:12]
-    (output, input_grad, small, a_all, gqkv_all, o_all, gt_all, b_all, gg_all, gu_all, hidden_all, gf_all) = refs[12:24]
+    (output, input_grad, small) = refs[12:15]
+    a_out, gqkv_out, o_out, gt_out, b_out, gg_all, gu_all, hidden_out, gf_out = refs[15:24]
     (
-        wa, wg, wu, wd, gains, natural_at, padded_at, cotangent_at, leaving, h_all, z_all, tf_all, gate_all, up_all, q_all, window,
-        got, sending, depth_win, depth_at, bias_at, cos_at, sin_at, stats, dkv, grad, acc, gg_at, gu_at,
-        keys_at, s_at, gp_at, p_at, gs_at, qs_at, us_at, move_send, move_recv,
+        wa, wg, wu, wd, gains, natural_at, padded_at, cotangent_at, leaving, h_all, z_all, tf_all, gate_all, up_all, q_all, window_two, window_one,
+        got_two, got_one, sending_two, sending_one, depth_win, depth_at, bias_at, cos_at, sin_at, stats, dkv, grad, acc, gg_at, gu_at,
+        keys_at, s_at, gp_at, p_at, gs_at, qs_at, us_at, move_send, move_recv, a_all, gqkv_all, o_all, gt_all, b_all, hidden_all, gf_all, factor_sem,
         load_sem, out_sem, kv_send, kv_recv, back_send, back_recv, depth_send, depth_recv,
     ) = refs[24:]
     narrow, wide = jnp.bfloat16, jnp.float32
@@ -1246,10 +1248,9 @@
         def _():
             depth_win[3 - away] = jnp.zeros((8, 128), wide)
             for recursion in range(RECUR):
-                window[recursion, 3 - away] = jnp.zeros((128, KV_WIDTH), narrow)
-
-    pl.semaphore_wait(barrier, 3 + span + span // 4 * (7 - 2 * span) + 2 * moves)
-    start_moves((cotangent,), (cotangent_at,), move_send.at[pl.ds(0, 1)], move_recv.at[pl.ds(0, 1)], target, moves)
+                window_two[recursion, 3 - away] = jnp.zeros((2, 128, 256), narrow)
+                window_one[recursion, 3 - away] = jnp.zeros((128, 128), narrow)
+
 
     def depth_copy(away, device):
         return remote(
@@ -1260,23 +1261,54 @@
             device,
         )
 
-    def kv_copy(recursion, slot, to_slot, sent, device):
+    def window(recursion, slot, pair):
+        if pair == 2:
+            return window_one.at[recursion, slot]
+        return window_two.at[recursion, slot, pair]
+
+    def kv_copy(recursion, pair, slot, to_slot, sent, device):
         return remote(
-            window.at[recursion, slot],
-            window.at[recursion, to_slot],
-            kv_send.at[recursion, sent],
-            kv_recv.at[recursion, to_slot],
+            window(recursion, slot, pair),
+            window(recursion, to_slot, pair),
+            kv_send.at[recursion, pair, sent],
+            kv_recv.at[recursion, pair, to_slot],
             device,
         )
 
-    def back_copy(recursion, slot, device):
+    def sending(slot, pair):
+        return sending_one.at[slot] if pair == 2 else sending_two.at[slot, pair]
+
+    def got(recursion, slot, pair):
+        return got_one.at[recursion, slot] if pair == 2 else got_two.at[recursion, slot, pair]
+
+    def back_copy(recursion, pair, slot, device):
         return remote(
-            sending.at[slot],
-            got.at[recursion, slot],
-            back_send.at[recursion, slot],
-            back_recv.at[recursion, slot],
+            sending(slot, pair),
+            got(recursion, slot, pair),
+            back_send.at[recursion, pair, slot],
+            back_recv.at[recursion, pair, slot],
             device,
         )
+
+    def pair_lanes(pair):
+        return slice(512, 640) if pair == 2 else slice(pair * 256, pair * 256 + 256)
+
+    def factor_copies(recursion, which):
+        pairs = (
+            (a_all, a_out),
+            (o_all, o_out),
+            (b_all, b_out),
+            (hidden_all, hidden_out),
+            (gf_all, gf_out),
+            (gt_all, gt_out),
+            (gqkv_all, gqkv_out),
+        )
+        return [
+            pltpu.make_async_copy(
+                pairs[i][0].at[recursion], pairs[i][1].at[recursion], factor_sem.at[i, recursion]
+            )
+            for i in which
+        ]
 
     def stage_copies(recursion):
         return [
@@ -1294,68 +1326,77 @@
         def _():
             action()
 
-    def send_keys(recursion):
-        when(span + 2 < 8, lambda: kv_copy(recursion, 3, 1, 0, neighbour(2)).start())
-        when(core == 0, lambda: kv_copy(recursion, 3, 2, 1, sibling).start())
+    def send_keys(recursion, pair):
+        when(span + 2 < 8, lambda: kv_copy(recursion, pair, 3, 1, 0, neighbour(2)).start())
+        when(core == 0, lambda: kv_copy(recursion, pair, 3, 2, 1, sibling).start())
         when(
             (core == 1) & (span + 3 < 8),
-            lambda: kv_copy(recursion, 3, 0, 1, neighbour(3)).start(),
-        )
-
-    def pass_keys_on(recursion):
+            lambda: kv_copy(recursion, pair, 3, 0, 1, neighbour(3)).start(),
+        )
+
+    def pass_keys_on(recursion, pair):
         @pl.when(span >= 2)
         def _():
-            kv_copy(recursion, 3, 1, 0, sibling).wait_recv()
-            kv_copy(recursion, 1, 2 * core, 2, sibling).start()
-
-    def wait_keys(recursion):
-        when(span >= 1, lambda: kv_copy(recursion, 3, 2, 1, sibling).wait_recv())
-        when(span >= 3, lambda: kv_copy(recursion, 3, 0, 1, sibling).wait_recv())
-
-    def wait_keys_sent(recursion):
-        when(span + 2 < 8, lambda: kv_copy(recursion, 3, 1, 0, sibling).wait_send())
-        when(core == 0, lambda: kv_copy(recursion, 3, 2, 1, sibling).wait_send())
+            kv_copy(recursion, pair, 3, 1, 0, sibling).wait_recv()
+            kv_copy(recursion, pair, 1, 2 * core, 2, sibling).start()
+
+    def wait_keys(recursion, pair):
+        when(span >= 1, lambda: kv_copy(recursion, pair, 3, 2, 1, sibling).wait_recv())
+        when(span >= 3, lambda: kv_copy(recursion, pair, 3, 0, 1, sibling).wait_recv())
+
+    def wait_keys_sent(recursion, pair):
+        when(span + 2 < 8, lambda: kv_copy(recursion, pair, 3, 1, 0, sibling).wait_send())
+        when(core == 0, lambda: kv_copy(recursion, pair, 3, 2, 1, sibling).wait_send())
         when(
             (core == 1) & (span + 3 < 8),
-            lambda: kv_copy(recursion, 3, 0, 1, sibling).wait_send(),
-        )
-        when(span >= 2, lambda: kv_copy(recursion, 1, 2, 2, sibling).wait_send())
-
-    def send_back(recursion):
+            lambda: kv_copy(recursion, pair, 3, 0, 1, sibling).wait_send(),
+        )
+        when(span >= 2, lambda: kv_copy(recursion, pair, 1, 2, 2, sibling).wait_send())
+
+    def send_back(recursion, pair):
+        at = pair_lanes(pair)
+
         @pl.when(span >= 2)
         def _():
-            sending[0] = dkv[pl.ds(pl.multiple_of(256 * (1 - core), 128), 128), :].astype(narrow)
-            back_copy(recursion, 0, sibling).start()
-
-        sending[2] = dkv[pl.ds(pl.multiple_of(256 * core, 128), 128), :].astype(narrow)
-        when(core == 1, lambda: back_copy(recursion, 2, sibling).start())
+            first = pl.multiple_of(256 * (1 - core), 128)
+            sending(0, pair)[...] = dkv[pl.ds(first, 128), at].astype(narrow)
+            back_copy(recursion, pair, 0, sibling).start()
+
+        sending(2, pair)[...] = dkv[
+            pl.ds(pl.multiple_of(256 * core, 128), 128), at
+        ].astype(narrow)
+        when(core == 1, lambda: back_copy(recursion, pair, 2, sibling).start())
         when(
             (core == 0) & (span >= 3),
-            lambda: back_copy(recursion, 2, neighbour(-3)).start(),
-        )
-
-    def pass_back_on(recursion):
+            lambda: back_copy(recursion, pair, 2, neighbour(-3)).start(),
+        )
+
+    def pass_back_on(recursion, pair):
         @pl.when(span >= 2)
         def _():
-            back_copy(recursion, 0, sibling).wait_recv()
-            sending[1] = (dkv[128:256, :] + got[recursion, 0].astype(wide)).astype(narrow)
-            back_copy(recursion, 1, neighbour(-2)).start()
-
-    def take_back(recursion):
+            back_copy(recursion, pair, 0, sibling).wait_recv()
+            sending(1, pair)[...] = (
+                dkv[128:256, pair_lanes(pair)] + got(recursion, 0, pair)[...].astype(wide)
+            ).astype(narrow)
+            back_copy(recursion, pair, 1, neighbour(-2)).start()
+
+    def take_back(recursion, pair):
+        at = pair_lanes(pair)
+
         @pl.when((core == 0) | (span + 3 < 8))
         def _():
-            back_copy(recursion, 2, sibling).wait_recv()
-            dkv[384:512, :] += got[recursion, 2].astype(wide)
+            back_copy(recursion, pair, 2, sibling).wait_recv()
+            dkv[384:512, at] += got(recursion, 2, pair)[...].astype(wide)
 
         @pl.when(span + 2 < 8)
         def _():
-            back_copy(recursion, 1, sibling).wait_recv()
-            dkv[384:512, :] += got[recursion, 1].astype(wide)
-
-    def wait_back_sent(recursion):
-        when(span >= 2, lambda: back_copy(recursion, 0, sibling).wait_send())
-        when(span >= 2, lambda: back_copy(recursion, 1, sibling).wait_send())
-        when((core == 1) | (span >= 3), lambda: back_copy(recursion, 2, sibling).wait_send())
+            back_copy(recursion, pair, 1, sibling).wait_recv()
+            dkv[384:512, at] += got(recursion, 1, pair)[...].astype(wide)
+
+    def wait_back_sent(recursion, pair):
+        when(span >= 2, lambda: back_copy(recursion, pair, 0, sibling).wait_send())
+        when(span >= 2, lambda: back_copy(recursion, pair, 1, sibling).wait_send())
+        when((core == 1) | (span >= 3), lambda: back_copy(recursion, pair, 2, sibling).wait_send())
 
     def add_pads():
         for block in range(32):
@@ -1370,8 +1411,6 @@
             ]
 
     here = device_of_span(group, span)
-    for away in (1, 2, 3):
-        when(span + away < 8, lambda: depth_copy(away, neighbour(away)).start())
 
     span_lane = meta[1:2, :]
     turn_cos = jnp.zeros((1, 128), wide)
@@ -1393,18 +1432,22 @@
     natural_at[...] = tokens[...].astype(wide)
     add_pads()
     h_all[0] = padded_at[...].T
+    pl.semaphore_wait(barrier, 3 + span + span // 4 * (7 - 2 * span) + 2 * moves)
+    for away in (1, 2, 3):
+        when(span + away < 8, lambda: depth_copy(away, neighbour(away)).start())
     small[...] = jnp.zeros((8, 1024), wide)
 
-    for away in (1, 2, 3):
-        when(span - away >= 0, lambda: depth_copy(away, here).wait_recv())
     row = lax.broadcasted_iota(jnp.int32, (128, 128), 0)
     column = lanes((128, 128))
     ones = jnp.ones((128, 128), wide)
-    for block in range(4):
-        held = depth_win[block]
-        depth_at[pl.ds(block * 128, 128), :] = dot_nn(
-            jnp.where(row == column, jnp.broadcast_to(held[0:1, :], (128, 128)), 0.0), ones
-        ).astype(narrow)
+    def set_depths():
+        for away in (1, 2, 3):
+            when(span - away >= 0, lambda: depth_copy(away, here).wait_recv())
+        for block in range(4):
+            held = depth_win[block]
+            depth_at[pl.ds(block * 128, 128), :] = dot_nn(
+                jnp.where(row == column, jnp.broadcast_to(held[0:1, :], (128, 128)), 0.0), ones
+            ).astype(narrow)
 
     def set_bias(recursion):
         level = recursion.astype(wide)
@@ -1441,12 +1484,12 @@
     def set_keys(recursion, pair):
         for block in range(4):
             at = pl.ds(block * 128, 128)
-            keys_at[at, 0:128] = window[recursion, block, :, pair * 128 : pair * 128 + 128]
+            keys_at[at, 0:128] = window(recursion, block, pair)[:, 0:128]
             keys_at[at, 128:256] = bias_at[at, :]
 
     def value_tile(recursion, pair):
-        at = 256 if pair == 2 else 384 + pair * 128
-        parts = [window[recursion, b, :, at : at + 128] for b in range(4)]
+        at = 0 if pair == 2 else 128
+        parts = [window(recursion, b, pair)[:, at : at + 128] for b in range(4)]
         return jnp.concatenate(parts, axis=0)
 
     def set_scores(recursion, pair, part, buffer):
@@ -1468,7 +1511,10 @@
         return jnp.where(row < 64, out[:, :128], out[:, 128:]).T
 
     def attend(recursion):
+        pass_keys_on(recursion, 0)
+        pass_keys_on(recursion, 1)
         for pair in range(3):
+            wait_keys(recursion, pair)
             set_keys(recursion, pair)
             values_t = value_tile(recursion, pair).T
             for part in range(3):
@@ -1495,6 +1541,8 @@
                     natural_at[head : head + 64, :] = out[:64, :128]
                     head = (6 * pair + 3 + part) * HEAD_SIZE
                     natural_at[head : head + 64, :] = out[64:, 128:]
+            if pair == 0:
+                pass_keys_on(recursion, 2)
 
     def upstream_of(pair, part):
         zero = jnp.zeros((64, 128), narrow)
@@ -1540,10 +1588,11 @@
             grad_keys = dot_nn(gs_at[:, 0 : 3 * width], qs_at[0 : 3 * width, :])
             grad_values = dot_nt(p_at[:, 0 : 3 * width], us_at[:, 0 : 3 * width])
             if pair == 2:
-                dkv[:, 256:384] = grad_keys + grad_values
+                dkv[:, 512:640] = grad_keys + grad_values
             else:
-                dkv[:, pair * 128 : pair * 128 + 128] = grad_keys
-                dkv[:, 384 + pair * 128 : 512 + pair * 128] = grad_values
+                dkv[:, pair * 256 : pair * 256 + 128] = grad_keys
+                dkv[:, pair * 256 + 128 : pair * 256 + 256] = grad_values
+            send_back(recursion, pair)
             out = dot_nn(keys_t, gs_at[:, 0 : 3 * width])
             for part in range(3):
                 at = (pair * 3 + part) * 128
@@ -1552,6 +1601,8 @@
                     cos_at[...] * 0.125,
                     sin_at[...] * -0.125,
                 ).astype(narrow)
+            if pair > 0:
+                pass_back_on(recursion, pair - 1)
 
     def rotate_keys(value, sine):
         cosine = cos_at[...]
@@ -1559,9 +1610,9 @@
         parts = []
         for tile in range(5):
             part = value[:, tile * 128 : tile * 128 + 128]
-            if tile < 2:
+            if tile in (0, 2):
                 part = rotated(part, cosine, sine)
-            elif tile == 2:
+            elif tile == 4:
                 part = jnp.where(low, rotated(part, cosine, sine), part)
             parts.append(part)
         return jnp.concatenate(parts, axis=1)
@@ -1578,8 +1629,10 @@
             loads[0].wait()
 
         pair_values = dot_nn(a_b, wa[:, KV_AT:O_AT])
-        window[recursion, 3] = rotate_keys(pair_values, sin_at[...]).astype(narrow)
-        send_keys(recursion)
+        pair_values = rotate_keys(pair_values, sin_at[...]).astype(narrow)
+        for pair in range(3):
+            window(recursion, 3, pair)[...] = pair_values[:, pair_lanes(pair)]
+            send_keys(recursion, pair)
         cosine, sine = cos_at[...] * 0.125, sin_at[...] * 0.125
         for first, width in ((0, 512), (512, 512), (1024, 128)):
             queries = dot_nn(a_all[recursion], wa[:, first : first + width])
@@ -1587,10 +1640,25 @@
                 q_all[recursion, :, first + at : first + at + 128] = rotated(
                     queries[:, at : at + 128], cosine, sine
                 ).astype(narrow)
+
+        @pl.when(recursion == 0)
+        def _():
+            set_depths()
+
         set_bias(recursion)
-        pass_keys_on(recursion)
-        wait_keys(recursion)
         attend(recursion)
+
+        @pl.when(recursion == 0)
+        def _():
+            start_moves(
+                (cotangent,),
+                (cotangent_at,),
+                move_send.at[pl.ds(0, 1)],
+                move_recv.at[pl.ds(0, 1)],
+                target,
+                moves,
+            )
+
         add_pads()
         o_pad = padded_at[...].T.astype(narrow)
         o_all[recursion] = o_pad
@@ -1606,9 +1674,8 @@
             for load in loads[1:]:
                 load.wait()
 
-        @pl.loop(0, FEEDFORWARD_UNITS // CHUNK)
-        def _(j):
-            at = pl.ds(pl.multiple_of(j * CHUNK, CHUNK), CHUNK)
+        for j in range(FEEDFORWARD_UNITS // CHUNK):
+            at = slice(j * CHUNK, j * CHUNK + CHUNK)
             gate = dot_nn(b_all[recursion], wg[:, at])
             up = dot_nn(b_all[recursion], wu[:, at])
             gate_all[recursion, :, at] = gate
@@ -1617,6 +1684,8 @@
             hidden_all[recursion, :, at] = hidden
             acc[...] += dot_nn(hidden, wd[at, :])
 
+        for copy in factor_copies(recursion, (0, 1, 2, 3)):
+            copy.start()
         tf_all[recursion] = acc[...]
         mixing = active_column(recursion) * mixing_gate(recursion)
         following = h_all[recursion] + mixing * acc[...]
@@ -1631,7 +1700,6 @@
             drop_pads()
             leaving[...] = natural_at[...].astype(narrow)
 
-    start_moves((leaving,), (output,), move_send.at[pl.ds(1, 1)], move_recv.at[pl.ds(1, 1)], source, moves)
     wait_moves((cotangent,), (cotangent_at,), move_send.at[pl.ds(0, 1)], move_recv.at[pl.ds(0, 1)], target, moves)
     natural_at[...] = cotangent_at[...].astype(wide)
     add_pads()
@@ -1640,6 +1708,18 @@
     @pl.loop(0, RECUR)
     def _(i):
         recursion = RECUR - 1 - i
+
+        @pl.when(i == 1)
+        def _():
+            start_moves(
+                (leaving,),
+                (output,),
+                move_send.at[pl.ds(1, 1)],
+                move_recv.at[pl.ds(1, 1)],
+                source,
+                moves,
+            )
+
         router_row = gains[pl.ds(2 + recursion, 1), :]
         active, gate_value = active_column(recursion), mixing_gate(recursion)
         upstream = grad[...]
@@ -1659,9 +1739,8 @@
             for copy in stage_copies(recursion + 1):
                 copy.wait()
 
-        @pl.loop(0, FEEDFORWARD_UNITS // CHUNK)
-        def _(j):
-            at = pl.ds(pl.multiple_of(j * CHUNK, CHUNK), CHUNK)
+        for j in range(FEEDFORWARD_UNITS // CHUNK):
+            at = slice(j * CHUNK, j * CHUNK + CHUNK)
             grad_hidden = dot_nt(gf_all[recursion], wd[at, :])
             gate, up = gate_all[recursion, :, at], up_all[recursion, :, at]
             sigmoid = jax.nn.sigmoid(gate)
@@ -1671,7 +1750,7 @@
             gu_at[:, at] = grad_up
             acc[...] += dot_nt(grad_gate, wg[:, at]) + dot_nt(grad_up, wu[:, at])
 
-        for copy in stage_copies(recursion):
+        for copy in stage_copies(recursion) + factor_copies(recursion, (4,)):
             copy.start()
         middle = z_all[recursion]
         inverse = inverse_rms(middle)
@@ -1682,22 +1761,27 @@
         grad_middle = inverse * (scaled - normal * inner)
         gt_b = (tf_all[recursion] + grad_middle).astype(narrow)
         gt_all[recursion] = gt_b
+        for copy in factor_copies(recursion, (5,)):
+            copy.start()
         grad[...] += grad_middle
         padded_at[...] = dot_nt(gt_b, wa[:, O_AT:]).T
         drop_pads()
         set_bias(recursion)
+
+        @pl.when(recursion < RECUR - 1)
+        def _():
+            for pair in range(3):
+                wait_back_sent(recursion + 1, pair)
+
         attend_back(recursion)
-
-        @pl.when(recursion < RECUR - 1)
-        def _():
-            wait_back_sent(recursion + 1)
-
-        send_back(recursion)
-        pass_back_on(recursion)
         acc[...] = dot_nt(gqkv_all[recursion, :, :KV_AT], wa[:, :KV_AT])
 
-        take_back(recursion)
+        pass_back_on(recursion, 2)
+        for pair in range(3):
+            take_back(recursion, pair)
         gqkv_all[recursion, :, KV_AT:] = rotate_keys(dkv[384:512, :], -sin_at[...]).astype(narrow)
+        for copy in factor_copies(recursion, (6,)):
+            copy.start()
         grad_normed = acc[...] + dot_nt(gqkv_all[recursion, :, KV_AT:], wa[:, KV_AT:O_AT])
         state = h_all[recursion]
         inverse = inverse_rms(state)
@@ -1709,6 +1793,9 @@
 
     for copy in stage_copies(0):
         copy.wait()
+    for recursion in range(RECUR):
+        for copy in factor_copies(recursion, range(7)):
+            copy.wait()
     padded_at[...] = grad[...].T
     drop_pads()
     input_grad[...] = natural_at[...].astype(narrow)
@@ -1717,8 +1804,10 @@
     for away in (1, 2, 3):
         when(span + away < 8, lambda: depth_copy(away, here).wait_send())
     for recursion in range(RECUR):
-        wait_keys_sent(recursion)
-    wait_back_sent(0)
+        for pair in range(3):
+            wait_keys_sent(recursion, pair)
+    for pair in range(3):
+        wait_back_sent(0, pair)
 
 
 def run_block(tokens, cotangent, meta, gains, weights):
@@ -1752,9 +1841,12 @@
         vmem((RECUR, 128, 2560), wide),
         vmem((RECUR, 128, 2560), wide),
         vmem((RECUR, 128, KV_AT), narrow),
-        vmem((RECUR, 4, 128, KV_WIDTH), narrow),
-        vmem((RECUR, 3, 128, KV_WIDTH), narrow),
-        vmem((3, 128, KV_WIDTH), narrow),
+        vmem((RECUR, 4, 2, 128, 256), narrow),
+        vmem((RECUR, 4, 128, 128), narrow),
+        vmem((RECUR, 3, 2, 128, 256), narrow),
+        vmem((RECUR, 3, 128, 128), narrow),
+        vmem((3, 2, 128, 256), narrow),
+        vmem((3, 128, 128), narrow),
         vmem((4, 8, 128), wide),
         vmem((512, 128), narrow),
         vmem((512, 128), narrow),
@@ -1775,12 +1867,14 @@
         vmem((128, 768), narrow),
         sems((2,)),
         sems((2,)),
+        *[vmem((RECUR, 128, width), narrow) for width in (1024, O_AT, 1024, 1024, 1024, 2560, 1024)],
+        sems((7, RECUR)),
         sems((4,)),
         sems((2,)),
-        sems((RECUR, 3)),
-        sems((RECUR, 3)),
-        sems((RECUR, 3)),
-        sems((RECUR, 3)),
+        sems((RECUR, 3, 3)),
+        sems((RECUR, 3, 3)),
+        sems((RECUR, 3, 3)),
+        sems((RECUR, 3, 3)),
         sems((3,)),
         sems((3,)),
     ]
@@ -1789,7 +1883,7 @@
         block_kernel,
         out_shape=[jax.ShapeDtypeStruct(shape, dtype) for shape, dtype in outs],
         in_specs=[here, anywhere] + [here] * 6 + [anywhere] * 4,
-        out_specs=[here] * 8 + [anywhere] * 2 + [here] * 2,
+        out_specs=[here] * 3 + [anywhere] * 9,
         scratch_shapes=scratch,
         compiler_params=pltpu.CompilerParams(
             collective_id=3, has_side_effects=True, vmem_limit_bytes=60 * 2**20
@@ -1837,26 +1931,31 @@
             out[first + tile, pl.ds(parity, pairs, stride=2), :] = jnp.where(low, one, two)
 
 
-def pack_own(flat, own, spread, places, tiles, natural, long_rows):
-    w_query, w_key, w_value, w_out, w_gate, w_up, w_down = flat
-    attention, gate, up, down = own
+def pack_wide(flat, own, tiles):
+    for source, out in zip(flat[4:6], own[1:3]):
+        for tile in range(20):
+            tiles[tile, 0:OWN_ROWS] = source[pl.ds(tile, OWN_ROWS, stride=20), :]
+            tiles[tile, OWN_ROWS:] = jnp.zeros((PADDED_ROWS - OWN_ROWS, 128), jnp.float32)
+            out[:, tile * 128 : tile * 128 + 128] = tiles[tile].astype(jnp.bfloat16)
+
+
+def pack_rest(flat, own, spread, tiles, natural, long_rows):
+    w_query, w_key, w_value, w_out = flat[:4]
+    attention, down = own[0], own[3]
     narrow = jnp.bfloat16
     tiles[...] = jnp.zeros(tiles.shape, jnp.float32)
     natural[...] = jnp.zeros(natural.shape, jnp.float32)
     pack_tiles(w_query, tiles, 0, HEAD_TILES, 15, 15)
-    pack_tiles(w_key, tiles, 9, ((0, 1), (2, 3), (4, -1)), 5, 15)
-    pack_tiles(w_value, tiles, 12, ((0, 1), (2, 3), (-1, 4)), 5, 15)
+    for tile, heads in ((9, (0, 1)), (11, (2, 3)), (13, (4, -1))):
+        pack_tiles(w_key, tiles, tile, (heads,), 5, 15)
+    for tile, heads in ((10, (0, 1)), (12, (2, 3)), (14, (-1, 4))):
+        pack_tiles(w_value, tiles, tile, (heads,), 5, 15)
     low = lax.broadcasted_iota(jnp.int32, (32, 128), 1) < 64
-    tiles[11] = jnp.where(low, tiles[11], tiles[14])
+    tiles[13] = jnp.where(low, tiles[13], tiles[14])
     for tile in range(14):
         attention[:, tile * 128 : tile * 128 + 128] = tiles[tile].astype(narrow)
     pack_tiles(w_out, natural, 0, NATURAL_TILES, 15, 15)
-    for source, out in ((w_gate, gate), (w_up, up)):
-        for tile in range(20):
-            tiles[tile, 0:OWN_ROWS] = source[pl.ds(tile, OWN_ROWS, stride=20), :]
-            tiles[tile, OWN_ROWS:] = jnp.zeros((PADDED_ROWS - OWN_ROWS, 128), jnp.float32)
-            out[:, tile * 128 : tile * 128 + 128] = tiles[tile].astype(narrow)
-    pack_tiles(w_down, long_rows, 0, NATURAL_TILES, 15, 40)
+    pack_tiles(flat[6], long_rows, 0, NATURAL_TILES, 15, 40)
     both = jnp.concatenate([side_by_side(natural), side_by_side(long_rows)], axis=0)
     both = dot_nn(both.astype(narrow), spread[...]).astype(narrow)
     attention[:, 1792:], down[...] = both[0:32], both[32:112]
@@ -1913,23 +2012,25 @@
     inside, places = refs[:7], refs[7]
     d_query, d_key, d_value, d_out, d_gate, d_up, d_down = refs[8:15]
     d_attn, d_ffn, d_router, output, input_grad = refs[15:20]
-    held, (spread, tiles, natural, long_rows, sems) = refs[20:26], refs[26:]
+    held, (spread, tiles, natural, long_rows, sems) = refs[20:27], refs[27:]
     copies = [
         pltpu.make_async_copy(src, dst, sems.at[i])
-        for i, (src, dst) in enumerate(zip(inside, held + (output,)))
+        for i, (src, dst) in enumerate(zip(inside, held))
     ]
     for copy in copies:
         copy.start()
     fill_spread(spread, places)
-    for copy in copies[:6]:
+    for copy in copies:
         copy.wait()
-    attention, gate, up, down, small, moved_grad = held
+    attention, gate, up, down, small, moved_grad, moved_output = held
+    output[...] = moved_output[...]
     input_grad[...] = moved_grad[...].astype(jnp.float32)
     for tile in range(14):
         tiles[tile] = attention[:, tile * 128 : tile * 128 + 128]
     unpack_tiles(tiles, 0, HEAD_TILES, 15, 15, d_query)
-    unpack_tiles(tiles, 9, ((0, 1), (2, 3), (4, -1)), 5, 15, d_key)
-    unpack_tiles(tiles, 11, ((-1, 4), (0, 1), (2, 3)), 5, 15, d_value)
+    none = (-1, -1)
+    unpack_tiles(tiles, 9, ((0, 1), none, (2, 3), none, (4, -1)), 5, 15, d_key)
+    unpack_tiles(tiles, 9, (none, (0, 1), none, (2, 3), (-1, 4)), 5, 15, d_value)
     for packed, out in ((gate, d_gate), (up, d_up)):
         for tile in range(20):
             out[pl.ds(tile, OWN_ROWS, stride=20), :] = packed[
@@ -1943,7 +2044,6 @@
     split_tiles(gathered[32:112], long_rows)
     unpack_tiles(long_rows, 0, NATURAL_TILES, 15, 40, d_down)
     d_attn[...], d_ffn[...], d_router[...] = gathered[112:113], gathered[113:114], gathered[114:117]
-    copies[6].wait()
 
 
 def unpack_gradients(sums, small, input_grad, output):
@@ -1962,8 +2062,8 @@
             jax.ShapeDtypeStruct((MODEL_WIDTH, 128), wide),
         ],
         in_specs=[anywhere] * 7 + [here],
-        out_specs=[here] * 10 + [anywhere, here],
-        scratch_shapes=[vmem(x.shape, x.dtype) for x in inside[:6]]
+        out_specs=[here] * 12,
+        scratch_shapes=[vmem(x.shape, x.dtype) for x in inside]
         + [
             vmem((MODEL_WIDTH, 1024), narrow),
             vmem((14, 32, 128), wide),

time: 322 us -> 298 us (0.925)
  Pallas kernels: 320 us -> 296 us
    pallas_call x1, Pallas kernels: 115 us -> 99.8 us  [run_block(): pl.pallas_call(block_kernel, out_shape=[jax.ShapeDtypeStruct(shape, dtype...]
    pallas_call x1, Pallas kernels: 10.6 us -> 4.56 us  [unpack_gradients(): pl.pallas_call(unpack_kernel, out_shape=[jax.ShapeDtypeStruct((rows, 128)...]
where the time goes in v4:
time: 298 us; the launch traced here: 297 us
  Pallas kernels  296 us (99%)
    pallas_call x1, Pallas kernels, reduce_gradients(): pl.pallas_call(reduce_kernel, out_shape=[jax.ShapeDtypeStruct(shape, jnp....  102 us
    pallas_call x1, Pallas kernels, run_block(): pl.pallas_call(block_kernel, out_shape=[jax.ShapeDtypeStruct(shape, dtype...  99.8 us
    pallas_call x1, Pallas kernels, gather_weights(): pl.pallas_call(gather_kernel, out_shape=[jax.ShapeDtypeStruct((32 * rows,...  89.9 us

profile of v4, /device:TPU:1, one launch (start us, length us, event | category | flops | bytes accessed | tf_op | source)
XLA Modules:
  0.0 296.7 jit_solution(12686786122218848380)
XLA Ops:
  0.6 89.9 %gather_weights.1 = (bf16[1024,2816]{1,0:T(8,128)(2,1)}, bf16[1024,2560]{1,0:T(8,128)(2,1)}, bf16[1024,2560]{1,0:T(8,128)(2,1)}, bf16[2560,1024]{1,0:T(8,128)(2,...) custom-call(f32[225,128]{1,0:T(8,128)} %bitcast.53, f32[75,128]{1,0:T(8,128)} %bitcast.55, f32[75,128]{1,0:T(8,128)} %bitcast.56, ...), custom_call_target="tpu_custom_call" | custom-call | tf_op jit(solution)/shard_map/gather_weights/pallas_call | solution.py:696
  90.5 99.8 %run_block.1 = (bf16[960,128]{1,0:T(8,128)(2,1)}, bf16[960,128]{1,0:T(8,128)(2,1)}, f32[8,1024]{1,0:T(8,128)}, bf16[3,128,1024]{2,1,0:T(8,128)(2,1)}, bf16[3,128...) custom-call(bf16[960,128]{1,0:T(8,128)(2,1)} %get-tuple-element.48.r, ...), custom_call_target="tpu_custom_call" | custom-call | tf_op jit(solution)/shard_map/run_block/pallas_call | solution.py:1882
  190.3 101.6 %reduce_gradients.1 = (f32[32,2816]{1,0:T(8,128)}, f32[32,2560]{1,0:T(8,128)}, f32[32,2560]{1,0:T(8,128)}, f32[80,1024]{1,0:T(8,128)}, f32[8,1024]{1,0:T(8,128)}, /*index=5*/bf16[960,128]{1,0:T(8,128)(2,1)}) custom-call(bf16[384,1024]{1,0:T(8,128)(2,1)} %bitcast.43, bf16[384,1792]{1,0:T(8,128)(2,1)} %bitcast.42, bf16[384,1024]{1,0:T(8,128)(2,1)} %bitcast.44, ...), custom_call_target="tpu_custom_call" | custom-call | tf_op jit(solution)/shard_map/reduce_gradients/pallas_call | solution.py:1148
  291.9 4.6 %unpack_gradients.1 = (f32[225,128]{1,0:T(8,128)}, f32[75,128]{1,0:T(8,128)}, f32[75,128]{1,0:T(8,128)}, f32[225,128]{1,0:T(8,128)}, f32[600,128]{1,0:T(8,128)},...) custom-call(f32[32,2816]{1,0:T(8,128)} %get-tuple-element.65.refs_0_, ...), custom_call_target="tpu_custom_call" | custom-call | tf_op jit(solution)/shard_map/unpack_gradients/pallas_call | solution.py:2054

commit v5 on v4

--- a/solution.py
+++ b/solution.py
@@ -1066,10 +1066,9 @@
         "z_late": z_late_event,
         "u_late": u_late_event,
     }
+    start_moves(leaving, arriving, move_send, move_recv, target, moves)
     for event in REDUCE_STEPS:
         actions[event[0]](*event[1:])
-        if event == REDUCE_STEPS[20]:
-            start_moves(leaving, arriving, move_send, move_recv, target, moves)
     wait_moves(leaving, arriving, move_send, move_recv, target, moves)
 
     for group in range(4):

time: 298 us -> 295 us (0.990)
  Pallas kernels: 296 us -> 293 us
where the time goes in v5:
time: 295 us; the launch traced here: 294 us
  Pallas kernels  293 us (99%)
    pallas_call x1, Pallas kernels, run_block(): pl.pallas_call(block_kernel, out_shape=[jax.ShapeDtypeStruct(shape, dtype...  99.8 us
    pallas_call x1, Pallas kernels, reduce_gradients(): pl.pallas_call(reduce_kernel, out_shape=[jax.ShapeDtypeStruct(shape, jnp....  98.8 us
    pallas_call x1, Pallas kernels, gather_weights(): pl.pallas_call(gather_kernel, out_shape=[jax.ShapeDtypeStruct((32 * rows,...  89.9 us

profile of v5, /device:TPU:1, one launch (start us, length us, event | category | flops | bytes accessed | tf_op | source)
XLA Modules:
  0.0 293.9 jit_solution(10513004202885253961)
XLA Ops:
  0.6 89.9 %gather_weights.1 = (bf16[1024,2816]{1,0:T(8,128)(2,1)}, bf16[1024,2560]{1,0:T(8,128)(2,1)}, bf16[1024,2560]{1,0:T(8,128)(2,1)}, bf16[2560,1024]{1,0:T(8,128)(2,...) custom-call(f32[225,128]{1,0:T(8,128)} %bitcast.53, f32[75,128]{1,0:T(8,128)} %bitcast.55, f32[75,128]{1,0:T(8,128)} %bitcast.56, ...), custom_call_target="tpu_custom_call" | custom-call | tf_op jit(solution)/shard_map/gather_weights/pallas_call | solution.py:696
  90.5 99.8 %run_block.1 = (bf16[960,128]{1,0:T(8,128)(2,1)}, bf16[960,128]{1,0:T(8,128)(2,1)}, f32[8,1024]{1,0:T(8,128)}, bf16[3,128,1024]{2,1,0:T(8,128)(2,1)}, bf16[3,128...) custom-call(bf16[960,128]{1,0:T(8,128)(2,1)} %get-tuple-element.48.r, ...), custom_call_target="tpu_custom_call" | custom-call | tf_op jit(solution)/shard_map/run_block/pallas_call | solution.py:1881
  190.3 98.8 %reduce_gradients.1 = (f32[32,2816]{1,0:T(8,128)}, f32[32,2560]{1,0:T(8,128)}, f32[32,2560]{1,0:T(8,128)}, f32[80,1024]{1,0:T(8,128)}, f32[8,1024]{1,0:T(8,128)}, /*index=5*/bf16[960,128]{1,0:T(8,128)(2,1)}) custom-call(bf16[384,1024]{1,0:T(8,128)(2,1)} %bitcast.43, bf16[384,1792]{1,0:T(8,128)(2,1)} %bitcast.42, bf16[384,1024]{1,0:T(8,128)(2,1)} %bitcast.44, ...), custom_call_target="tpu_custom_call" | custom-call | tf_op jit(solution)/shard_map/reduce_gradients/pallas_call | solution.py:1147
  289.2 4.6 %unpack_gradients.1 = (f32[225,128]{1,0:T(8,128)}, f32[75,128]{1,0:T(8,128)}, f32[75,128]{1,0:T(8,128)}, f32[225,128]{1,0:T(8,128)}, f32[600,128]{1,0:T(8,128)},...) custom-call(f32[32,2816]{1,0:T(8,128)} %get-tuple-element.65.refs_0_, ...), custom_call_target="tpu_custom_call" | custom-call | tf_op jit(solution)/shard_map/unpack_gradients/pallas_call | solution.py:2053
